TPU v7x, 128 devices: a whole 4x4x4 slice. The times are simulated.
128 devices in a mesh: row: 8 (over z, core), col: 16 (over y, x).
Axes of the slice: x: 4, y: 4, z: 4, core: 2. Of those that a mesh axis runs over, the one named last changes fastest.
Arguments:
- hidden: bfloat16 [1408, 16384], P('col', 'row'), may hold values from -18 to 18
- gain_in: bfloat16 [1408], replicated, may hold values from 0.5 to 1.5
- w_query: bfloat16 [1408, 1408], P('col'), may hold values from -0.3125 to 0.3125
- w_pair: bfloat16 [2, 1408, 1408], P(None, 'col'), may hold values from -0.15625 to 0.15625
- kv_cache: bfloat16 [2, 1408, 16384], P(None, 'col', 'row'), may hold values from -103 to 103
- recompute_rows: int32 [8, 200], P('row'), may hold values from 0 to 2047, as said below
- segment_ids: int32 [16384], P('row'), may hold values from -1 to 1, as said below
- w_out: bfloat16 [1408, 1408], P('col'), may hold values from -0.3125 to 0.3125
- gain_merge: bfloat16 [1408], replicated, may hold values from 0.5 to 1.5
- w_merge: bfloat16 [4, 1408, 1408], P(None, 'col'), may hold values from -0.078125 to 0.078125
- requests: int32 [8, 16, 85], P('row'), may hold values from -1 to 511, as said below
Outputs:
- delivered: bfloat16 [8, 16, 85, 1408], P('row', 'col')
Inputs may be any that keep to these rules, and one draw needn't show every extreme that they name: `segment_ids`: ids do not fall along the tokens except to -1 for the padding at the end; every image covers a multiple of 4 tokens and starts at a multiple of 4. `recompute_rows`: the 200 offsets of one index of row are distinct. `requests`: for each index of row, the lists of all owners together name each of its 512 merged tokens exactly once; unused slots hold -1 and follow the used ones.
All inputs are finite; a program needn't handle non-finite values.
Results may differ from a plain program's by a relative error of at most 0.025.
The roundings to bfloat16 on the way count: a program that leaves them out, or rounds other values in their place, can miss the bound.
Values may be sent and summed in bfloat16 or wider, within the bound.
A program may use at most 128 MiB of HBM per device.

v0:
```python
import jax
import jax.numpy as jnp
from jax import lax
from jax.sharding import PartitionSpec as P

HD = 88


EPSILON = 1e-06
MASKED = -1e30
KEY_BLOCK = 1024


def on_device(
    hidden,
    gain_in,
    w_query,
    w_pair,
    kv_cache,
    recompute_rows,
    segment_ids,
    w_out,
    gain_merge,
    w_merge,
    requests,
):
    local_width, tok_rows = hidden.shape
    model_width = w_query.shape[1]
    heads_here = local_width // HD
    score_scale = HD ** (-0.5)
    column_start = lax.axis_index("col") * local_width
    full_rows = lax.all_gather(hidden, "col", axis=0, tiled=True)
    full_float = full_rows.astype(jnp.float32)
    in_mean = jnp.sum(full_float, axis=0, keepdims=True) / model_width
    in_square = jnp.sum(full_float * full_float, axis=0, keepdims=True) / model_width
    normed = (
        (full_float - in_mean)
        * lax.rsqrt(in_square - in_mean * in_mean + EPSILON)
        * gain_in.astype(jnp.float32)[:, None]
    ).astype(jnp.bfloat16)
    queries = jnp.dot(w_query, normed, preferred_element_type=jnp.float32).astype(jnp.bfloat16)
    picked_rows = recompute_rows[0]
    normed_picked = jnp.take(normed, picked_rows, axis=1)
    fresh_pairs = jnp.dot(
        w_pair.reshape(2 * local_width, model_width),
        normed_picked,
        preferred_element_type=jnp.float32,
    )
    fresh_pairs = fresh_pairs.astype(jnp.bfloat16).reshape(2, local_width, -1)
    keys_values = kv_cache.at[:, :, picked_rows].set(fresh_pairs)
    query_heads = queries.reshape(heads_here, HD, tok_rows)
    segment_grid = segment_ids.reshape(1, 1, tok_rows)

    def take_block(carried, pair_block, segment_block):
        running_max, running_sum, weighted = carried
        key_block = pair_block[0].reshape(heads_here, HD, -1)
        value_block = pair_block[1].reshape(heads_here, HD, -1)
        scores = (
            jnp.einsum("hdq,hdk->hqk", query_heads, key_block, preferred_element_type=jnp.float32)
            * score_scale
        )
        allowed = (segment_ids[:, None] == segment_block[None, :])[None, :, :]
        new_max = jnp.maximum(running_max, jnp.max(jnp.where(allowed, scores, MASKED), axis=2))
        weights_exp = jnp.where(allowed, jnp.exp(scores - new_max[:, :, None]), 0.0)
        factor = jnp.exp(running_max - new_max)
        running_sum = running_sum * factor + jnp.sum(weights_exp, axis=2)
        product = jnp.einsum(
            "hqk,hdk->hdq",
            weights_exp.astype(jnp.bfloat16),
            value_block,
            preferred_element_type=jnp.float32,
        )
        weighted = weighted * factor[:, None, :] + product
        return (new_max, running_sum, weighted)

    starting = (
        jnp.full((heads_here, tok_rows), MASKED, jnp.float32),
        jnp.zeros((heads_here, tok_rows), jnp.float32),
        jnp.zeros((heads_here, HD, tok_rows), jnp.float32),
    )
    carried = starting
    pair_rows = lax.all_gather(keys_values, "row", axis=2, tiled=True)
    segment_rows = lax.all_gather(segment_grid, "row", axis=2, tiled=True)
    segment_line = segment_rows[0, 0]
    piece_rows = pair_rows.shape[2]
    whole_blocks = piece_rows // KEY_BLOCK

    def loop_body(block_index, loop_state):
        pair_block = lax.dynamic_slice_in_dim(pair_rows, block_index * KEY_BLOCK, KEY_BLOCK, 2)
        segment_block = lax.dynamic_slice_in_dim(
            segment_line, block_index * KEY_BLOCK, KEY_BLOCK, 0
        )
        return take_block(loop_state, pair_block, segment_block)

    carried = lax.fori_loop(0, whole_blocks, loop_body, carried)
    running_max, running_sum, weighted = carried
    attended = (
        (weighted / running_sum[:, None, :]).astype(jnp.bfloat16).reshape(local_width, tok_rows)
    )
    gain_part = lax.dynamic_slice_in_dim(gain_merge, column_start, local_width, 0).astype(
        jnp.float32
    )[:, None]
    partial_out = lax.dot_general(
        w_out, attended, (((0,), (0,)), ((), ())), preferred_element_type=jnp.float32
    )
    summed = lax.psum(partial_out.astype(jnp.bfloat16), "col").astype(jnp.float32)
    updated = full_float + summed
    row_mean = jnp.sum(updated, axis=0, keepdims=True) / model_width
    row_square = jnp.sum(updated * updated, axis=0, keepdims=True) / model_width
    own_part = lax.dynamic_slice_in_dim(updated, column_start, local_width, 0)
    merger_in = (
        (own_part - row_mean) * lax.rsqrt(row_square - row_mean * row_mean + EPSILON) * gain_part
    ).astype(jnp.bfloat16)
    merged_rows = tok_rows // 4
    grouped = merger_in.reshape(local_width, merged_rows, 4)
    merged = jnp.einsum("cgi,icd->gd", grouped, w_merge, preferred_element_type=jnp.float32)
    wanted_rows = requests[0]
    is_valid = wanted_rows >= 0
    safe_index = jnp.where(is_valid, wanted_rows, 0)
    picked = jnp.where(is_valid[:, :, None], merged[safe_index], 0.0)
    owned_rows = lax.psum_scatter(
        picked.astype(jnp.bfloat16), "col", scatter_dimension=0, tiled=True
    )
    return owned_rows.reshape(1, 1, owned_rows.shape[1], model_width)


def solution(mesh):
    placed = (
        P("col", "row"),
        P(),
        P("col", None),
        P(None, "col", None),
        P(None, "col", "row"),
        P("row", None),
        P("row"),
        P("col", None),
        P(),
        P(None, "col", None),
        P("row", None, None),
    )
    return jax.shard_map(
        on_device,
        mesh=mesh,
        in_specs=placed,
        out_specs=P("row", "col", None, None),
        check_vma=False,
    )
```

profile of v0, /device:TPU:78, one launch (start us, length us, event | category | flops | bytes accessed | tf_op | source)
XLA Modules:
  0.0 630.0 jit_solution(8836994563244462151)
XLA Ops:
  11.8 56.7 %all-gather.4.cloned.1.call-done = bf16[1408,2048]{1,0:T(8,128)(2,1)} async-done(((bf16[88,2048]{1,0:T(8,128)(2,1)}), bf16[1408,2048]{1,0:T(8,128)(2,1)}) %all-gather.4.cloned.1.call-update) | async-done | bytes 5767184 | tf_op jit(solution)/shard_map/all_gather | solution.py:32
  68.5 8.4 %copy.22 = bf16[1408,2048]{0,1:T(8,128)(2,1)} copy(bf16[1408,2048]{1,0:T(8,128)(2,1)} %all-gather.4.cloned.1.call-done) | data formatting | bytes 11534336 | tf_op jit(solution)/shard_map/all_gather | solution.py:32
  85.4 5.0 gather_fusion
  91.0 6.9 %scatter_fusion = bf16[2,88,2048]{1,0,2:T(2,128)(2,1)S(1)} fusion(bf16[2,88,2048]{1,0,2:T(2,128)(2,1)S(1)} %copy.24, s32[200]{0:T(256)S(1)} %bitcast.104, bf16[200,2,88]{2,1,0:T(2,128)(2,1)S(1)} %bitcast.99), kind=kCustom, calls=%fused_computation.2 | custom fusion | bytes 212000 | tf_op jit(solution)/shard_map/scatter | solution.py:50
  99.9 11.7 %all-gather = s32[16384]{0:T(1024)S(1)} all-gather(s32[2048]{0:T(1024)S(1)} %copy-done.2), channel_id=2, replica_groups=mesh['row'=8,'col'=16] {'row'}, dimensions={0}, use_global_device_ids=true | all-gather | bytes 73728 | tf_op jit(solution)/shard_map/all_gather | solution.py:83
  111.6 4.9 fusion.26
  116.5 22.0 %all-gather.6.cloned.1.call-done = bf16[2,88,16384]{2,1,0:T(8,128)(2,1)} async-done(((bf16[2,88,2048]{2,1,0:T(8,128)(2,1)}), bf16[2,88,16384]{2,1,0:T(8,128)(2,1)}) %all-gather.6.cloned.1.call-update) | async-done | bytes 5767184 | tf_op jit(solution)/shard_map/all_gather | solution.py:82
  138.5 249.8 %while.18 = (s32[]{:T(128)}, f32[1,2048]{1,0:T(1,128)S(1)}, f32[1,2048]{1,0:T(1,128)S(1)}, f32[1,88,2048]{2,1,0:T(8,128)S(1)}, s32[2048]{0:T(1024)S(1)}, /*index...) while((s32[]{:T(128)}, f32[1,2048]{1,0:T(1,128)S(1)}, ...), condition=%wide.region_6.7_spmd.clone, body=%wide.region_3.0_spmd.clone.sunk | while | flops 768108544 | bytes 27504848 | solution.py:95
  138.5 5.6 fusion.46
  144.1 4.6 fusion.48
  148.7 5.4 fusion.50
  154.2 5.5 fusion.46
  159.7 4.6 fusion.48
  164.3 5.4 fusion.50
  169.8 5.5 fusion.46
  179.9 5.4 fusion.50
  185.4 5.5 fusion.46
  195.6 5.4 fusion.50
  201.0 5.5 fusion.46
  211.2 5.4 fusion.50
  216.6 5.5 fusion.46
  226.8 5.4 fusion.50
  232.2 5.5 fusion.46
  237.8 4.6 fusion.48
  242.4 5.4 fusion.50
  247.8 5.5 fusion.46
  258.0 5.4 fusion.50
  263.5 5.5 fusion.46
  273.6 5.4 fusion.50
  279.1 5.5 fusion.46
  284.6 4.6 fusion.48
  289.2 5.4 fusion.50
  294.7 5.5 fusion.46
  304.9 5.4 fusion.50
  310.3 5.5 fusion.46
  320.5 5.4 fusion.50
  325.9 5.5 fusion.46
  336.1 5.4 fusion.50
  341.5 5.5 fusion.46
  351.7 5.4 fusion.50
  357.1 5.5 fusion.46
  367.3 5.4 fusion.50
  372.7 5.5 fusion.46
  382.9 5.4 fusion.50
  393.8 116.4 %all-reduce.3.cloned.1.call-done = bf16[1408,2048]{0,1:T(8,128)(2,1)} async-done(((bf16[1408,2048]{0,1:T(8,128)(2,1)}), bf16[1408,2048]{0,1:T(8,128)(2,1)}) %all-reduce.3.cloned.1.call-update) | async-done | bytes 5767184 | tf_op jit(solution)/shard_map/psum | solution.py:106
  510.1 10.2 %fusion.33 = (f32[2048]{0:T(1024)S(1)}, f32[2048]{0:T(1024)S(1)}, f32[1408,2048]{0,1:T(8,128)}) fusion(bf16[1408,2048]{0,1:T(8,128)(2,1)} %all-reduce.3.cloned.1.call-done, bf16[1408,2048]{0,1:T(8,128)(2,1)} %copy.22), kind=kLoop, calls=%fused_computation.65 | loop fusion | flops 17297408 | bytes 23085056 | tf_op jit(solution)/shard_map/reduce_sum | solution.py:108
  523.8 6.0 gather_fusion.1
  537.6 85.9 %reduce-scatter.4.cloned.1.call-done = bf16[1,85,1408]{2,1,0:T(8,128)(2,1)} async-done(((bf16[16,85,1408]{2,1,0:T(8,128)(2,1)}), bf16[1,85,1408]{2,1,0:T(8,128)(2,1)}) %reduce-scatter.4.cloned.1.call-update) | async-done | bytes 239376
  (123 shorter events, 88.9 us)
Async XLA Ops:
  6.5 516.3 %copy-start = (bf16[4,88,1408]{2,1,0:T(8,128)(2,1)S(1)}, bf16[4,88,1408]{2,1,0:T(8,128)(2,1)}, u32[]{:S(2)}) copy-start(bf16[4,88,1408]{2,1,0:T(8,128)(2,1)} %param.22) | copy-start | bytes 2973700
  6.5 62.0 %all-gather.4.cloned.1.call-start = ((), (), s32[]{:S(2)}) async-start(), calls=%async_computation.1 | async-start | bytes 6127616 | tf_op jit(solution)/shard_map/all_gather | solution.py:32
  7.3 131.3 %all-gather.6.cloned.1.call-start = ((), (), s32[]{:S(2)}) async-start(), calls=%async_computation.2 | async-start | bytes 6488064 | tf_op jit(solution)/shard_map/all_gather | solution.py:82
  76.9 4.5 copy-start.1
  81.4 9.0 %copy-start.6 = (bf16[2,88,1408]{2,1,0:T(8,128)(2,1)S(1)}, bf16[2,88,1408]{2,1,0:T(8,128)(2,1)}, u32[]{:S(2)}) copy-start(bf16[2,88,1408]{2,1,0:T(8,128)(2,1)} %param.16) | copy-start | bytes 1486852
  85.4 14.5 %copy-start.2 = (s32[2048]{0:T(1024)S(1)}, s32[2048]{0:T(1024)}, u32[]{:S(2)}) copy-start(s32[2048]{0:T(1024)} %param.19) | copy-start | bytes 24580
  85.4 26.2 %copy-start.3 = (bf16[88,1408]{1,0:T(8,128)(2,1)S(1)}, bf16[88,1408]{1,0:T(8,128)(2,1)}, u32[]{:S(2)}) copy-start(bf16[88,1408]{1,0:T(8,128)(2,1)} %param.15) | copy-start | bytes 743428
  99.8 410.3 %all-reduce.3.cloned.1.call-start = ((), (), s32[]{:S(2)}) async-start(), calls=%async_computation.3 | async-start | bytes 11534336 | tf_op jit(solution)/shard_map/psum | solution.py:106
  138.5 249.8 %copy-start.4 = (bf16[88,1408]{1,0:T(8,128)(2,1)S(1)}, bf16[88,1408]{1,0:T(8,128)(2,1)}, u32[]{:S(2)}) copy-start(bf16[88,1408]{1,0:T(8,128)(2,1)} %param.20) | copy-start | bytes 743428
  388.3 4.5 copy-start.5
  392.6 230.9 %reduce-scatter.4.cloned.1.call-start = ((), (), s32[]{:S(2)}) async-start(), calls=%async_computation.4 | async-start | bytes 4212736
Sparse Core Ops, SparseCore 0:
  9.5 58.9 all-gather.3
  99.9 38.5 all-gather.5
  392.7 117.3 all-reduce.2
  537.8 85.6 reduce-scatter.3
where the time goes:
time: 634 us; the launch traced here: 630 us
  waiting for transfers between devices  282 us (44%)
  matrix products  185 us (29%)
  other arithmetic  102 us (16%)
  local copies, waits for them, and re-layouts  35 us (6%)
  between operations  13.3 us (2%)
  blocking collectives  11.7 us (2%)
    psum x1, waiting for transfers between devices, on_device(): lax.psum(partial_out.astype(jnp.bfloat16), 'col').astype(jnp.float32)  116 us
    dot_general x16, matrix products, take_block(): jnp.einsum('hdq,hdk->hqk', query_heads, key_block, preferred_element_type...  88.5 us
    unnamed x5, waiting for transfers between devices  86.6 us
    dot_general x16, matrix products, take_block(): jnp.einsum('hqk,hdk->hdq', weights_exp.astype(jnp.bfloat16), value_block,...  86.2 us
    reduce_sum x16, other arithmetic, take_block(): running_sum = running_sum * factor + jnp.sum(weights_exp, axis=2)  73.2 us
    all_gather x1, waiting for transfers between devices, on_device(): full_rows = lax.all_gather(hidden, 'col', axis=0, tiled=True)  56.7 us
    all_gather x1, waiting for transfers between devices, on_device(): pair_rows = lax.all_gather(keys_values, 'row', axis=2, tiled=True)  22 us
  transfers between devices with their start and end apart: 4, of which 4 were waited for; matrix products, arithmetic and copies ran while one was open for 2% of the time, Pallas kernels for 0%

commit v1 on v0

--- a/solution.py
+++ b/solution.py
@@ -26,10 +26,12 @@
 ):
     local_width, tok_rows = hidden.shape
     model_width = w_query.shape[1]
+    n_col = model_width // local_width
     heads_here = local_width // HD
     score_scale = HD ** (-0.5)
-    column_start = lax.axis_index("col") * local_width
+    col_index = lax.axis_index("col")
     full_rows = lax.all_gather(hidden, "col", axis=0, tiled=True)
+    out_weight = lax.all_gather(w_out, "col", axis=0, tiled=True)
     full_float = full_rows.astype(jnp.float32)
     in_mean = jnp.sum(full_float, axis=0, keepdims=True) / model_width
     in_square = jnp.sum(full_float * full_float, axis=0, keepdims=True) / model_width
@@ -49,7 +51,14 @@
     fresh_pairs = fresh_pairs.astype(jnp.bfloat16).reshape(2, local_width, -1)
     keys_values = kv_cache.at[:, :, picked_rows].set(fresh_pairs)
     query_heads = queries.reshape(heads_here, HD, tok_rows)
-    segment_grid = segment_ids.reshape(1, 1, tok_rows)
+
+    pair_local = jnp.concatenate(
+        [keys_values.reshape(2 * local_width, tok_rows), segment_ids.astype(jnp.bfloat16)[None, :]],
+        axis=0,
+    )
+    pair_all = lax.all_gather(pair_local, "row", axis=1, tiled=True)
+    pair_rows = pair_all[: 2 * local_width].reshape(2, local_width, -1)
+    segment_line = pair_all[2 * local_width].astype(jnp.int32)
 
     def take_block(carried, pair_block, segment_block):
         running_max, running_sum, weighted = carried
@@ -78,10 +87,6 @@
         jnp.zeros((heads_here, tok_rows), jnp.float32),
         jnp.zeros((heads_here, HD, tok_rows), jnp.float32),
     )
-    carried = starting
-    pair_rows = lax.all_gather(keys_values, "row", axis=2, tiled=True)
-    segment_rows = lax.all_gather(segment_grid, "row", axis=2, tiled=True)
-    segment_line = segment_rows[0, 0]
     piece_rows = pair_rows.shape[2]
     whole_blocks = piece_rows // KEY_BLOCK
 
@@ -92,36 +97,34 @@
         )
         return take_block(loop_state, pair_block, segment_block)
 
-    carried = lax.fori_loop(0, whole_blocks, loop_body, carried)
-    running_max, running_sum, weighted = carried
+    running_max, running_sum, weighted = lax.fori_loop(0, whole_blocks, loop_body, starting)
     attended = (
         (weighted / running_sum[:, None, :]).astype(jnp.bfloat16).reshape(local_width, tok_rows)
     )
-    gain_part = lax.dynamic_slice_in_dim(gain_merge, column_start, local_width, 0).astype(
-        jnp.float32
-    )[:, None]
-    partial_out = lax.dot_general(
-        w_out, attended, (((0,), (0,)), ((), ())), preferred_element_type=jnp.float32
+    chunk = tok_rows // n_col
+    attended_chunk = lax.all_to_all(attended, "col", 1, 0, tiled=True)
+    x_chunk = lax.dynamic_slice_in_dim(full_float, col_index * chunk, chunk, 1)
+    projected = lax.dot_general(
+        out_weight, attended_chunk, (((0,), (0,)), ((), ())), preferred_element_type=jnp.float32
     )
-    summed = lax.psum(partial_out.astype(jnp.bfloat16), "col").astype(jnp.float32)
-    updated = full_float + summed
+    updated = x_chunk + projected
     row_mean = jnp.sum(updated, axis=0, keepdims=True) / model_width
     row_square = jnp.sum(updated * updated, axis=0, keepdims=True) / model_width
-    own_part = lax.dynamic_slice_in_dim(updated, column_start, local_width, 0)
-    merger_in = (
-        (own_part - row_mean) * lax.rsqrt(row_square - row_mean * row_mean + EPSILON) * gain_part
+    merger_chunk = (
+        (updated - row_mean)
+        * lax.rsqrt(row_square - row_mean * row_mean + EPSILON)
+        * gain_merge.astype(jnp.float32)[:, None]
     ).astype(jnp.bfloat16)
+    merger_in = lax.all_to_all(merger_chunk, "col", 0, 1, tiled=True)
     merged_rows = tok_rows // 4
     grouped = merger_in.reshape(local_width, merged_rows, 4)
     merged = jnp.einsum("cgi,icd->gd", grouped, w_merge, preferred_element_type=jnp.float32)
-    wanted_rows = requests[0]
+    merged_sum = lax.psum(merged.astype(jnp.bfloat16), "col")
+    wanted_rows = lax.dynamic_index_in_dim(requests[0], col_index, 0, keepdims=False)
     is_valid = wanted_rows >= 0
     safe_index = jnp.where(is_valid, wanted_rows, 0)
-    picked = jnp.where(is_valid[:, :, None], merged[safe_index], 0.0)
-    owned_rows = lax.psum_scatter(
-        picked.astype(jnp.bfloat16), "col", scatter_dimension=0, tiled=True
-    )
-    return owned_rows.reshape(1, 1, owned_rows.shape[1], model_width)
+    picked = jnp.where(is_valid[:, None], merged_sum[safe_index], jnp.zeros((), jnp.bfloat16))
+    return picked.reshape(1, 1, picked.shape[0], model_width)
 
 
 def solution(mesh):

time: 634 us -> 534 us (0.84)
  waiting for transfers between devices: 282 us -> 177 us
  starting transfers between devices: 0.35 us -> 7.51 us
    unnamed x5 -> x4, waiting for transfers between devices: 86.6 us -> 1.24 us
    psum x1, waiting for transfers between devices: 116 us -> 85.2 us  [on_device(): merged_sum = lax.psum(merged.astype(jnp.bfloat16), 'col')]
    all_to_all x0 -> x1, blocking collectives: none -> 13.1 us  [on_device(): merger_in = lax.all_to_all(merger_chunk, 'col', 0, 1, tiled=True)]
    all_gather x1 -> x2, waiting for transfers between devices: 22 us -> 34.3 us  [the longest x1 34.3 us: on_device(): pair_all = lax.all_gather(pair_local, 'row', axis=1, tiled=True)]
    all_gather x1 -> x0, blocking collectives: 11.7 us -> none  [on_device(): segment_rows = lax.all_gather(segment_grid, 'row', axis=2, tiled=True)]
    reduce_sum x1 -> x0, other arithmetic: 10.2 us -> none  [on_device(): row_mean = jnp.sum(updated, axis=0, keepdims=True) / model_width]
    gather x2 -> x1, local copies, waits for them, and re-layouts: 9.95 us -> 2.53 us  [on_device(): merged_sum[safe_index]]
    all_to_all x0 -> x1, starting transfers between devices: none -> 7.21 us  [on_device(): attended_chunk = lax.all_to_all(attended, 'col', 1, 0, tiled=True)]
  transfers between devices with their start and end apart: 4 -> 5, of which waited for: 4 -> 3; matrix products, arithmetic and copies ran while one was open for 2% -> 52% of each run, Pallas kernels for 0% -> 0%
where the time goes in v1:
time: 534 us; the launch traced here: 530 us
  matrix products  187 us (35%)
  waiting for transfers between devices  177 us (33%)
  other arithmetic  97.7 us (18%)
  local copies, waits for them, and re-layouts  33.4 us (6%)
  between operations  13.4 us (3%)
  blocking collectives  13.1 us (2%)
  starting transfers between devices  7.51 us (1%)
    dot_general x16, matrix products, take_block(): jnp.einsum('hdq,hdk->hqk', query_heads, key_block, preferred_element_type...  89.9 us
    dot_general x16, matrix products, take_block(): jnp.einsum('hqk,hdk->hdq', weights_exp.astype(jnp.bfloat16), value_block,...  86.8 us
    psum x1, waiting for transfers between devices, on_device(): merged_sum = lax.psum(merged.astype(jnp.bfloat16), 'col')  85.2 us
    reduce_sum x16, other arithmetic, take_block(): running_sum = running_sum * factor + jnp.sum(weights_exp, axis=2)  73.6 us
    all_gather x1, waiting for transfers between devices, on_device(): full_rows = lax.all_gather(hidden, 'col', axis=0, tiled=True)  56 us
    all_gather x1, waiting for transfers between devices, on_device(): pair_all = lax.all_gather(pair_local, 'row', axis=1, tiled=True)  34.3 us
    all_to_all x1, blocking collectives, on_device(): merger_in = lax.all_to_all(merger_chunk, 'col', 0, 1, tiled=True)  13.1 us
  transfers between devices with their start and end apart: 5, of which 3 were waited for; matrix products, arithmetic and copies ran while one was open for 52% of the time, Pallas kernels for 0%

profile of v1, /device:TPU:78, one launch (start us, length us, event | category | flops | bytes accessed | tf_op | source)
XLA Modules:
  0.0 529.7 jit_solution(17478060739190972676)
XLA Ops:
  12.5 56.0 %all-gather.4.cloned.1.call-done = bf16[1408,2048]{1,0:T(8,128)(2,1)} async-done(((bf16[88,2048]{1,0:T(8,128)(2,1)}), bf16[1408,2048]{1,0:T(8,128)(2,1)}) %all-gather.4.cloned.1.call-update) | async-done | bytes 5767184 | tf_op jit(solution)/shard_map/all_gather | solution.py:33
  68.5 8.3 %copy.31 = bf16[1408,2048]{0,1:T(8,128)(2,1)} copy(bf16[1408,2048]{1,0:T(8,128)(2,1)} %all-gather.4.cloned.1.call-done) | data formatting | bytes 11534336 | tf_op jit(solution)/shard_map/all_gather | solution.py:33
  85.3 5.0 gather_fusion
  90.9 6.9 %scatter_fusion = bf16[2,88,2048]{1,0,2:T(2,128)(2,1)S(1)} fusion(bf16[2,88,2048]{1,0,2:T(2,128)(2,1)S(1)} %copy.33, s32[200]{0:T(256)S(1)} %bitcast.125, bf16[200,2,88]{2,1,0:T(2,128)(2,1)S(1)} %bitcast.118), kind=kCustom, calls=%fused_computation.2 | custom fusion | bytes 212000 | tf_op jit(solution)/shard_map/scatter | solution.py:52
  100.3 4.7 fusion.23
  105.0 34.3 %all-gather.6.cloned.1.call-done = bf16[177,16384]{1,0:T(8,128)(2,1)} async-done(((bf16[177,2048]{1,0:T(8,128)(2,1)}), bf16[177,16384]{1,0:T(8,128)(2,1)}) %all-gather.6.cloned.1.call-update) | async-done | bytes 5799952 | tf_op jit(solution)/shard_map/all_gather | solution.py:59
  139.3 5.8 %slice.29 = bf16[176,16384]{1,0:T(8,128)(2,1)} slice(bf16[177,16384]{1,0:T(8,128)(2,1)} %all-gather.6.cloned.1.call-done), slice={[0:176], [0:16384]} | slice | bytes 11534336 | tf_op jit(solution)/shard_map/slice | solution.py:60
  146.1 252.2 %while.18 = (s32[]{:T(128)}, f32[1,2048]{1,0:T(1,128)S(1)}, f32[1,2048]{1,0:T(1,128)S(1)}, f32[1,88,2048]{2,1,0:T(8,128)S(1)}, s32[2048]{0:T(1024)S(1)}, /*index...) while((s32[]{:T(128)}, f32[1,2048]{1,0:T(1,128)S(1)}, ...), condition=%wide.region_6.7_spmd.clone, body=%wide.region_3.0_spmd.clone.sunk | while | flops 768108544 | bytes 27504848 | solution.py:100
  146.1 5.6 %fusion.45 = (f32[2048]{0:T(1024)S(1)}, f32[1024,2048]{1,0:T(8,128)}) fusion(s32[2048]{0:T(1024)S(1)} %get-tuple-element.290, s32[1024]{0:T(1024)S(1)} %dynamic_slice.32, bf16[1,88,2048]{2,1,0:T(8,128)(2,1)S(1)} %get-tuple-element.293, bf16[2,88,16384]{2,1,0:T(8,128)(2,1)} %get-tuple-element.292, s32[]{:T(128)S(6)} %select_n.132), kind=kOutput, calls=%fused_computation.5.clone.1 | convolution fusion | flops 377485312 | bytes 8949764 | tf_op jit(solution)/shard_map/while/body/eval_jaxpr/hdq,hdk->hqk/dot_general | solution.py:68
  151.8 4.8 fusion.47
  156.6 5.5 %fusion.49 = f32[1,88,2048]{2,1,0:T(8,128)S(1)} fusion(f32[1024,2048]{1,0:T(8,128)} %get-tuple-element.257, f32[2048]{0:T(1024)S(1)} %bitcast.110, s32[2048]{0:T(1024)S(1)} %get-tuple-element.290, s32[1024]{0:T(1024)S(1)} %dynamic_slice.32, f32[1,88,2048]{2,1,0:T(8,128)S(1)} %get-tuple-element.276, f32[2048]{0:T(1024)S(1)} %bitcast.120, ...), kind=kOutput, calls=%fused_computation.12.clone.1 | convolution fusion | flops 380125184 | bytes 10039305 | tf_op jit(solution)/shard_map/while/body/eval_jaxpr/hqk,hdk->hdq/dot_general | solution.py:76
  162.1 5.6 %fusion.45 = (f32[2048]{0:T(1024)S(1)}, f32[1024,2048]{1,0:T(8,128)}) fusion(s32[2048]{0:T(1024)S(1)} %get-tuple-element.290, s32[1024]{0:T(1024)S(1)} %dynamic_slice.32, bf16[1,88,2048]{2,1,0:T(8,128)(2,1)S(1)} %get-tuple-element.293, bf16[2,88,16384]{2,1,0:T(8,128)(2,1)} %get-tuple-element.292, s32[]{:T(128)S(6)} %select_n.132), kind=kOutput, calls=%fused_computation.5.clone.1 | convolution fusion | flops 377485312 | bytes 8949764 | tf_op jit(solution)/shard_map/while/body/eval_jaxpr/hdq,hdk->hqk/dot_general | solution.py:68
  172.4 5.7 %fusion.49 = f32[1,88,2048]{2,1,0:T(8,128)S(1)} fusion(f32[1024,2048]{1,0:T(8,128)} %get-tuple-element.257, f32[2048]{0:T(1024)S(1)} %bitcast.110, s32[2048]{0:T(1024)S(1)} %get-tuple-element.290, s32[1024]{0:T(1024)S(1)} %dynamic_slice.32, f32[1,88,2048]{2,1,0:T(8,128)S(1)} %get-tuple-element.276, f32[2048]{0:T(1024)S(1)} %bitcast.120, ...), kind=kOutput, calls=%fused_computation.12.clone.1 | convolution fusion | flops 380125184 | bytes 10039305 | tf_op jit(solution)/shard_map/while/body/eval_jaxpr/hqk,hdk->hdq/dot_general | solution.py:76
  178.2 5.6 %fusion.45 = (f32[2048]{0:T(1024)S(1)}, f32[1024,2048]{1,0:T(8,128)}) fusion(s32[2048]{0:T(1024)S(1)} %get-tuple-element.290, s32[1024]{0:T(1024)S(1)} %dynamic_slice.32, bf16[1,88,2048]{2,1,0:T(8,128)(2,1)S(1)} %get-tuple-element.293, bf16[2,88,16384]{2,1,0:T(8,128)(2,1)} %get-tuple-element.292, s32[]{:T(128)S(6)} %select_n.132), kind=kOutput, calls=%fused_computation.5.clone.1 | convolution fusion | flops 377485312 | bytes 8949764 | tf_op jit(solution)/shard_map/while/body/eval_jaxpr/hdq,hdk->hqk/dot_general | solution.py:68
  183.8 4.7 fusion.47
  188.6 5.4 %fusion.49 = f32[1,88,2048]{2,1,0:T(8,128)S(1)} fusion(f32[1024,2048]{1,0:T(8,128)} %get-tuple-element.257, f32[2048]{0:T(1024)S(1)} %bitcast.110, s32[2048]{0:T(1024)S(1)} %get-tuple-element.290, s32[1024]{0:T(1024)S(1)} %dynamic_slice.32, f32[1,88,2048]{2,1,0:T(8,128)S(1)} %get-tuple-element.276, f32[2048]{0:T(1024)S(1)} %bitcast.120, ...), kind=kOutput, calls=%fused_computation.12.clone.1 | convolution fusion | flops 380125184 | bytes 10039305 | tf_op jit(solution)/shard_map/while/body/eval_jaxpr/hqk,hdk->hdq/dot_general | solution.py:76
  194.0 5.6 %fusion.45 = (f32[2048]{0:T(1024)S(1)}, f32[1024,2048]{1,0:T(8,128)}) fusion(s32[2048]{0:T(1024)S(1)} %get-tuple-element.290, s32[1024]{0:T(1024)S(1)} %dynamic_slice.32, bf16[1,88,2048]{2,1,0:T(8,128)(2,1)S(1)} %get-tuple-element.293, bf16[2,88,16384]{2,1,0:T(8,128)(2,1)} %get-tuple-element.292, s32[]{:T(128)S(6)} %select_n.132), kind=kOutput, calls=%fused_computation.5.clone.1 | convolution fusion | flops 377485312 | bytes 8949764 | tf_op jit(solution)/shard_map/while/body/eval_jaxpr/hdq,hdk->hqk/dot_general | solution.py:68
  199.7 4.6 fusion.47
  204.3 5.4 %fusion.49 = f32[1,88,2048]{2,1,0:T(8,128)S(1)} fusion(f32[1024,2048]{1,0:T(8,128)} %get-tuple-element.257, f32[2048]{0:T(1024)S(1)} %bitcast.110, s32[2048]{0:T(1024)S(1)} %get-tuple-element.290, s32[1024]{0:T(1024)S(1)} %dynamic_slice.32, f32[1,88,2048]{2,1,0:T(8,128)S(1)} %get-tuple-element.276, f32[2048]{0:T(1024)S(1)} %bitcast.120, ...), kind=kOutput, calls=%fused_computation.12.clone.1 | convolution fusion | flops 380125184 | bytes 10039305 | tf_op jit(solution)/shard_map/while/body/eval_jaxpr/hqk,hdk->hdq/dot_general | solution.py:76
  209.8 5.6 %fusion.45 = (f32[2048]{0:T(1024)S(1)}, f32[1024,2048]{1,0:T(8,128)}) fusion(s32[2048]{0:T(1024)S(1)} %get-tuple-element.290, s32[1024]{0:T(1024)S(1)} %dynamic_slice.32, bf16[1,88,2048]{2,1,0:T(8,128)(2,1)S(1)} %get-tuple-element.293, bf16[2,88,16384]{2,1,0:T(8,128)(2,1)} %get-tuple-element.292, s32[]{:T(128)S(6)} %select_n.132), kind=kOutput, calls=%fused_computation.5.clone.1 | convolution fusion | flops 377485312 | bytes 8949764 | tf_op jit(solution)/shard_map/while/body/eval_jaxpr/hdq,hdk->hqk/dot_general | solution.py:68
  215.4 4.6 fusion.47
  220.0 5.4 %fusion.49 = f32[1,88,2048]{2,1,0:T(8,128)S(1)} fusion(f32[1024,2048]{1,0:T(8,128)} %get-tuple-element.257, f32[2048]{0:T(1024)S(1)} %bitcast.110, s32[2048]{0:T(1024)S(1)} %get-tuple-element.290, s32[1024]{0:T(1024)S(1)} %dynamic_slice.32, f32[1,88,2048]{2,1,0:T(8,128)S(1)} %get-tuple-element.276, f32[2048]{0:T(1024)S(1)} %bitcast.120, ...), kind=kOutput, calls=%fused_computation.12.clone.1 | convolution fusion | flops 380125184 | bytes 10039305 | tf_op jit(solution)/shard_map/while/body/eval_jaxpr/hqk,hdk->hdq/dot_general | solution.py:76
  225.5 5.6 %fusion.45 = (f32[2048]{0:T(1024)S(1)}, f32[1024,2048]{1,0:T(8,128)}) fusion(s32[2048]{0:T(1024)S(1)} %get-tuple-element.290, s32[1024]{0:T(1024)S(1)} %dynamic_slice.32, bf16[1,88,2048]{2,1,0:T(8,128)(2,1)S(1)} %get-tuple-element.293, bf16[2,88,16384]{2,1,0:T(8,128)(2,1)} %get-tuple-element.292, s32[]{:T(128)S(6)} %select_n.132), kind=kOutput, calls=%fused_computation.5.clone.1 | convolution fusion | flops 377485312 | bytes 8949764 | tf_op jit(solution)/shard_map/while/body/eval_jaxpr/hdq,hdk->hqk/dot_general | solution.py:68
  235.7 5.4 %fusion.49 = f32[1,88,2048]{2,1,0:T(8,128)S(1)} fusion(f32[1024,2048]{1,0:T(8,128)} %get-tuple-element.257, f32[2048]{0:T(1024)S(1)} %bitcast.110, s32[2048]{0:T(1024)S(1)} %get-tuple-element.290, s32[1024]{0:T(1024)S(1)} %dynamic_slice.32, f32[1,88,2048]{2,1,0:T(8,128)S(1)} %get-tuple-element.276, f32[2048]{0:T(1024)S(1)} %bitcast.120, ...), kind=kOutput, calls=%fused_computation.12.clone.1 | convolution fusion | flops 380125184 | bytes 10039305 | tf_op jit(solution)/shard_map/while/body/eval_jaxpr/hqk,hdk->hdq/dot_general | solution.py:76
  241.2 5.6 %fusion.45 = (f32[2048]{0:T(1024)S(1)}, f32[1024,2048]{1,0:T(8,128)}) fusion(s32[2048]{0:T(1024)S(1)} %get-tuple-element.290, s32[1024]{0:T(1024)S(1)} %dynamic_slice.32, bf16[1,88,2048]{2,1,0:T(8,128)(2,1)S(1)} %get-tuple-element.293, bf16[2,88,16384]{2,1,0:T(8,128)(2,1)} %get-tuple-element.292, s32[]{:T(128)S(6)} %select_n.132), kind=kOutput, calls=%fused_computation.5.clone.1 | convolution fusion | flops 377485312 | bytes 8949764 | tf_op jit(solution)/shard_map/while/body/eval_jaxpr/hdq,hdk->hqk/dot_general | solution.py:68
  251.4 5.4 %fusion.49 = f32[1,88,2048]{2,1,0:T(8,128)S(1)} fusion(f32[1024,2048]{1,0:T(8,128)} %get-tuple-element.257, f32[2048]{0:T(1024)S(1)} %bitcast.110, s32[2048]{0:T(1024)S(1)} %get-tuple-element.290, s32[1024]{0:T(1024)S(1)} %dynamic_slice.32, f32[1,88,2048]{2,1,0:T(8,128)S(1)} %get-tuple-element.276, f32[2048]{0:T(1024)S(1)} %bitcast.120, ...), kind=kOutput, calls=%fused_computation.12.clone.1 | convolution fusion | flops 380125184 | bytes 10039305 | tf_op jit(solution)/shard_map/while/body/eval_jaxpr/hqk,hdk->hdq/dot_general | solution.py:76
  256.9 5.6 %fusion.45 = (f32[2048]{0:T(1024)S(1)}, f32[1024,2048]{1,0:T(8,128)}) fusion(s32[2048]{0:T(1024)S(1)} %get-tuple-element.290, s32[1024]{0:T(1024)S(1)} %dynamic_slice.32, bf16[1,88,2048]{2,1,0:T(8,128)(2,1)S(1)} %get-tuple-element.293, bf16[2,88,16384]{2,1,0:T(8,128)(2,1)} %get-tuple-element.292, s32[]{:T(128)S(6)} %select_n.132), kind=kOutput, calls=%fused_computation.5.clone.1 | convolution fusion | flops 377485312 | bytes 8949764 | tf_op jit(solution)/shard_map/while/body/eval_jaxpr/hdq,hdk->hqk/dot_general | solution.py:68
  267.2 5.4 %fusion.49 = f32[1,88,2048]{2,1,0:T(8,128)S(1)} fusion(f32[1024,2048]{1,0:T(8,128)} %get-tuple-element.257, f32[2048]{0:T(1024)S(1)} %bitcast.110, s32[2048]{0:T(1024)S(1)} %get-tuple-element.290, s32[1024]{0:T(1024)S(1)} %dynamic_slice.32, f32[1,88,2048]{2,1,0:T(8,128)S(1)} %get-tuple-element.276, f32[2048]{0:T(1024)S(1)} %bitcast.120, ...), kind=kOutput, calls=%fused_computation.12.clone.1 | convolution fusion | flops 380125184 | bytes 10039305 | tf_op jit(solution)/shard_map/while/body/eval_jaxpr/hqk,hdk->hdq/dot_general | solution.py:76
  272.6 5.6 %fusion.45 = (f32[2048]{0:T(1024)S(1)}, f32[1024,2048]{1,0:T(8,128)}) fusion(s32[2048]{0:T(1024)S(1)} %get-tuple-element.290, s32[1024]{0:T(1024)S(1)} %dynamic_slice.32, bf16[1,88,2048]{2,1,0:T(8,128)(2,1)S(1)} %get-tuple-element.293, bf16[2,88,16384]{2,1,0:T(8,128)(2,1)} %get-tuple-element.292, s32[]{:T(128)S(6)} %select_n.132), kind=kOutput, calls=%fused_computation.5.clone.1 | convolution fusion | flops 377485312 | bytes 8949764 | tf_op jit(solution)/shard_map/while/body/eval_jaxpr/hdq,hdk->hqk/dot_general | solution.py:68
  282.9 5.4 %fusion.49 = f32[1,88,2048]{2,1,0:T(8,128)S(1)} fusion(f32[1024,2048]{1,0:T(8,128)} %get-tuple-element.257, f32[2048]{0:T(1024)S(1)} %bitcast.110, s32[2048]{0:T(1024)S(1)} %get-tuple-element.290, s32[1024]{0:T(1024)S(1)} %dynamic_slice.32, f32[1,88,2048]{2,1,0:T(8,128)S(1)} %get-tuple-element.276, f32[2048]{0:T(1024)S(1)} %bitcast.120, ...), kind=kOutput, calls=%fused_computation.12.clone.1 | convolution fusion | flops 380125184 | bytes 10039305 | tf_op jit(solution)/shard_map/while/body/eval_jaxpr/hqk,hdk->hdq/dot_general | solution.py:76
  288.3 5.6 %fusion.45 = (f32[2048]{0:T(1024)S(1)}, f32[1024,2048]{1,0:T(8,128)}) fusion(s32[2048]{0:T(1024)S(1)} %get-tuple-element.290, s32[1024]{0:T(1024)S(1)} %dynamic_slice.32, bf16[1,88,2048]{2,1,0:T(8,128)(2,1)S(1)} %get-tuple-element.293, bf16[2,88,16384]{2,1,0:T(8,128)(2,1)} %get-tuple-element.292, s32[]{:T(128)S(6)} %select_n.132), kind=kOutput, calls=%fused_computation.5.clone.1 | convolution fusion | flops 377485312 | bytes 8949764 | tf_op jit(solution)/shard_map/while/body/eval_jaxpr/hdq,hdk->hqk/dot_general | solution.py:68
  298.6 5.4 %fusion.49 = f32[1,88,2048]{2,1,0:T(8,128)S(1)} fusion(f32[1024,2048]{1,0:T(8,128)} %get-tuple-element.257, f32[2048]{0:T(1024)S(1)} %bitcast.110, s32[2048]{0:T(1024)S(1)} %get-tuple-element.290, s32[1024]{0:T(1024)S(1)} %dynamic_slice.32, f32[1,88,2048]{2,1,0:T(8,128)S(1)} %get-tuple-element.276, f32[2048]{0:T(1024)S(1)} %bitcast.120, ...), kind=kOutput, calls=%fused_computation.12.clone.1 | convolution fusion | flops 380125184 | bytes 10039305 | tf_op jit(solution)/shard_map/while/body/eval_jaxpr/hqk,hdk->hdq/dot_general | solution.py:76
  304.0 5.6 %fusion.45 = (f32[2048]{0:T(1024)S(1)}, f32[1024,2048]{1,0:T(8,128)}) fusion(s32[2048]{0:T(1024)S(1)} %get-tuple-element.290, s32[1024]{0:T(1024)S(1)} %dynamic_slice.32, bf16[1,88,2048]{2,1,0:T(8,128)(2,1)S(1)} %get-tuple-element.293, bf16[2,88,16384]{2,1,0:T(8,128)(2,1)} %get-tuple-element.292, s32[]{:T(128)S(6)} %select_n.132), kind=kOutput, calls=%fused_computation.5.clone.1 | convolution fusion | flops 377485312 | bytes 8949764 | tf_op jit(solution)/shard_map/while/body/eval_jaxpr/hdq,hdk->hqk/dot_general | solution.py:68
  314.3 5.4 %fusion.49 = f32[1,88,2048]{2,1,0:T(8,128)S(1)} fusion(f32[1024,2048]{1,0:T(8,128)} %get-tuple-element.257, f32[2048]{0:T(1024)S(1)} %bitcast.110, s32[2048]{0:T(1024)S(1)} %get-tuple-element.290, s32[1024]{0:T(1024)S(1)} %dynamic_slice.32, f32[1,88,2048]{2,1,0:T(8,128)S(1)} %get-tuple-element.276, f32[2048]{0:T(1024)S(1)} %bitcast.120, ...), kind=kOutput, calls=%fused_computation.12.clone.1 | convolution fusion | flops 380125184 | bytes 10039305 | tf_op jit(solution)/shard_map/while/body/eval_jaxpr/hqk,hdk->hdq/dot_general | solution.py:76
  319.7 5.6 %fusion.45 = (f32[2048]{0:T(1024)S(1)}, f32[1024,2048]{1,0:T(8,128)}) fusion(s32[2048]{0:T(1024)S(1)} %get-tuple-element.290, s32[1024]{0:T(1024)S(1)} %dynamic_slice.32, bf16[1,88,2048]{2,1,0:T(8,128)(2,1)S(1)} %get-tuple-element.293, bf16[2,88,16384]{2,1,0:T(8,128)(2,1)} %get-tuple-element.292, s32[]{:T(128)S(6)} %select_n.132), kind=kOutput, calls=%fused_computation.5.clone.1 | convolution fusion | flops 377485312 | bytes 8949764 | tf_op jit(solution)/shard_map/while/body/eval_jaxpr/hdq,hdk->hqk/dot_general | solution.py:68
  330.0 5.4 %fusion.49 = f32[1,88,2048]{2,1,0:T(8,128)S(1)} fusion(f32[1024,2048]{1,0:T(8,128)} %get-tuple-element.257, f32[2048]{0:T(1024)S(1)} %bitcast.110, s32[2048]{0:T(1024)S(1)} %get-tuple-element.290, s32[1024]{0:T(1024)S(1)} %dynamic_slice.32, f32[1,88,2048]{2,1,0:T(8,128)S(1)} %get-tuple-element.276, f32[2048]{0:T(1024)S(1)} %bitcast.120, ...), kind=kOutput, calls=%fused_computation.12.clone.1 | convolution fusion | flops 380125184 | bytes 10039305 | tf_op jit(solution)/shard_map/while/body/eval_jaxpr/hqk,hdk->hdq/dot_general | solution.py:76
  335.5 5.6 %fusion.45 = (f32[2048]{0:T(1024)S(1)}, f32[1024,2048]{1,0:T(8,128)}) fusion(s32[2048]{0:T(1024)S(1)} %get-tuple-element.290, s32[1024]{0:T(1024)S(1)} %dynamic_slice.32, bf16[1,88,2048]{2,1,0:T(8,128)(2,1)S(1)} %get-tuple-element.293, bf16[2,88,16384]{2,1,0:T(8,128)(2,1)} %get-tuple-element.292, s32[]{:T(128)S(6)} %select_n.132), kind=kOutput, calls=%fused_computation.5.clone.1 | convolution fusion | flops 377485312 | bytes 8949764 | tf_op jit(solution)/shard_map/while/body/eval_jaxpr/hdq,hdk->hqk/dot_general | solution.py:68
  345.7 5.4 %fusion.49 = f32[1,88,2048]{2,1,0:T(8,128)S(1)} fusion(f32[1024,2048]{1,0:T(8,128)} %get-tuple-element.257, f32[2048]{0:T(1024)S(1)} %bitcast.110, s32[2048]{0:T(1024)S(1)} %get-tuple-element.290, s32[1024]{0:T(1024)S(1)} %dynamic_slice.32, f32[1,88,2048]{2,1,0:T(8,128)S(1)} %get-tuple-element.276, f32[2048]{0:T(1024)S(1)} %bitcast.120, ...), kind=kOutput, calls=%fused_computation.12.clone.1 | convolution fusion | flops 380125184 | bytes 10039305 | tf_op jit(solution)/shard_map/while/body/eval_jaxpr/hqk,hdk->hdq/dot_general | solution.py:76
  351.2 5.6 %fusion.45 = (f32[2048]{0:T(1024)S(1)}, f32[1024,2048]{1,0:T(8,128)}) fusion(s32[2048]{0:T(1024)S(1)} %get-tuple-element.290, s32[1024]{0:T(1024)S(1)} %dynamic_slice.32, bf16[1,88,2048]{2,1,0:T(8,128)(2,1)S(1)} %get-tuple-element.293, bf16[2,88,16384]{2,1,0:T(8,128)(2,1)} %get-tuple-element.292, s32[]{:T(128)S(6)} %select_n.132), kind=kOutput, calls=%fused_computation.5.clone.1 | convolution fusion | flops 377485312 | bytes 8949764 | tf_op jit(solution)/shard_map/while/body/eval_jaxpr/hdq,hdk->hqk/dot_general | solution.py:68
  361.4 5.4 %fusion.49 = f32[1,88,2048]{2,1,0:T(8,128)S(1)} fusion(f32[1024,2048]{1,0:T(8,128)} %get-tuple-element.257, f32[2048]{0:T(1024)S(1)} %bitcast.110, s32[2048]{0:T(1024)S(1)} %get-tuple-element.290, s32[1024]{0:T(1024)S(1)} %dynamic_slice.32, f32[1,88,2048]{2,1,0:T(8,128)S(1)} %get-tuple-element.276, f32[2048]{0:T(1024)S(1)} %bitcast.120, ...), kind=kOutput, calls=%fused_computation.12.clone.1 | convolution fusion | flops 380125184 | bytes 10039305 | tf_op jit(solution)/shard_map/while/body/eval_jaxpr/hqk,hdk->hdq/dot_general | solution.py:76
  366.9 5.6 %fusion.45 = (f32[2048]{0:T(1024)S(1)}, f32[1024,2048]{1,0:T(8,128)}) fusion(s32[2048]{0:T(1024)S(1)} %get-tuple-element.290, s32[1024]{0:T(1024)S(1)} %dynamic_slice.32, bf16[1,88,2048]{2,1,0:T(8,128)(2,1)S(1)} %get-tuple-element.293, bf16[2,88,16384]{2,1,0:T(8,128)(2,1)} %get-tuple-element.292, s32[]{:T(128)S(6)} %select_n.132), kind=kOutput, calls=%fused_computation.5.clone.1 | convolution fusion | flops 377485312 | bytes 8949764 | tf_op jit(solution)/shard_map/while/body/eval_jaxpr/hdq,hdk->hqk/dot_general | solution.py:68
  377.1 5.4 %fusion.49 = f32[1,88,2048]{2,1,0:T(8,128)S(1)} fusion(f32[1024,2048]{1,0:T(8,128)} %get-tuple-element.257, f32[2048]{0:T(1024)S(1)} %bitcast.110, s32[2048]{0:T(1024)S(1)} %get-tuple-element.290, s32[1024]{0:T(1024)S(1)} %dynamic_slice.32, f32[1,88,2048]{2,1,0:T(8,128)S(1)} %get-tuple-element.276, f32[2048]{0:T(1024)S(1)} %bitcast.120, ...), kind=kOutput, calls=%fused_computation.12.clone.1 | convolution fusion | flops 380125184 | bytes 10039305 | tf_op jit(solution)/shard_map/while/body/eval_jaxpr/hqk,hdk->hdq/dot_general | solution.py:76
  382.6 5.6 %fusion.45 = (f32[2048]{0:T(1024)S(1)}, f32[1024,2048]{1,0:T(8,128)}) fusion(s32[2048]{0:T(1024)S(1)} %get-tuple-element.290, s32[1024]{0:T(1024)S(1)} %dynamic_slice.32, bf16[1,88,2048]{2,1,0:T(8,128)(2,1)S(1)} %get-tuple-element.293, bf16[2,88,16384]{2,1,0:T(8,128)(2,1)} %get-tuple-element.292, s32[]{:T(128)S(6)} %select_n.132), kind=kOutput, calls=%fused_computation.5.clone.1 | convolution fusion | flops 377485312 | bytes 8949764 | tf_op jit(solution)/shard_map/while/body/eval_jaxpr/hdq,hdk->hqk/dot_general | solution.py:68
  392.9 5.4 %fusion.49 = f32[1,88,2048]{2,1,0:T(8,128)S(1)} fusion(f32[1024,2048]{1,0:T(8,128)} %get-tuple-element.257, f32[2048]{0:T(1024)S(1)} %bitcast.110, s32[2048]{0:T(1024)S(1)} %get-tuple-element.290, s32[1024]{0:T(1024)S(1)} %dynamic_slice.32, f32[1,88,2048]{2,1,0:T(8,128)S(1)} %get-tuple-element.276, f32[2048]{0:T(1024)S(1)} %bitcast.120, ...), kind=kOutput, calls=%fused_computation.12.clone.1 | convolution fusion | flops 380125184 | bytes 10039305 | tf_op jit(solution)/shard_map/while/body/eval_jaxpr/hqk,hdk->hdq/dot_general | solution.py:76
  399.3 7.2 %all-to-all-start = ((bf16[88,16,128]{2,0,1:T(8,128)(2,1)}), bf16[88,16,128]{2,0,1:T(8,128)(2,1)S(1)}, u32[]{:S(2)}, u32[]{:S(2)}) async-start(bf16[88,16,128]{2,0,1:T(8,128)(2,1)} %copy.35), calls=%async_computation | async-start | bytes 720896 | tf_op jit(solution)/shard_map/all_to_all | solution.py:105
  406.6 7.6 %convert_element_type.50 = f32[1408,2048]{0,1:T(8,128)} convert(bf16[1408,2048]{0,1:T(8,128)(2,1)} %copy.31) | non-fusion elementwise | flops 2883584 | bytes 17301504 | tf_op jit(solution)/shard_map/convert_element_type | solution.py:35
  417.8 13.1 %all_to_all.35 = bf16[16,88,128]{2,1,0:T(8,128)(2,1)S(1)} all-to-all(bf16[16,88,128]{2,1,0:T(8,128)(2,1)S(1)} %bitcast.114), channel_id=1, replica_groups=mesh['row'=8,'col'=16] {'col'}, dimensions={0} | all-to-all | bytes 720896 | tf_op jit(solution)/shard_map/all_to_all | solution.py:118
  434.7 85.2 %all-reduce.2.cloned.1.call-done = bf16[512,1408]{1,0:T(8,128)(2,1)} async-done(((bf16[512,1408]{1,0:T(8,128)(2,1)}), bf16[512,1408]{1,0:T(8,128)(2,1)}) %all-reduce.2.cloned.1.call-update) | async-done | bytes 1441808 | tf_op jit(solution)/shard_map/psum | solution.py:122
  (131 shorter events, 86.1 us)
Async XLA Ops:
  6.5 424.6 %copy-start = (bf16[4,88,1408]{2,1,0:T(8,128)(2,1)S(1)}, bf16[4,88,1408]{2,1,0:T(8,128)(2,1)}, u32[]{:S(2)}) copy-start(bf16[4,88,1408]{2,1,0:T(8,128)(2,1)} %param.22) | copy-start | bytes 2973700
  6.5 62.0 %all-gather.4.cloned.1.call-start = ((), (), s32[]{:S(2)}) async-start(), calls=%async_computation.2 | async-start | bytes 6127616 | tf_op jit(solution)/shard_map/all_gather | solution.py:33
  7.3 132.1 %all-gather.6.cloned.1.call-start = ((), (), s32[]{:S(2)}) async-start(), calls=%async_computation.3 | async-start | bytes 6782976 | tf_op jit(solution)/shard_map/all_gather | solution.py:59
  76.9 4.5 copy-start.1
  81.4 9.0 %copy-start.5 = (bf16[2,88,1408]{2,1,0:T(8,128)(2,1)S(1)}, bf16[2,88,1408]{2,1,0:T(8,128)(2,1)}, u32[]{:S(2)}) copy-start(bf16[2,88,1408]{2,1,0:T(8,128)(2,1)} %param.16) | copy-start | bytes 1486852
  85.3 15.0 %copy-start.3 = (bf16[88,1408]{1,0:T(8,128)(2,1)S(1)}, bf16[88,1408]{1,0:T(8,128)(2,1)}, u32[]{:S(2)}) copy-start(bf16[88,1408]{1,0:T(8,128)(2,1)} %param.15) | copy-start | bytes 743428
  99.5 314.6 %all-gather.8.cloned.1.call-start = ((), (), s32[]{:S(2)}) async-start(), calls=%async_computation.4 | async-start | bytes 4212736 | tf_op jit(solution)/shard_map/all_gather | solution.py:34
  100.3 45.8 %copy-start.2 = (s32[2048]{0:T(1024)S(1)}, s32[2048]{0:T(1024)}, u32[]{:S(2)}) copy-start(s32[2048]{0:T(1024)} %param.19) | copy-start | bytes 24580
  146.1 260.4 %copy-start.4 = (bf16[1408]{0:T(1024)(128)(2,1)S(1)}, bf16[1408]{0:T(1024)(128)(2,1)}, u32[]{:S(2)}) copy-start(bf16[1408]{0:T(1024)(128)(2,1)} %param.21) | copy-start | bytes 8452
  399.3 14.8 %all-to-all-start = ((bf16[88,16,128]{2,0,1:T(8,128)(2,1)}), bf16[88,16,128]{2,0,1:T(8,128)(2,1)S(1)}, u32[]{:S(2)}, u32[]{:S(2)}) async-start(bf16[88,16,128]{2,0,1:T(8,128)(2,1)} %copy.35), calls=%async_computation | async-start | bytes 720896 | tf_op jit(solution)/shard_map/all_to_all | solution.py:105
  406.5 113.4 %all-reduce.2.cloned.1.call-start = ((), (), s32[]{:S(2)}) async-start(), calls=%async_computation.5 | async-start | bytes 2883584 | tf_op jit(solution)/shard_map/psum | solution.py:122
Sparse Core Ops, SparseCore 0:
  9.5 58.9 all-gather.3
  99.7 39.6 all-gather.5
  141.5 50.3 all-gather.7
  433.4 86.4 all-reduce.1

commit v2 on v1

--- a/solution.py
+++ b/solution.py
@@ -115,15 +115,15 @@
         * lax.rsqrt(row_square - row_mean * row_mean + EPSILON)
         * gain_merge.astype(jnp.float32)[:, None]
     ).astype(jnp.bfloat16)
-    merger_in = lax.all_to_all(merger_chunk, "col", 0, 1, tiled=True)
-    merged_rows = tok_rows // 4
-    grouped = merger_in.reshape(local_width, merged_rows, 4)
-    merged = jnp.einsum("cgi,icd->gd", grouped, w_merge, preferred_element_type=jnp.float32)
-    merged_sum = lax.psum(merged.astype(jnp.bfloat16), "col")
+    merge_weight, _ = lax.optimization_barrier((w_merge, pair_all))
+    merge_full = lax.all_gather(merge_weight, "col", axis=1, tiled=True)
+    grouped = merger_chunk.reshape(model_width, chunk // 4, 4)
+    merged_here = jnp.einsum("fgi,ifd->gd", grouped, merge_full, preferred_element_type=jnp.float32)
+    merged_all = lax.all_gather(merged_here.astype(jnp.bfloat16), "col", axis=0, tiled=True)
     wanted_rows = lax.dynamic_index_in_dim(requests[0], col_index, 0, keepdims=False)
     is_valid = wanted_rows >= 0
     safe_index = jnp.where(is_valid, wanted_rows, 0)
-    picked = jnp.where(is_valid[:, None], merged_sum[safe_index], jnp.zeros((), jnp.bfloat16))
+    picked = jnp.where(is_valid[:, None], merged_all[safe_index], jnp.zeros((), jnp.bfloat16))
     return picked.reshape(1, 1, picked.shape[0], model_width)
 
 

time: 534 us -> 486 us (0.910)
  waiting for transfers between devices: 177 us -> 133 us
  blocking collectives: 13.1 us -> 0 us
  matrix products: 187 us -> 194 us
    psum x1 -> x0, waiting for transfers between devices: 85.2 us -> none  [on_device(): merged_sum = lax.psum(merged.astype(jnp.bfloat16), 'col')]
    all_gather x0 -> x2, waiting for transfers between devices: none -> 41.7 us  [the longest x1 41.7 us: on_device(): lax.all_gather(merged_here.astype(jnp.bfloat16), 'col', axis=0, tiled=True)]
    all_to_all x1 -> x0, blocking collectives: 13.1 us -> none  [on_device(): merger_in = lax.all_to_all(merger_chunk, 'col', 0, 1, tiled=True)]
    dot_general x1, matrix products: 2.11 us -> 8.8 us  [on_device(): jnp.einsum('fgi,ifd->gd', grouped, merge_full, preferred_element_type=jnp...]
  transfers between devices with their start and end apart: 5 -> 6, of which waited for: 3 -> 3; matrix products, arithmetic and copies ran while one was open for 52% -> 59% of each run, Pallas kernels for 0% -> 0%
where the time goes in v2:
time: 486 us; the launch traced here: 481 us
  matrix products  194 us (40%)
  waiting for transfers between devices  133 us (27%)
  other arithmetic  99.2 us (20%)
  local copies, waits for them, and re-layouts  33 us (7%)
  between operations  13.4 us (3%)
  starting transfers between devices  7.45 us (2%)
    dot_general x16, matrix products, take_block(): jnp.einsum('hdq,hdk->hqk', query_heads, key_block, preferred_element_type...  89.1 us
    dot_general x16, matrix products, take_block(): jnp.einsum('hqk,hdk->hdq', weights_exp.astype(jnp.bfloat16), value_block,...  88.1 us
    reduce_sum x16, other arithmetic, take_block(): running_sum = running_sum * factor + jnp.sum(weights_exp, axis=2)  74.9 us
    all_gather x1, waiting for transfers between devices, on_device(): full_rows = lax.all_gather(hidden, 'col', axis=0, tiled=True)  56 us
    all_gather x1, waiting for transfers between devices, on_device(): lax.all_gather(merged_here.astype(jnp.bfloat16), 'col', axis=0, tiled=True)  41.7 us
    all_gather x1, waiting for transfers between devices, on_device(): pair_all = lax.all_gather(pair_local, 'row', axis=1, tiled=True)  34.1 us
  transfers between devices with their start and end apart: 6, of which 3 were waited for; matrix products, arithmetic and copies ran while one was open for 59% of the time, Pallas kernels for 0%

profile of v2, /device:TPU:78, one launch (start us, length us, event | category | flops | bytes accessed | tf_op | source)
XLA Modules:
  0.0 481.4 jit_solution(13265763063287293929)
XLA Ops:
  12.5 56.0 %all-gather.6.cloned.1.call-done = bf16[1408,2048]{1,0:T(8,128)(2,1)} async-done(((bf16[88,2048]{1,0:T(8,128)(2,1)}), bf16[1408,2048]{1,0:T(8,128)(2,1)}) %all-gather.6.cloned.1.call-update) | async-done | bytes 5767184 | tf_op jit(solution)/shard_map/all_gather | solution.py:33
  68.5 8.3 %copy.28 = bf16[1408,2048]{0,1:T(8,128)(2,1)} copy(bf16[1408,2048]{1,0:T(8,128)(2,1)} %all-gather.6.cloned.1.call-done) | data formatting | bytes 11534336 | tf_op jit(solution)/shard_map/all_gather | solution.py:33
  85.4 5.0 %gather_fusion = bf16[200,1408]{1,0:T(8,128)(2,1)S(1)} fusion(bf16[1408,2048]{0,1:T(8,128)(2,1)} %multiply_convert_fusion, s32[1024]{0:T(1024)S(1)} %pad_clamp_fusion.1), kind=kCustom, calls=%fused_computation | custom fusion | bytes 1127200 | tf_op jit(solution)/shard_map/jit(_take)/gather | solution.py:45
  90.9 6.9 %scatter_fusion = bf16[2,88,2048]{1,0,2:T(2,128)(2,1)S(1)} fusion(bf16[2,88,2048]{1,0,2:T(2,128)(2,1)S(1)} %copy.30, s32[200]{0:T(256)S(1)} %bitcast.122, bf16[200,2,88]{2,1,0:T(2,128)(2,1)S(1)} %bitcast.115), kind=kCustom, calls=%fused_computation.2 | custom fusion | bytes 212000 | tf_op jit(solution)/shard_map/scatter | solution.py:52
  105.2 34.1 %all-gather.8.cloned.1.call-done = bf16[177,16384]{1,0:T(8,128)(2,1)} async-done(((bf16[177,2048]{1,0:T(8,128)(2,1)}), bf16[177,16384]{1,0:T(8,128)(2,1)}) %all-gather.8.cloned.1.call-update) | async-done | bytes 5799952 | tf_op jit(solution)/shard_map/all_gather | solution.py:59
  139.4 5.8 %slice.29 = bf16[176,16384]{1,0:T(8,128)(2,1)} slice(bf16[177,16384]{1,0:T(8,128)(2,1)} %all-gather.8.cloned.1.call-done), slice={[0:176], [0:16384]} | slice | bytes 11534336 | tf_op jit(solution)/shard_map/slice | solution.py:60
  146.2 254.0 %while.18 = (s32[]{:T(128)}, f32[1,2048]{1,0:T(1,128)S(1)}, f32[1,2048]{1,0:T(1,128)S(1)}, f32[1,88,2048]{2,1,0:T(8,128)S(1)}, s32[2048]{0:T(1024)S(1)}, /*index...) while((s32[]{:T(128)}, f32[1,2048]{1,0:T(1,128)S(1)}, ...), condition=%wide.region_6.7_spmd.clone, body=%wide.region_3.0_spmd.clone.sunk | while | flops 768108544 | bytes 27504848 | solution.py:100
  146.2 5.6 %fusion.45 = (f32[2048]{0:T(1024)S(1)}, f32[1024,2048]{1,0:T(8,128)}) fusion(s32[2048]{0:T(1024)S(1)} %get-tuple-element.292, s32[1024]{0:T(1024)S(1)} %dynamic_slice.32, bf16[1,88,2048]{2,1,0:T(8,128)(2,1)S(1)} %get-tuple-element.295, bf16[2,88,16384]{2,1,0:T(8,128)(2,1)} %get-tuple-element.294, s32[]{:T(128)S(6)} %select_n.132), kind=kOutput, calls=%fused_computation.5.clone.1 | convolution fusion | flops 377485312 | bytes 8949764 | tf_op jit(solution)/shard_map/while/body/eval_jaxpr/hdq,hdk->hqk/dot_general | solution.py:68
  151.8 4.8 fusion.47
  156.6 5.5 %fusion.49 = f32[1,88,2048]{2,1,0:T(8,128)S(1)} fusion(f32[1024,2048]{1,0:T(8,128)} %get-tuple-element.259, f32[2048]{0:T(1024)S(1)} %bitcast.110, s32[2048]{0:T(1024)S(1)} %get-tuple-element.292, s32[1024]{0:T(1024)S(1)} %dynamic_slice.32, f32[1,88,2048]{2,1,0:T(8,128)S(1)} %get-tuple-element.278, f32[2048]{0:T(1024)S(1)} %bitcast.117, ...), kind=kOutput, calls=%fused_computation.12.clone.1 | convolution fusion | flops 380125184 | bytes 10039305 | tf_op jit(solution)/shard_map/while/body/eval_jaxpr/hqk,hdk->hdq/dot_general | solution.py:76
  162.1 5.6 %fusion.45 = (f32[2048]{0:T(1024)S(1)}, f32[1024,2048]{1,0:T(8,128)}) fusion(s32[2048]{0:T(1024)S(1)} %get-tuple-element.292, s32[1024]{0:T(1024)S(1)} %dynamic_slice.32, bf16[1,88,2048]{2,1,0:T(8,128)(2,1)S(1)} %get-tuple-element.295, bf16[2,88,16384]{2,1,0:T(8,128)(2,1)} %get-tuple-element.294, s32[]{:T(128)S(6)} %select_n.132), kind=kOutput, calls=%fused_computation.5.clone.1 | convolution fusion | flops 377485312 | bytes 8949764 | tf_op jit(solution)/shard_map/while/body/eval_jaxpr/hdq,hdk->hqk/dot_general | solution.py:68
  172.3 5.7 %fusion.49 = f32[1,88,2048]{2,1,0:T(8,128)S(1)} fusion(f32[1024,2048]{1,0:T(8,128)} %get-tuple-element.259, f32[2048]{0:T(1024)S(1)} %bitcast.110, s32[2048]{0:T(1024)S(1)} %get-tuple-element.292, s32[1024]{0:T(1024)S(1)} %dynamic_slice.32, f32[1,88,2048]{2,1,0:T(8,128)S(1)} %get-tuple-element.278, f32[2048]{0:T(1024)S(1)} %bitcast.117, ...), kind=kOutput, calls=%fused_computation.12.clone.1 | convolution fusion | flops 380125184 | bytes 10039305 | tf_op jit(solution)/shard_map/while/body/eval_jaxpr/hqk,hdk->hdq/dot_general | solution.py:76
  178.1 5.6 %fusion.45 = (f32[2048]{0:T(1024)S(1)}, f32[1024,2048]{1,0:T(8,128)}) fusion(s32[2048]{0:T(1024)S(1)} %get-tuple-element.292, s32[1024]{0:T(1024)S(1)} %dynamic_slice.32, bf16[1,88,2048]{2,1,0:T(8,128)(2,1)S(1)} %get-tuple-element.295, bf16[2,88,16384]{2,1,0:T(8,128)(2,1)} %get-tuple-element.294, s32[]{:T(128)S(6)} %select_n.132), kind=kOutput, calls=%fused_computation.5.clone.1 | convolution fusion | flops 377485312 | bytes 8949764 | tf_op jit(solution)/shard_map/while/body/eval_jaxpr/hdq,hdk->hqk/dot_general | solution.py:68
  183.7 4.7 fusion.47
  188.5 5.4 %fusion.49 = f32[1,88,2048]{2,1,0:T(8,128)S(1)} fusion(f32[1024,2048]{1,0:T(8,128)} %get-tuple-element.259, f32[2048]{0:T(1024)S(1)} %bitcast.110, s32[2048]{0:T(1024)S(1)} %get-tuple-element.292, s32[1024]{0:T(1024)S(1)} %dynamic_slice.32, f32[1,88,2048]{2,1,0:T(8,128)S(1)} %get-tuple-element.278, f32[2048]{0:T(1024)S(1)} %bitcast.117, ...), kind=kOutput, calls=%fused_computation.12.clone.1 | convolution fusion | flops 380125184 | bytes 10039305 | tf_op jit(solution)/shard_map/while/body/eval_jaxpr/hqk,hdk->hdq/dot_general | solution.py:76
  193.9 5.6 %fusion.45 = (f32[2048]{0:T(1024)S(1)}, f32[1024,2048]{1,0:T(8,128)}) fusion(s32[2048]{0:T(1024)S(1)} %get-tuple-element.292, s32[1024]{0:T(1024)S(1)} %dynamic_slice.32, bf16[1,88,2048]{2,1,0:T(8,128)(2,1)S(1)} %get-tuple-element.295, bf16[2,88,16384]{2,1,0:T(8,128)(2,1)} %get-tuple-element.294, s32[]{:T(128)S(6)} %select_n.132), kind=kOutput, calls=%fused_computation.5.clone.1 | convolution fusion | flops 377485312 | bytes 8949764 | tf_op jit(solution)/shard_map/while/body/eval_jaxpr/hdq,hdk->hqk/dot_general | solution.py:68
  204.2 6.2 %fusion.49 = f32[1,88,2048]{2,1,0:T(8,128)S(1)} fusion(f32[1024,2048]{1,0:T(8,128)} %get-tuple-element.259, f32[2048]{0:T(1024)S(1)} %bitcast.110, s32[2048]{0:T(1024)S(1)} %get-tuple-element.292, s32[1024]{0:T(1024)S(1)} %dynamic_slice.32, f32[1,88,2048]{2,1,0:T(8,128)S(1)} %get-tuple-element.278, f32[2048]{0:T(1024)S(1)} %bitcast.117, ...), kind=kOutput, calls=%fused_computation.12.clone.1 | convolution fusion | flops 380125184 | bytes 10039305 | tf_op jit(solution)/shard_map/while/body/eval_jaxpr/hqk,hdk->hdq/dot_general | solution.py:76
  210.4 5.6 %fusion.45 = (f32[2048]{0:T(1024)S(1)}, f32[1024,2048]{1,0:T(8,128)}) fusion(s32[2048]{0:T(1024)S(1)} %get-tuple-element.292, s32[1024]{0:T(1024)S(1)} %dynamic_slice.32, bf16[1,88,2048]{2,1,0:T(8,128)(2,1)S(1)} %get-tuple-element.295, bf16[2,88,16384]{2,1,0:T(8,128)(2,1)} %get-tuple-element.294, s32[]{:T(128)S(6)} %select_n.132), kind=kOutput, calls=%fused_computation.5.clone.1 | convolution fusion | flops 377485312 | bytes 8949764 | tf_op jit(solution)/shard_map/while/body/eval_jaxpr/hdq,hdk->hqk/dot_general | solution.py:68
  220.8 5.4 %fusion.49 = f32[1,88,2048]{2,1,0:T(8,128)S(1)} fusion(f32[1024,2048]{1,0:T(8,128)} %get-tuple-element.259, f32[2048]{0:T(1024)S(1)} %bitcast.110, s32[2048]{0:T(1024)S(1)} %get-tuple-element.292, s32[1024]{0:T(1024)S(1)} %dynamic_slice.32, f32[1,88,2048]{2,1,0:T(8,128)S(1)} %get-tuple-element.278, f32[2048]{0:T(1024)S(1)} %bitcast.117, ...), kind=kOutput, calls=%fused_computation.12.clone.1 | convolution fusion | flops 380125184 | bytes 10039305 | tf_op jit(solution)/shard_map/while/body/eval_jaxpr/hqk,hdk->hdq/dot_general | solution.py:76
  226.2 5.6 %fusion.45 = (f32[2048]{0:T(1024)S(1)}, f32[1024,2048]{1,0:T(8,128)}) fusion(s32[2048]{0:T(1024)S(1)} %get-tuple-element.292, s32[1024]{0:T(1024)S(1)} %dynamic_slice.32, bf16[1,88,2048]{2,1,0:T(8,128)(2,1)S(1)} %get-tuple-element.295, bf16[2,88,16384]{2,1,0:T(8,128)(2,1)} %get-tuple-element.294, s32[]{:T(128)S(6)} %select_n.132), kind=kOutput, calls=%fused_computation.5.clone.1 | convolution fusion | flops 377485312 | bytes 8949764 | tf_op jit(solution)/shard_map/while/body/eval_jaxpr/hdq,hdk->hqk/dot_general | solution.py:68
  231.8 5.3 %fusion.47 = f32[2048]{0:T(1024)S(1)} fusion(f32[1024,2048]{1,0:T(8,128)} %get-tuple-element.259, f32[2048]{0:T(1024)S(1)} %bitcast.109, s32[2048]{0:T(1024)S(1)} %get-tuple-element.292, s32[1024]{0:T(1024)S(1)} %dynamic_slice.32), kind=kLoop, calls=%fused_computation.9.clone.1 | loop fusion | flops 10483712 | bytes 8417280 | tf_op jit(solution)/shard_map/while/body/eval_jaxpr/reduce_sum | solution.py:75
  237.1 5.4 %fusion.49 = f32[1,88,2048]{2,1,0:T(8,128)S(1)} fusion(f32[1024,2048]{1,0:T(8,128)} %get-tuple-element.259, f32[2048]{0:T(1024)S(1)} %bitcast.110, s32[2048]{0:T(1024)S(1)} %get-tuple-element.292, s32[1024]{0:T(1024)S(1)} %dynamic_slice.32, f32[1,88,2048]{2,1,0:T(8,128)S(1)} %get-tuple-element.278, f32[2048]{0:T(1024)S(1)} %bitcast.117, ...), kind=kOutput, calls=%fused_computation.12.clone.1 | convolution fusion | flops 380125184 | bytes 10039305 | tf_op jit(solution)/shard_map/while/body/eval_jaxpr/hqk,hdk->hdq/dot_general | solution.py:76
  242.6 5.6 %fusion.45 = (f32[2048]{0:T(1024)S(1)}, f32[1024,2048]{1,0:T(8,128)}) fusion(s32[2048]{0:T(1024)S(1)} %get-tuple-element.292, s32[1024]{0:T(1024)S(1)} %dynamic_slice.32, bf16[1,88,2048]{2,1,0:T(8,128)(2,1)S(1)} %get-tuple-element.295, bf16[2,88,16384]{2,1,0:T(8,128)(2,1)} %get-tuple-element.294, s32[]{:T(128)S(6)} %select_n.132), kind=kOutput, calls=%fused_computation.5.clone.1 | convolution fusion | flops 377485312 | bytes 8949764 | tf_op jit(solution)/shard_map/while/body/eval_jaxpr/hdq,hdk->hqk/dot_general | solution.py:68
  248.2 4.8 fusion.47
  253.0 5.7 %fusion.49 = f32[1,88,2048]{2,1,0:T(8,128)S(1)} fusion(f32[1024,2048]{1,0:T(8,128)} %get-tuple-element.259, f32[2048]{0:T(1024)S(1)} %bitcast.110, s32[2048]{0:T(1024)S(1)} %get-tuple-element.292, s32[1024]{0:T(1024)S(1)} %dynamic_slice.32, f32[1,88,2048]{2,1,0:T(8,128)S(1)} %get-tuple-element.278, f32[2048]{0:T(1024)S(1)} %bitcast.117, ...), kind=kOutput, calls=%fused_computation.12.clone.1 | convolution fusion | flops 380125184 | bytes 10039305 | tf_op jit(solution)/shard_map/while/body/eval_jaxpr/hqk,hdk->hdq/dot_general | solution.py:76
  258.7 5.6 %fusion.45 = (f32[2048]{0:T(1024)S(1)}, f32[1024,2048]{1,0:T(8,128)}) fusion(s32[2048]{0:T(1024)S(1)} %get-tuple-element.292, s32[1024]{0:T(1024)S(1)} %dynamic_slice.32, bf16[1,88,2048]{2,1,0:T(8,128)(2,1)S(1)} %get-tuple-element.295, bf16[2,88,16384]{2,1,0:T(8,128)(2,1)} %get-tuple-element.294, s32[]{:T(128)S(6)} %select_n.132), kind=kOutput, calls=%fused_computation.5.clone.1 | convolution fusion | flops 377485312 | bytes 8949764 | tf_op jit(solution)/shard_map/while/body/eval_jaxpr/hdq,hdk->hqk/dot_general | solution.py:68
  264.3 4.7 fusion.47
  269.1 5.6 %fusion.49 = f32[1,88,2048]{2,1,0:T(8,128)S(1)} fusion(f32[1024,2048]{1,0:T(8,128)} %get-tuple-element.259, f32[2048]{0:T(1024)S(1)} %bitcast.110, s32[2048]{0:T(1024)S(1)} %get-tuple-element.292, s32[1024]{0:T(1024)S(1)} %dynamic_slice.32, f32[1,88,2048]{2,1,0:T(8,128)S(1)} %get-tuple-element.278, f32[2048]{0:T(1024)S(1)} %bitcast.117, ...), kind=kOutput, calls=%fused_computation.12.clone.1 | convolution fusion | flops 380125184 | bytes 10039305 | tf_op jit(solution)/shard_map/while/body/eval_jaxpr/hqk,hdk->hdq/dot_general | solution.py:76
  274.8 5.6 %fusion.45 = (f32[2048]{0:T(1024)S(1)}, f32[1024,2048]{1,0:T(8,128)}) fusion(s32[2048]{0:T(1024)S(1)} %get-tuple-element.292, s32[1024]{0:T(1024)S(1)} %dynamic_slice.32, bf16[1,88,2048]{2,1,0:T(8,128)(2,1)S(1)} %get-tuple-element.295, bf16[2,88,16384]{2,1,0:T(8,128)(2,1)} %get-tuple-element.294, s32[]{:T(128)S(6)} %select_n.132), kind=kOutput, calls=%fused_computation.5.clone.1 | convolution fusion | flops 377485312 | bytes 8949764 | tf_op jit(solution)/shard_map/while/body/eval_jaxpr/hdq,hdk->hqk/dot_general | solution.py:68
  285.1 5.4 %fusion.49 = f32[1,88,2048]{2,1,0:T(8,128)S(1)} fusion(f32[1024,2048]{1,0:T(8,128)} %get-tuple-element.259, f32[2048]{0:T(1024)S(1)} %bitcast.110, s32[2048]{0:T(1024)S(1)} %get-tuple-element.292, s32[1024]{0:T(1024)S(1)} %dynamic_slice.32, f32[1,88,2048]{2,1,0:T(8,128)S(1)} %get-tuple-element.278, f32[2048]{0:T(1024)S(1)} %bitcast.117, ...), kind=kOutput, calls=%fused_computation.12.clone.1 | convolution fusion | flops 380125184 | bytes 10039305 | tf_op jit(solution)/shard_map/while/body/eval_jaxpr/hqk,hdk->hdq/dot_general | solution.py:76
  290.6 5.6 %fusion.45 = (f32[2048]{0:T(1024)S(1)}, f32[1024,2048]{1,0:T(8,128)}) fusion(s32[2048]{0:T(1024)S(1)} %get-tuple-element.292, s32[1024]{0:T(1024)S(1)} %dynamic_slice.32, bf16[1,88,2048]{2,1,0:T(8,128)(2,1)S(1)} %get-tuple-element.295, bf16[2,88,16384]{2,1,0:T(8,128)(2,1)} %get-tuple-element.294, s32[]{:T(128)S(6)} %select_n.132), kind=kOutput, calls=%fused_computation.5.clone.1 | convolution fusion | flops 377485312 | bytes 8949764 | tf_op jit(solution)/shard_map/while/body/eval_jaxpr/hdq,hdk->hqk/dot_general | solution.py:68
  300.8 5.4 %fusion.49 = f32[1,88,2048]{2,1,0:T(8,128)S(1)} fusion(f32[1024,2048]{1,0:T(8,128)} %get-tuple-element.259, f32[2048]{0:T(1024)S(1)} %bitcast.110, s32[2048]{0:T(1024)S(1)} %get-tuple-element.292, s32[1024]{0:T(1024)S(1)} %dynamic_slice.32, f32[1,88,2048]{2,1,0:T(8,128)S(1)} %get-tuple-element.278, f32[2048]{0:T(1024)S(1)} %bitcast.117, ...), kind=kOutput, calls=%fused_computation.12.clone.1 | convolution fusion | flops 380125184 | bytes 10039305 | tf_op jit(solution)/shard_map/while/body/eval_jaxpr/hqk,hdk->hdq/dot_general | solution.py:76
  306.2 5.6 %fusion.45 = (f32[2048]{0:T(1024)S(1)}, f32[1024,2048]{1,0:T(8,128)}) fusion(s32[2048]{0:T(1024)S(1)} %get-tuple-element.292, s32[1024]{0:T(1024)S(1)} %dynamic_slice.32, bf16[1,88,2048]{2,1,0:T(8,128)(2,1)S(1)} %get-tuple-element.295, bf16[2,88,16384]{2,1,0:T(8,128)(2,1)} %get-tuple-element.294, s32[]{:T(128)S(6)} %select_n.132), kind=kOutput, calls=%fused_computation.5.clone.1 | convolution fusion | flops 377485312 | bytes 8949764 | tf_op jit(solution)/shard_map/while/body/eval_jaxpr/hdq,hdk->hqk/dot_general | solution.py:68
  316.4 5.4 %fusion.49 = f32[1,88,2048]{2,1,0:T(8,128)S(1)} fusion(f32[1024,2048]{1,0:T(8,128)} %get-tuple-element.259, f32[2048]{0:T(1024)S(1)} %bitcast.110, s32[2048]{0:T(1024)S(1)} %get-tuple-element.292, s32[1024]{0:T(1024)S(1)} %dynamic_slice.32, f32[1,88,2048]{2,1,0:T(8,128)S(1)} %get-tuple-element.278, f32[2048]{0:T(1024)S(1)} %bitcast.117, ...), kind=kOutput, calls=%fused_computation.12.clone.1 | convolution fusion | flops 380125184 | bytes 10039305 | tf_op jit(solution)/shard_map/while/body/eval_jaxpr/hqk,hdk->hdq/dot_general | solution.py:76
  321.9 5.6 %fusion.45 = (f32[2048]{0:T(1024)S(1)}, f32[1024,2048]{1,0:T(8,128)}) fusion(s32[2048]{0:T(1024)S(1)} %get-tuple-element.292, s32[1024]{0:T(1024)S(1)} %dynamic_slice.32, bf16[1,88,2048]{2,1,0:T(8,128)(2,1)S(1)} %get-tuple-element.295, bf16[2,88,16384]{2,1,0:T(8,128)(2,1)} %get-tuple-element.294, s32[]{:T(128)S(6)} %select_n.132), kind=kOutput, calls=%fused_computation.5.clone.1 | convolution fusion | flops 377485312 | bytes 8949764 | tf_op jit(solution)/shard_map/while/body/eval_jaxpr/hdq,hdk->hqk/dot_general | solution.py:68
  332.1 5.4 %fusion.49 = f32[1,88,2048]{2,1,0:T(8,128)S(1)} fusion(f32[1024,2048]{1,0:T(8,128)} %get-tuple-element.259, f32[2048]{0:T(1024)S(1)} %bitcast.110, s32[2048]{0:T(1024)S(1)} %get-tuple-element.292, s32[1024]{0:T(1024)S(1)} %dynamic_slice.32, f32[1,88,2048]{2,1,0:T(8,128)S(1)} %get-tuple-element.278, f32[2048]{0:T(1024)S(1)} %bitcast.117, ...), kind=kOutput, calls=%fused_computation.12.clone.1 | convolution fusion | flops 380125184 | bytes 10039305 | tf_op jit(solution)/shard_map/while/body/eval_jaxpr/hqk,hdk->hdq/dot_general | solution.py:76
  337.6 5.6 %fusion.45 = (f32[2048]{0:T(1024)S(1)}, f32[1024,2048]{1,0:T(8,128)}) fusion(s32[2048]{0:T(1024)S(1)} %get-tuple-element.292, s32[1024]{0:T(1024)S(1)} %dynamic_slice.32, bf16[1,88,2048]{2,1,0:T(8,128)(2,1)S(1)} %get-tuple-element.295, bf16[2,88,16384]{2,1,0:T(8,128)(2,1)} %get-tuple-element.294, s32[]{:T(128)S(6)} %select_n.132), kind=kOutput, calls=%fused_computation.5.clone.1 | convolution fusion | flops 377485312 | bytes 8949764 | tf_op jit(solution)/shard_map/while/body/eval_jaxpr/hdq,hdk->hqk/dot_general | solution.py:68
  347.8 5.4 %fusion.49 = f32[1,88,2048]{2,1,0:T(8,128)S(1)} fusion(f32[1024,2048]{1,0:T(8,128)} %get-tuple-element.259, f32[2048]{0:T(1024)S(1)} %bitcast.110, s32[2048]{0:T(1024)S(1)} %get-tuple-element.292, s32[1024]{0:T(1024)S(1)} %dynamic_slice.32, f32[1,88,2048]{2,1,0:T(8,128)S(1)} %get-tuple-element.278, f32[2048]{0:T(1024)S(1)} %bitcast.117, ...), kind=kOutput, calls=%fused_computation.12.clone.1 | convolution fusion | flops 380125184 | bytes 10039305 | tf_op jit(solution)/shard_map/while/body/eval_jaxpr/hqk,hdk->hdq/dot_general | solution.py:76
  353.2 5.6 %fusion.45 = (f32[2048]{0:T(1024)S(1)}, f32[1024,2048]{1,0:T(8,128)}) fusion(s32[2048]{0:T(1024)S(1)} %get-tuple-element.292, s32[1024]{0:T(1024)S(1)} %dynamic_slice.32, bf16[1,88,2048]{2,1,0:T(8,128)(2,1)S(1)} %get-tuple-element.295, bf16[2,88,16384]{2,1,0:T(8,128)(2,1)} %get-tuple-element.294, s32[]{:T(128)S(6)} %select_n.132), kind=kOutput, calls=%fused_computation.5.clone.1 | convolution fusion | flops 377485312 | bytes 8949764 | tf_op jit(solution)/shard_map/while/body/eval_jaxpr/hdq,hdk->hqk/dot_general | solution.py:68
  363.4 5.4 %fusion.49 = f32[1,88,2048]{2,1,0:T(8,128)S(1)} fusion(f32[1024,2048]{1,0:T(8,128)} %get-tuple-element.259, f32[2048]{0:T(1024)S(1)} %bitcast.110, s32[2048]{0:T(1024)S(1)} %get-tuple-element.292, s32[1024]{0:T(1024)S(1)} %dynamic_slice.32, f32[1,88,2048]{2,1,0:T(8,128)S(1)} %get-tuple-element.278, f32[2048]{0:T(1024)S(1)} %bitcast.117, ...), kind=kOutput, calls=%fused_computation.12.clone.1 | convolution fusion | flops 380125184 | bytes 10039305 | tf_op jit(solution)/shard_map/while/body/eval_jaxpr/hqk,hdk->hdq/dot_general | solution.py:76
  368.9 5.6 %fusion.45 = (f32[2048]{0:T(1024)S(1)}, f32[1024,2048]{1,0:T(8,128)}) fusion(s32[2048]{0:T(1024)S(1)} %get-tuple-element.292, s32[1024]{0:T(1024)S(1)} %dynamic_slice.32, bf16[1,88,2048]{2,1,0:T(8,128)(2,1)S(1)} %get-tuple-element.295, bf16[2,88,16384]{2,1,0:T(8,128)(2,1)} %get-tuple-element.294, s32[]{:T(128)S(6)} %select_n.132), kind=kOutput, calls=%fused_computation.5.clone.1 | convolution fusion | flops 377485312 | bytes 8949764 | tf_op jit(solution)/shard_map/while/body/eval_jaxpr/hdq,hdk->hqk/dot_general | solution.py:68
  379.1 5.4 %fusion.49 = f32[1,88,2048]{2,1,0:T(8,128)S(1)} fusion(f32[1024,2048]{1,0:T(8,128)} %get-tuple-element.259, f32[2048]{0:T(1024)S(1)} %bitcast.110, s32[2048]{0:T(1024)S(1)} %get-tuple-element.292, s32[1024]{0:T(1024)S(1)} %dynamic_slice.32, f32[1,88,2048]{2,1,0:T(8,128)S(1)} %get-tuple-element.278, f32[2048]{0:T(1024)S(1)} %bitcast.117, ...), kind=kOutput, calls=%fused_computation.12.clone.1 | convolution fusion | flops 380125184 | bytes 10039305 | tf_op jit(solution)/shard_map/while/body/eval_jaxpr/hqk,hdk->hdq/dot_general | solution.py:76
  384.6 5.6 %fusion.45 = (f32[2048]{0:T(1024)S(1)}, f32[1024,2048]{1,0:T(8,128)}) fusion(s32[2048]{0:T(1024)S(1)} %get-tuple-element.292, s32[1024]{0:T(1024)S(1)} %dynamic_slice.32, bf16[1,88,2048]{2,1,0:T(8,128)(2,1)S(1)} %get-tuple-element.295, bf16[2,88,16384]{2,1,0:T(8,128)(2,1)} %get-tuple-element.294, s32[]{:T(128)S(6)} %select_n.132), kind=kOutput, calls=%fused_computation.5.clone.1 | convolution fusion | flops 377485312 | bytes 8949764 | tf_op jit(solution)/shard_map/while/body/eval_jaxpr/hdq,hdk->hqk/dot_general | solution.py:68
  394.8 5.4 %fusion.49 = f32[1,88,2048]{2,1,0:T(8,128)S(1)} fusion(f32[1024,2048]{1,0:T(8,128)} %get-tuple-element.259, f32[2048]{0:T(1024)S(1)} %bitcast.110, s32[2048]{0:T(1024)S(1)} %get-tuple-element.292, s32[1024]{0:T(1024)S(1)} %dynamic_slice.32, f32[1,88,2048]{2,1,0:T(8,128)S(1)} %get-tuple-element.278, f32[2048]{0:T(1024)S(1)} %bitcast.117, ...), kind=kOutput, calls=%fused_computation.12.clone.1 | convolution fusion | flops 380125184 | bytes 10039305 | tf_op jit(solution)/shard_map/while/body/eval_jaxpr/hqk,hdk->hdq/dot_general | solution.py:76
  401.2 7.1 %all-to-all-start = ((bf16[88,16,128]{2,0,1:T(8,128)(2,1)}), bf16[88,16,128]{2,0,1:T(8,128)(2,1)S(1)}, u32[]{:S(2)}, u32[]{:S(2)}) async-start(bf16[88,16,128]{2,0,1:T(8,128)(2,1)} %copy.32), calls=%async_computation | async-start | bytes 720896 | tf_op jit(solution)/shard_map/all_to_all | solution.py:105
  408.4 7.7 %convert_element_type.50 = f32[1408,2048]{0,1:T(8,128)} convert(bf16[1408,2048]{0,1:T(8,128)(2,1)} %copy.28) | non-fusion elementwise | flops 2883584 | bytes 17301504 | tf_op jit(solution)/shard_map/convert_element_type | solution.py:35
  419.6 8.8 %fusion.23 = bf16[32,1408]{1,0:T(8,128)(2,1)} fusion(bf16[4,1408,1408]{2,1,0:T(8,128)(2,1)} %all-gather.12.cloned.1.call-done, bf16[1408,32,4]{0,2,1:T(4,128)(2,1)S(1)} %reshape.212), kind=kOutput, calls=%fused_computation.36 | convolution fusion | flops 507555840 | bytes 16310272 | tf_op jit(solution)/shard_map/fgi,ifd->gd/dot_general | solution.py:121
  429.8 41.7 %all-gather.14.cloned.1.call-done = bf16[512,1408]{1,0:T(8,128)(2,1)} async-done(((bf16[32,1408]{1,0:T(8,128)(2,1)}), bf16[512,1408]{1,0:T(8,128)(2,1)}) %all-gather.14.cloned.1.call-update) | async-done | bytes 1441808 | tf_op jit(solution)/shard_map/all_gather | solution.py:122
  (132 shorter events, 84.3 us)
Async XLA Ops:
  6.5 83.8 %copy-start = (bf16[2,88,1408]{2,1,0:T(8,128)(2,1)S(1)}, bf16[2,88,1408]{2,1,0:T(8,128)(2,1)}, u32[]{:S(2)}) copy-start(bf16[2,88,1408]{2,1,0:T(8,128)(2,1)} %param.16) | copy-start | bytes 1486852
  6.5 62.0 %all-gather.6.cloned.1.call-start = ((), (), s32[]{:S(2)}) async-start(), calls=%async_computation.1 | async-start | bytes 6127616 | tf_op jit(solution)/shard_map/all_gather | solution.py:33
  7.3 132.1 %all-gather.8.cloned.1.call-start = ((), (), s32[]{:S(2)}) async-start(), calls=%async_computation.2 | async-start | bytes 6782976 | tf_op jit(solution)/shard_map/all_gather | solution.py:59
  76.8 4.5 copy-start.2
  85.4 15.2 %copy-start.4 = (bf16[88,1408]{1,0:T(8,128)(2,1)S(1)}, bf16[88,1408]{1,0:T(8,128)(2,1)}, u32[]{:S(2)}) copy-start(bf16[88,1408]{1,0:T(8,128)(2,1)} %param.15) | copy-start | bytes 743428
  99.6 316.5 %all-gather.10.cloned.1.call-start = ((), (), s32[]{:S(2)}) async-start(), calls=%async_computation.3 | async-start | bytes 4212736 | tf_op jit(solution)/shard_map/all_gather | solution.py:34
  100.3 319.3 %all-gather.12.cloned.1.call-start = ((), (), s32[]{:S(2)}) async-start(), calls=%async_computation.4 | async-start | bytes 16850944 | tf_op jit(solution)/shard_map/all_gather | solution.py:119
  100.6 45.6 %copy-start.3 = (s32[2048]{0:T(1024)S(1)}, s32[2048]{0:T(1024)}, u32[]{:S(2)}) copy-start(s32[2048]{0:T(1024)} %param.19) | copy-start | bytes 24580
  146.2 262.2 %copy-start.5 = (bf16[1408]{0:T(1024)(128)(2,1)S(1)}, bf16[1408]{0:T(1024)(128)(2,1)}, u32[]{:S(2)}) copy-start(bf16[1408]{0:T(1024)(128)(2,1)} %param.21) | copy-start | bytes 8452
  401.2 14.9 %all-to-all-start = ((bf16[88,16,128]{2,0,1:T(8,128)(2,1)}), bf16[88,16,128]{2,0,1:T(8,128)(2,1)S(1)}, u32[]{:S(2)}, u32[]{:S(2)}) async-start(bf16[88,16,128]{2,0,1:T(8,128)(2,1)} %copy.32), calls=%async_computation | async-start | bytes 720896 | tf_op jit(solution)/shard_map/all_to_all | solution.py:105
  408.3 63.2 %all-gather.14.cloned.1.call-start = ((), (), s32[]{:S(2)}) async-start(), calls=%async_computation.5 | async-start | bytes 1531904 | tf_op jit(solution)/shard_map/all_gather | solution.py:122
  419.5 55.4 %copy-start.1 = (bf16[2,88,1408]{2,1,0:T(8,128)(2,1)S(1)}, bf16[2,88,1408]{2,1,0:T(8,128)(2,1)}, u32[]{:S(2)}) copy-start(bf16[2,88,1408]{2,1,0:T(8,128)(2,1)} %param.16) | copy-start | bytes 1486852
Sparse Core Ops, SparseCore 0:
  9.5 58.9 all-gather.5
  99.7 39.6 all-gather.7
  141.5 50.3 all-gather.9
  194.0 106.2 all-gather.11
  428.6 42.9 all-gather.13

commit v3 on v2

v3 whole, which is shorter than its diff:
```python
import jax
import jax.numpy as jnp
from jax import lax
import functools
from jax.experimental import pallas as pl
from jax.experimental.pallas import tpu as pltpu
from jax.sharding import PartitionSpec as P

HD = 88


EPSILON = 1e-06
MASKED = -1e30
PADW = 96
Q_BLOCK = 512
K_BLOCK = 1024


def _attn_kernel(kb_map, flags, q_ref, qs_ref, k_ref, v_ref, o_ref, m_ref, l_ref, acc_ref, *, scale, n_steps):
    qb = pl.program_id(0)
    j = pl.program_id(1)
    flag = flags[qb, j]

    @pl.when(j == 0)
    def _():
        m_ref[...] = jnp.full(m_ref.shape, MASKED, jnp.float32)
        l_ref[...] = jnp.zeros(l_ref.shape, jnp.float32)
        acc_ref[...] = jnp.zeros(acc_ref.shape, jnp.float32)

    def step(masked):
        q = q_ref[...]
        k = k_ref[...]
        s = jnp.dot(q, k, preferred_element_type=jnp.float32) * scale
        if masked:
            key_seg = k[HD:HD + 1, :].astype(jnp.float32)
            s = jnp.where(qs_ref[...] == key_seg, s, MASKED)
        m_prev = m_ref[...]
        m_new = jnp.maximum(m_prev, jnp.max(s, axis=1, keepdims=True))
        p = jnp.exp(s - m_new)
        alpha = jnp.exp(m_prev - m_new)
        l_ref[...] = alpha * l_ref[...] + jnp.sum(p, axis=1, keepdims=True)
        pv = lax.dot_general(
            p.astype(jnp.bfloat16), v_ref[...], (((1,), (1,)), ((), ())),
            preferred_element_type=jnp.float32,
        )
        acc_ref[...] = alpha * acc_ref[...] + pv
        m_ref[...] = m_new

    @pl.when(flag == 1)
    def _():
        step(True)

    @pl.when(flag == 2)
    def _():
        step(False)

    @pl.when(j == n_steps - 1)
    def _():
        o_ref[...] = (acc_ref[...] / l_ref[...]).astype(o_ref.dtype)


def block_tables(q_seg, k_seg, q_start):
    n_q = q_seg.shape[0] // Q_BLOCK
    n_k = k_seg.shape[0] // K_BLOCK
    values = jnp.arange(-1, 2, dtype=jnp.int32)
    q_has = jnp.any(q_seg.reshape(n_q, Q_BLOCK, 1) == values, axis=1).astype(jnp.float32)
    k_has = jnp.any(k_seg.reshape(n_k, K_BLOCK, 1) == values, axis=1).astype(jnp.float32)
    shared = jnp.dot(q_has, k_has.T) > 0
    single = (jnp.sum(q_has, axis=1)[:, None] == 1) & (jnp.sum(k_has, axis=1)[None, :] == 1)
    diag = (q_start + jnp.arange(n_q, dtype=jnp.int32) * Q_BLOCK) // K_BLOCK
    order = (diag[:, None] + jnp.arange(n_k, dtype=jnp.int32)[None, :]) % n_k
    need = jnp.take_along_axis(shared, order, axis=1)
    full = jnp.take_along_axis(single, order, axis=1)
    rank = jnp.cumsum(need.astype(jnp.int32), axis=1) - 1
    count = jnp.sum(need.astype(jnp.int32), axis=1)
    pos = jnp.where(need, rank, n_k + jnp.arange(n_k)[None, :])
    perm = jnp.argsort(pos, axis=1)
    kb_sorted = jnp.take_along_axis(order, perm, axis=1)
    full_sorted = jnp.take_along_axis(full, perm, axis=1)
    step = jnp.arange(n_k, dtype=jnp.int32)[None, :]
    live = step < count[:, None]
    last = jnp.take_along_axis(kb_sorted, (count - 1)[:, None], axis=1)
    kb_map = jnp.where(live, kb_sorted, last).astype(jnp.int32)
    flags = jnp.where(live, jnp.where(full_sorted, 2, 1), 0).astype(jnp.int32)
    return kb_map, flags


def attention(q_t, q_seg_f, kv, kb_map, flags, scale, interpret=False):
    n_tok = q_t.shape[0]
    n_keys = kv.shape[2]
    n_q = n_tok // Q_BLOCK
    n_k = n_keys // K_BLOCK
    kernel = functools.partial(_attn_kernel, scale=scale, n_steps=n_k)
    grid_spec = pltpu.PrefetchScalarGridSpec(
        num_scalar_prefetch=2,
        grid=(n_q, n_k),
        in_specs=[
            pl.BlockSpec((Q_BLOCK, PADW), lambda i, j, km, fl: (i, 0)),
            pl.BlockSpec((Q_BLOCK, 1), lambda i, j, km, fl: (i, 0)),
            pl.BlockSpec((None, PADW, K_BLOCK), lambda i, j, km, fl: (0, 0, km[i, j])),
            pl.BlockSpec((None, PADW, K_BLOCK), lambda i, j, km, fl: (1, 0, km[i, j])),
        ],
        out_specs=pl.BlockSpec((Q_BLOCK, PADW), lambda i, j, km, fl: (i, 0)),
        scratch_shapes=[
            pltpu.VMEM((Q_BLOCK, 1), jnp.float32),
            pltpu.VMEM((Q_BLOCK, 1), jnp.float32),
            pltpu.VMEM((Q_BLOCK, PADW), jnp.float32),
        ],
    )
    return pl.pallas_call(
        kernel,
        grid_spec=grid_spec,
        out_shape=jax.ShapeDtypeStruct((n_tok, PADW), jnp.bfloat16),
        compiler_params=pltpu.CompilerParams(dimension_semantics=("arbitrary", "arbitrary")),
        interpret=interpret,
    )(kb_map, flags, q_t, q_seg_f, kv, kv)


def on_device(
    hidden,
    gain_in,
    w_query,
    w_pair,
    kv_cache,
    recompute_rows,
    segment_ids,
    w_out,
    gain_merge,
    w_merge,
    requests,
):
    local_width, tok_rows = hidden.shape
    model_width = w_query.shape[1]
    n_col = model_width // local_width
    heads_here = local_width // HD
    score_scale = HD ** (-0.5)
    col_index = lax.axis_index("col")
    full_rows = lax.all_gather(hidden, "col", axis=0, tiled=True)
    out_weight = lax.all_gather(w_out, "col", axis=0, tiled=True)
    full_float = full_rows.astype(jnp.float32)
    in_mean = jnp.sum(full_float, axis=0, keepdims=True) / model_width
    in_square = jnp.sum(full_float * full_float, axis=0, keepdims=True) / model_width
    normed = (
        (full_float - in_mean)
        * lax.rsqrt(in_square - in_mean * in_mean + EPSILON)
        * gain_in.astype(jnp.float32)[:, None]
    ).astype(jnp.bfloat16)
    query_rows = lax.dot_general(
        normed, w_query, (((0,), (1,)), ((), ())), preferred_element_type=jnp.float32
    ).astype(jnp.bfloat16)
    query_rows = jnp.pad(query_rows, ((0, 0), (0, PADW - HD)))
    picked_rows = recompute_rows[0]
    normed_picked = jnp.take(normed, picked_rows, axis=1)
    fresh_pairs = jnp.dot(
        w_pair.reshape(2 * local_width, model_width),
        normed_picked,
        preferred_element_type=jnp.float32,
    )
    fresh_pairs = fresh_pairs.astype(jnp.bfloat16).reshape(2, local_width, -1)
    keys_values = kv_cache.at[:, :, picked_rows].set(fresh_pairs)

    pair_local = jnp.pad(keys_values, ((0, 0), (0, PADW - HD), (0, 0)))
    pair_local = pair_local.at[0, HD].set(segment_ids.astype(jnp.bfloat16))
    pair_all = lax.all_gather(pair_local, "row", axis=2, tiled=True)
    segment_line = pair_all[0, HD].astype(jnp.int32)
    kb_map, flags = block_tables(segment_ids, segment_line, lax.axis_index("row") * tok_rows)
    attended_rows = attention(
        query_rows, segment_ids.astype(jnp.float32)[:, None], pair_all, kb_map, flags, score_scale
    )
    attended = attended_rows[:, :HD].T
    chunk = tok_rows // n_col
    attended_chunk = lax.all_to_all(attended, "col", 1, 0, tiled=True)
    x_chunk = lax.dynamic_slice_in_dim(full_float, col_index * chunk, chunk, 1)
    projected = lax.dot_general(
        out_weight, attended_chunk, (((0,), (0,)), ((), ())), preferred_element_type=jnp.float32
    )
    updated = x_chunk + projected
    row_mean = jnp.sum(updated, axis=0, keepdims=True) / model_width
    row_square = jnp.sum(updated * updated, axis=0, keepdims=True) / model_width
    merger_chunk = (
        (updated - row_mean)
        * lax.rsqrt(row_square - row_mean * row_mean + EPSILON)
        * gain_merge.astype(jnp.float32)[:, None]
    ).astype(jnp.bfloat16)
    merge_weight, _ = lax.optimization_barrier((w_merge, pair_all))
    merge_full = lax.all_gather(merge_weight, "col", axis=1, tiled=True)
    grouped = merger_chunk.reshape(model_width, chunk // 4, 4)
    merged_here = jnp.einsum("fgi,ifd->gd", grouped, merge_full, preferred_element_type=jnp.float32)
    merged_all = lax.all_gather(merged_here.astype(jnp.bfloat16), "col", axis=0, tiled=True)
    wanted_rows = lax.dynamic_index_in_dim(requests[0], col_index, 0, keepdims=False)
    is_valid = wanted_rows >= 0
    safe_index = jnp.where(is_valid, wanted_rows, 0)
    picked = jnp.where(is_valid[:, None], merged_all[safe_index], jnp.zeros((), jnp.bfloat16))
    return picked.reshape(1, 1, picked.shape[0], model_width)


def solution(mesh):
    placed = (
        P("col", "row"),
        P(),
        P("col", None),
        P(None, "col", None),
        P(None, "col", "row"),
        P("row", None),
        P("row"),
        P("col", None),
        P(),
        P(None, "col", None),
        P("row", None, None),
    )
    return jax.shard_map(
        on_device,
        mesh=mesh,
        in_specs=placed,
        out_specs=P("row", "col", None, None),
        check_vma=False,
    )
```

time: 486 us -> 372 us (0.77)
  matrix products: 194 us -> 17.3 us
  Pallas kernels: 0 us -> 90.1 us
  other arithmetic: 99.2 us -> 28.9 us
  waiting for transfers between devices: 133 us -> 173 us
  local copies, waits for them, and re-layouts: 33 us -> 38.5 us
    dot_general x33 -> x2, matrix products: 182 us -> 4.84 us  [the longest x1 4.65 us: on_device(): lax.dot_general(normed, w_query, (((0,), (1,)), ((), ())), preferred_elem...]
    pallas_call x0 -> x1, Pallas kernels: none -> 90.1 us  [attention(): pl.pallas_call(kernel, grid_spec=grid_spec, out_shape=jax.ShapeDtypeStruc...]
    reduce_sum x16 -> x3, other arithmetic: 74.9 us -> 0.24 us  [the longest x1 0.2 us: block_tables(): count = jnp.sum(need.astype(jnp.int32), axis=1)]
    all_gather x1, waiting for transfers between devices: 0.02 us -> 34.4 us  [on_device(): merge_full = lax.all_gather(merge_weight, 'col', axis=1, tiled=True)]
    all_gather x1, waiting for transfers between devices: 34.1 us -> 39.9 us  [on_device(): pair_all = lax.all_gather(pair_local, 'row', axis=2, tiled=True)]
    slice x1 -> x0, local copies, waits for them, and re-layouts: 5.75 us -> none  [on_device(): pair_rows = pair_all[:2 * local_width].reshape(2, local_width, -1)]
  transfers between devices with their start and end apart: 6 -> 6, of which waited for: 3 -> 5; matrix products, arithmetic and copies ran while one was open for 59% -> 10% of each run, Pallas kernels for 0% -> 24%
where the time goes in v3:
time: 372 us; the launch traced here: 368 us
  waiting for transfers between devices  173 us (47%)
  Pallas kernels  90.1 us (24%)
  local copies, waits for them, and re-layouts  38.5 us (10%)
  other arithmetic  28.9 us (8%)
  matrix products  17.3 us (5%)
  between operations  13.4 us (4%)
  starting transfers between devices  7.57 us (2%)
    pallas_call x1, Pallas kernels, attention(): pl.pallas_call(kernel, grid_spec=grid_spec, out_shape=jax.ShapeDtypeStruc...  90.1 us
    all_gather x1, waiting for transfers between devices, on_device(): full_rows = lax.all_gather(hidden, 'col', axis=0, tiled=True)  53.9 us
    all_gather x1, waiting for transfers between devices, on_device(): lax.all_gather(merged_here.astype(jnp.bfloat16), 'col', axis=0, tiled=True)  41.8 us
    all_gather x1, waiting for transfers between devices, on_device(): pair_all = lax.all_gather(pair_local, 'row', axis=2, tiled=True)  39.9 us
    all_gather x1, waiting for transfers between devices, on_device(): merge_full = lax.all_gather(merge_weight, 'col', axis=1, tiled=True)  34.4 us
    dot_general x1, matrix products, on_device(): jnp.einsum('fgi,ifd->gd', grouped, merge_full, preferred_element_type=jnp...  8.77 us
    all_gather x1, local copies, waits for them, and re-layouts, on_device(): full_rows = lax.all_gather(hidden, 'col', axis=0, tiled=True)  8.37 us
    scatter x2, local copies, waits for them, and re-layouts, on_device(): keys_values = kv_cache.at[:, :, picked_rows].set(fresh_pairs)  7.64 us
  transfers between devices with their start and end apart: 6, of which 5 were waited for; matrix products, arithmetic and copies ran while one was open for 10% of the time, Pallas kernels for 24%

profile of v3, /device:TPU:78, one launch (start us, length us, event | category | flops | bytes accessed | tf_op | source)
XLA Modules:
  0.0 368.5 jit_solution(1414576717289153619)
XLA Ops:
  6.5 0.7 all-gather.6.cloned.1.call-update
  7.3 0.7 convert_element_type.58
  8.0 2.4 copy.66
  10.4 0.7 compare_select_fusion
  11.1 0.7 fusion.14
  11.8 1.4 and_reduce_fusion
  13.1 0.7 compare_and_fusion.2
  13.8 0.8 fusion.13
  14.6 53.9 %all-gather.6.cloned.1.call-done = bf16[1408,2048]{1,0:T(8,128)(2,1)} async-done(((bf16[88,2048]{1,0:T(8,128)(2,1)}), bf16[1408,2048]{1,0:T(8,128)(2,1)}) %all-gather.6.cloned.1.call-update) | async-done | bytes 5767184 | tf_op jit(solution)/shard_map/all_gather | solution.py:138
  68.5 8.4 %copy.64 = bf16[1408,2048]{0,1:T(8,128)(2,1)} copy(bf16[1408,2048]{1,0:T(8,128)(2,1)} %all-gather.6.cloned.1.call-done) | data formatting | bytes 11534336 | tf_op jit(solution)/shard_map/all_gather | solution.py:138
  76.9 4.5 %convert_reduce_fusion = (f32[2048]{0:T(1024)S(1)}, f32[2048]{0:T(1024)S(1)}) fusion(bf16[1408,2048]{0,1:T(8,128)(2,1)} %copy.64), kind=kLoop, calls=%fused_computation.10 | loop fusion | flops 11530240 | bytes 5783552 | tf_op jit(solution)/shard_map/reduce_sum | solution.py:141
  81.4 4.0 %multiply_convert_fusion = bf16[1408,2048]{0,1:T(8,128)(2,1)} fusion(bf16[1408,2048]{0,1:T(8,128)(2,1)S(1)} %copy-done.2, f32[1408]{0:T(1024)S(1)} %convert_element_type.58, f32[2048]{0:T(1024)S(1)} %get-tuple-element.29, f32[2048]{0:T(1024)S(1)} %get-tuple-element.28), kind=kLoop, calls=%fused_computation.8 | loop fusion | flops 14417920 | bytes 11556352 | tf_op jit(solution)/shard_map/convert_element_type | solution.py:147
  85.4 5.0 %gather_fusion = bf16[200,1408]{1,0:T(8,128)(2,1)S(1)} fusion(bf16[1408,2048]{0,1:T(8,128)(2,1)} %multiply_convert_fusion, s32[1024]{0:T(1024)S(1)} %pad_clamp_fusion.1), kind=kCustom, calls=%fused_computation.3 | custom fusion | bytes 1127200 | tf_op jit(solution)/shard_map/jit(_take)/gather | solution.py:153
  90.4 0.4 convolution_convert_fusion.1
  91.0 6.9 %scatter_fusion = bf16[2,88,2048]{1,0,2:T(2,128)(2,1)S(1)} fusion(bf16[2,88,2048]{1,0,2:T(2,128)(2,1)S(1)} %copy.66, s32[200]{0:T(256)S(1)} %bitcast.70, bf16[200,2,88]{2,1,0:T(2,128)(2,1)S(1)} %bitcast.66), kind=kCustom, calls=%fused_computation.7 | custom fusion | bytes 212000 | tf_op jit(solution)/shard_map/scatter | solution.py:160
  97.8 0.8 copy.67
  98.7 1.9 broadcast_select_fusion
  100.6 1.4 scatter.13
  102.0 0.9 copy-done.3
  103.0 0.7 all-gather.10.cloned.1.call-update
  103.9 39.9 %all-gather.8.cloned.1.call-done.k_ref.v_ref = bf16[2,96,16384]{2,1,0:T(8,128)(2,1)} async-done(((bf16[2,96,2048]{2,1,0:T(8,128)(2,1)}), bf16[2,96,16384]{2,1,0:T(8,128)(2,1)}) %all-gather.8.cloned.1.call-update) | async-done | bytes 6291472 | tf_op jit(solution)/shard_map/all_gather | solution.py:164
  144.1 1.3 copy.77.qs_ref
  145.7 4.6 %convolution_convert_fusion = bf16[2048,88]{0,1:T(8,128)(2,1)S(1)} fusion(bf16[1408,2048]{0,1:T(8,128)(2,1)} %multiply_convert_fusion, bf16[88,1408]{1,0:T(8,128)(2,1)S(1)} %copy-done.4), kind=kOutput, calls=%fused_computation.13 | convolution fusion | flops 507691008 | bytes 6375424 | tf_op jit(solution)/shard_map/dot_general | solution.py:148
  150.3 0.3 copy.76
  150.6 0.9 pad.12.q_ref
  151.5 1.1 fusion.6
  152.7 0.2 compare_reduce_fusion
  153.1 0.9 gather_fusion.4
  154.2 0.9 gather_fusion.5
  155.7 0.7 sort.17
  156.6 0.9 gather_fusion.2
  157.6 0.9 gather_fusion.6
  158.5 0.6 select_select_fusion
  159.2 0.6 gather_fusion.3
  159.8 0.6 fusion.8.kb_map
  160.5 90.1 %shard_map.109 = bf16[2048,96]{1,0:T(8,128)(2,1)} custom-call(s32[4,16]{1,0:T(4,128)} %fusion.8.kb_map, s32[4,16]{1,0:T(4,128)} %get-tuple-element.30.flags, bf16[2048,96]{1,0:T(8,128)(2,1)} %pad.12.q_ref, f32[2048,1]{1,0:T(8,128)} %copy.77.qs_ref, bf16[2,96,16384]{2,1,0:T(8,128)(2,1)} %all-gather.8.cloned.1.call-done.k_ref.v_ref, ...), custom_call_target="tpu_custom_call" | custom-call | tf_op jit(solution)/shard_map/pallas_call | solution.py:110
  250.5 2.0 copy.78
  252.5 7.2 %all-to-all-start = ((bf16[88,16,128]{2,0,1:T(8,128)(2,1)}), bf16[88,16,128]{2,0,1:T(8,128)(2,1)S(1)}, u32[]{:S(2)}, u32[]{:S(2)}) async-start(bf16[88,16,128]{2,0,1:T(8,128)(2,1)} %copy.78), calls=%async_computation | async-start | bytes 720896 | tf_op jit(solution)/shard_map/all_to_all | solution.py:172
  259.8 7.6 %convert_element_type.57 = f32[1408,2048]{0,1:T(8,128)} convert(bf16[1408,2048]{0,1:T(8,128)(2,1)} %copy.64) | non-fusion elementwise | flops 2883584 | bytes 17301504 | tf_op jit(solution)/shard_map/convert_element_type | solution.py:140
  267.4 1.3 all-to-all-done
  268.7 3.3 fusion.12
  272.3 34.4 %all-gather.12.cloned.1.call-done = bf16[4,1408,1408]{2,1,0:T(8,128)(2,1)} async-done(((bf16[4,88,1408]{2,1,0:T(8,128)(2,1)}), bf16[4,1408,1408]{2,1,0:T(8,128)(2,1)}) %all-gather.12.cloned.1.call-update) | async-done | bytes 15859728 | tf_op jit(solution)/shard_map/all_gather | solution.py:186
  306.7 8.8 %fusion.1 = bf16[32,1408]{1,0:T(8,128)(2,1)} fusion(bf16[4,1408,1408]{2,1,0:T(8,128)(2,1)} %all-gather.12.cloned.1.call-done, bf16[1408,32,4]{0,2,1:T(4,128)(2,1)S(1)} %reshape.303), kind=kOutput, calls=%fused_computation.15 | convolution fusion | flops 507555840 | bytes 16310272 | tf_op jit(solution)/shard_map/fgi,ifd->gd/dot_general | solution.py:188
  315.5 0.7 fusion.9
  316.2 0.7 compare_bitcast_fusion
  316.9 41.8 %all-gather.14.cloned.1.call-done = bf16[512,1408]{1,0:T(8,128)(2,1)} async-done(((bf16[32,1408]{1,0:T(8,128)(2,1)}), bf16[512,1408]{1,0:T(8,128)(2,1)}) %all-gather.14.cloned.1.call-update) | async-done | bytes 1441808 | tf_op jit(solution)/shard_map/all_gather | solution.py:189
  358.6 2.5 gather_fusion.1
  361.2 0.8 bitcast_select_fusion
  (63 shorter events, 2.8 us)
Async XLA Ops:
  6.5 83.9 %copy-start = (bf16[2,88,1408]{2,1,0:T(8,128)(2,1)S(1)}, bf16[2,88,1408]{2,1,0:T(8,128)(2,1)}, u32[]{:S(2)}) copy-start(bf16[2,88,1408]{2,1,0:T(8,128)(2,1)} %param.18) | copy-start | bytes 1486852
  6.5 62.0 %all-gather.6.cloned.1.call-start = ((), (), s32[]{:S(2)}) async-start(), calls=%async_computation.1 | async-start | bytes 6127616 | tf_op jit(solution)/shard_map/all_gather | solution.py:138
  7.3 136.6 %all-gather.8.cloned.1.call-start = ((), (), s32[]{:S(2)}) async-start(), calls=%async_computation.2 | async-start | bytes 7077888 | tf_op jit(solution)/shard_map/all_gather | solution.py:164
  76.9 4.5 %copy-start.2 = (bf16[1408,2048]{0,1:T(8,128)(2,1)S(1)}, bf16[1408,2048]{0,1:T(8,128)(2,1)}, u32[]{:S(2)}) copy-start(bf16[1408,2048]{0,1:T(8,128)(2,1)} %copy.64) | copy-start | bytes 17301508
  85.4 58.5 %copy-start.5 = (s32[2048]{0:T(1024)S(1)}, s32[2048]{0:T(1024)}, u32[]{:S(2)}) copy-start(s32[2048]{0:T(1024)} %param.21) | copy-start | bytes 24580
  85.4 60.3 %copy-start.4 = (bf16[88,1408]{1,0:T(8,128)(2,1)S(1)}, bf16[88,1408]{1,0:T(8,128)(2,1)}, u32[]{:S(2)}) copy-start(bf16[88,1408]{1,0:T(8,128)(2,1)} %param.17) | copy-start | bytes 743428
  102.0 0.9 copy-start.3
  102.9 164.5 %all-gather.10.cloned.1.call-start = ((), (), s32[]{:S(2)}) async-start(), calls=%async_computation.3 | async-start | bytes 4212736 | tf_op jit(solution)/shard_map/all_gather | solution.py:139
  103.7 203.0 %all-gather.12.cloned.1.call-start = ((), (), s32[]{:S(2)}) async-start(), calls=%async_computation.4 | async-start | bytes 16850944 | tf_op jit(solution)/shard_map/all_gather | solution.py:186
  160.5 99.4 %copy-start.6 = (bf16[1408]{0:T(1024)(128)(2,1)S(1)}, bf16[1408]{0:T(1024)(128)(2,1)}, u32[]{:S(2)}) copy-start(bf16[1408]{0:T(1024)(128)(2,1)} %param.23) | copy-start | bytes 8452
  252.5 16.2 %all-to-all-start = ((bf16[88,16,128]{2,0,1:T(8,128)(2,1)}), bf16[88,16,128]{2,0,1:T(8,128)(2,1)S(1)}, u32[]{:S(2)}, u32[]{:S(2)}) async-start(bf16[88,16,128]{2,0,1:T(8,128)(2,1)} %copy.78), calls=%async_computation | async-start | bytes 720896 | tf_op jit(solution)/shard_map/all_to_all | solution.py:172
  259.8 98.9 %all-gather.14.cloned.1.call-start = ((), (), s32[]{:S(2)}) async-start(), calls=%async_computation.5 | async-start | bytes 1531904 | tf_op jit(solution)/shard_map/all_gather | solution.py:189
  272.2 89.7 %copy-start.1 = (bf16[2,88,1408]{2,1,0:T(8,128)(2,1)S(1)}, bf16[2,88,1408]{2,1,0:T(8,128)(2,1)}, u32[]{:S(2)}) copy-start(bf16[2,88,1408]{2,1,0:T(8,128)(2,1)} %param.18) | copy-start | bytes 1486852
Sparse Core Ops, SparseCore 0:
  9.5 58.9 all-gather.5
  103.0 40.7 all-gather.7
  146.0 50.4 all-gather.9
  198.5 108.1 all-gather.11
  315.6 42.9 all-gather.13

commit v4 on v3

--- a/solution.py
+++ b/solution.py
@@ -150,7 +150,17 @@
     ).astype(jnp.bfloat16)
     query_rows = jnp.pad(query_rows, ((0, 0), (0, PADW - HD)))
     picked_rows = recompute_rows[0]
-    normed_picked = jnp.take(normed, picked_rows, axis=1)
+    hidden_picked = jnp.take(hidden, picked_rows, axis=1)
+    picked_copies = jnp.broadcast_to(hidden_picked[None], (n_col,) + hidden_picked.shape)
+    picked_full = lax.all_to_all(picked_copies, "col", 0, 0, tiled=True)
+    picked_float = picked_full.reshape(model_width, -1).astype(jnp.float32)
+    picked_mean = jnp.sum(picked_float, axis=0, keepdims=True) / model_width
+    picked_square = jnp.sum(picked_float * picked_float, axis=0, keepdims=True) / model_width
+    normed_picked = (
+        (picked_float - picked_mean)
+        * lax.rsqrt(picked_square - picked_mean * picked_mean + EPSILON)
+        * gain_in.astype(jnp.float32)[:, None]
+    ).astype(jnp.bfloat16)
     fresh_pairs = jnp.dot(
         w_pair.reshape(2 * local_width, model_width),
         normed_picked,
@@ -161,6 +171,7 @@
 
     pair_local = jnp.pad(keys_values, ((0, 0), (0, PADW - HD), (0, 0)))
     pair_local = pair_local.at[0, HD].set(segment_ids.astype(jnp.bfloat16))
+    pair_local, _ = lax.optimization_barrier((pair_local, full_rows))
     pair_all = lax.all_gather(pair_local, "row", axis=2, tiled=True)
     segment_line = pair_all[0, HD].astype(jnp.int32)
     kb_map, flags = block_tables(segment_ids, segment_line, lax.axis_index("row") * tok_rows)

time: 372 us -> 349 us (0.938)
  waiting for transfers between devices: 173 us -> 151 us
  starting transfers between devices: 7.57 us -> 14.9 us
  other arithmetic: 28.9 us -> 23.6 us
    all_gather x1, waiting for transfers between devices: 53.9 us -> 29 us  [on_device(): full_rows = lax.all_gather(hidden, 'col', axis=0, tiled=True)]
    all_to_all x0 -> x1, waiting for transfers between devices: none -> 8.34 us  [on_device(): picked_full = lax.all_to_all(picked_copies, 'col', 0, 0, tiled=True)]
    all_to_all x0 -> x1, starting transfers between devices: none -> 7.31 us  [on_device(): picked_full = lax.all_to_all(picked_copies, 'col', 0, 0, tiled=True)]
    all_gather x1, waiting for transfers between devices: 34.4 us -> 28.5 us  [on_device(): merge_full = lax.all_gather(merge_weight, 'col', axis=1, tiled=True)]
    gather x1, local copies, waits for them, and re-layouts: 5.01 us -> 0.8 us  [on_device(): hidden_picked = jnp.take(hidden, picked_rows, axis=1)]
    convert_element_type x1, other arithmetic: 3.99 us -> 0.27 us  [on_device(): normed_picked = ((picked_float - picked_mean) * lax.rsqrt(picked_square -...]
  transfers between devices with their start and end apart: 6 -> 7, of which waited for: 5 -> 6; matrix products, arithmetic and copies ran while one was open for 10% -> 18% of each run, Pallas kernels for 24% -> 26%
where the time goes in v4:
time: 349 us; the launch traced here: 345 us
  waiting for transfers between devices  151 us (43%)
  Pallas kernels  90.1 us (26%)
  local copies, waits for them, and re-layouts  36.5 us (10%)
  other arithmetic  23.6 us (7%)
  matrix products  15.4 us (4%)
  starting transfers between devices  14.9 us (4%)
  between operations  13.4 us (4%)
    pallas_call x1, Pallas kernels, attention(): pl.pallas_call(kernel, grid_spec=grid_spec, out_shape=jax.ShapeDtypeStruc...  90.1 us
    all_gather x1, waiting for transfers between devices, on_device(): pair_all = lax.all_gather(pair_local, 'row', axis=2, tiled=True)  41.7 us
    all_gather x1, waiting for transfers between devices, on_device(): lax.all_gather(merged_here.astype(jnp.bfloat16), 'col', axis=0, tiled=True)  41.4 us
    all_gather x1, waiting for transfers between devices, on_device(): full_rows = lax.all_gather(hidden, 'col', axis=0, tiled=True)  29 us
    all_gather x1, waiting for transfers between devices, on_device(): merge_full = lax.all_gather(merge_weight, 'col', axis=1, tiled=True)  28.5 us
    dot_general x1, matrix products, on_device(): jnp.einsum('fgi,ifd->gd', grouped, merge_full, preferred_element_type=jnp...  8.77 us
    all_gather x1, local copies, waits for them, and re-layouts, on_device(): full_rows = lax.all_gather(hidden, 'col', axis=0, tiled=True)  8.41 us
    all_to_all x1, waiting for transfers between devices, on_device(): picked_full = lax.all_to_all(picked_copies, 'col', 0, 0, tiled=True)  8.34 us
  transfers between devices with their start and end apart: 7, of which 6 were waited for; matrix products, arithmetic and copies ran while one was open for 18% of the time, Pallas kernels for 26%

profile of v4, /device:TPU:78, one launch (start us, length us, event | category | flops | bytes accessed | tf_op | source)
XLA Modules:
  0.0 345.2 jit_solution(332980604293940255)
XLA Ops:
  6.5 0.7 all-gather.6.cloned.1.call-update
  7.3 1.3 copy.73
  8.5 0.7 compare_select_fusion
  9.2 0.8 gather_fusion
  10.0 0.7 compare_and_fusion.2
  10.9 0.9 broadcast_in_dim.58
  11.8 7.3 %all-to-all-start = ((bf16[16,88,200]{2,1,0:T(8,128)(2,1)}), bf16[16,88,200]{2,1,0:T(8,128)(2,1)S(1)}, u32[]{:S(2)}, u32[]{:S(2)}) async-start(bf16[16,88,200]{2,1,0:T(8,128)(2,1)} %broadcast_in_dim.58), calls=%async_computation | async-start | bytes 1441792 | tf_op jit(solution)/shard_map/all_to_all | solution.py:155
  19.2 0.8 mul.104
  20.0 2.4 copy.76
  22.4 0.6 fusion.16
  23.0 0.7 and_reduce_fusion
  23.7 8.3 %all-to-all-done = bf16[16,88,200]{2,1,0:T(8,128)(2,1)S(1)} async-done(((bf16[16,88,200]{2,1,0:T(8,128)(2,1)}), bf16[16,88,200]{2,1,0:T(8,128)(2,1)S(1)}, u32[]{:S(2)}, u32[]{:S(2)}) %all-to-all-start) | async-done | bytes 563232 | tf_op jit(solution)/shard_map/all_to_all | solution.py:155
  32.6 0.3 convolution_convert_fusion
  33.1 6.9 %scatter_fusion = bf16[2,88,2048]{1,0,2:T(2,128)(2,1)S(1)} fusion(bf16[2,88,2048]{1,0,2:T(2,128)(2,1)S(1)} %copy.76, s32[200]{0:T(256)S(1)} %bitcast.74, bf16[200,2,88]{2,1,0:T(2,128)(2,1)S(1)} %bitcast.70), kind=kCustom, calls=%fused_computation.7 | custom fusion | bytes 212000 | tf_op jit(solution)/shard_map/scatter | solution.py:170
  39.9 0.8 copy.77
  40.8 1.9 broadcast_select_fusion
  42.7 1.4 scatter.13
  44.1 29.0 %all-gather.6.cloned.1.call-done = bf16[1408,2048]{1,0:T(8,128)(2,1)} async-done(((bf16[88,2048]{1,0:T(8,128)(2,1)}), bf16[1408,2048]{1,0:T(8,128)(2,1)}) %all-gather.6.cloned.1.call-update) | async-done | bytes 5767184 | tf_op jit(solution)/shard_map/all_gather | solution.py:138
  73.2 0.7 all-gather.10.cloned.1.call-update
  73.9 41.7 %all-gather.8.cloned.1.call-done.k_ref.v_ref = bf16[2,96,16384]{2,1,0:T(8,128)(2,1)} async-done(((bf16[2,96,2048]{2,1,0:T(8,128)(2,1)}), bf16[2,96,16384]{2,1,0:T(8,128)(2,1)}) %all-gather.8.cloned.1.call-update) | async-done | bytes 6291472 | tf_op jit(solution)/shard_map/all_gather | solution.py:175
  115.9 1.3 copy.87.qs_ref
  117.5 8.4 %copy.72 = bf16[1408,2048]{0,1:T(8,128)(2,1)} copy(bf16[1408,2048]{1,0:T(8,128)(2,1)} %all-gather.6.cloned.1.call-done) | data formatting | bytes 11534336 | tf_op jit(solution)/shard_map/all_gather | solution.py:138
  125.9 4.5 %convert_reduce_fusion = (f32[2048]{0:T(1024)S(1)}, f32[2048]{0:T(1024)S(1)}) fusion(bf16[1408,2048]{0,1:T(8,128)(2,1)} %copy.72), kind=kLoop, calls=%fused_computation.10 | loop fusion | flops 11530240 | bytes 5783552 | tf_op jit(solution)/shard_map/reduce_sum | solution.py:141
  130.5 2.8 fusion.2
  133.3 0.3 copy.86
  133.5 0.9 pad.12.q_ref
  134.4 1.1 fusion.9
  136.0 0.9 gather_fusion.4
  137.1 0.9 gather_fusion.5
  138.6 0.7 sort.17
  139.5 0.9 gather_fusion.2
  140.5 0.9 gather_fusion.6
  141.5 0.6 select_select_fusion
  142.1 0.6 gather_fusion.3
  142.8 0.7 fusion.11.kb_map
  143.4 90.1 %shard_map.109 = bf16[2048,96]{1,0:T(8,128)(2,1)} custom-call(s32[4,16]{1,0:T(4,128)} %fusion.11.kb_map, s32[4,16]{1,0:T(4,128)} %get-tuple-element.34.flags, bf16[2048,96]{1,0:T(8,128)(2,1)} %pad.12.q_ref, f32[2048,1]{1,0:T(8,128)} %copy.87.qs_ref, bf16[2,96,16384]{2,1,0:T(8,128)(2,1)} %all-gather.8.cloned.1.call-done.k_ref.v_ref, ...), custom_call_target="tpu_custom_call" | custom-call | tf_op jit(solution)/shard_map/pallas_call | solution.py:110
  233.5 2.0 copy.88
  235.5 7.2 %all-to-all-start.1 = ((bf16[88,16,128]{2,0,1:T(8,128)(2,1)}), bf16[88,16,128]{2,0,1:T(8,128)(2,1)S(1)}, u32[]{:S(2)}, u32[]{:S(2)}) async-start(bf16[88,16,128]{2,0,1:T(8,128)(2,1)} %copy.88), calls=%async_computation.1 | async-start | bytes 720896 | tf_op jit(solution)/shard_map/all_to_all | solution.py:183
  243.0 7.7 %convert_element_type.70 = f32[1408,2048]{0,1:T(8,128)} convert(bf16[1408,2048]{0,1:T(8,128)(2,1)} %copy.72) | non-fusion elementwise | flops 2883584 | bytes 17301504 | tf_op jit(solution)/shard_map/convert_element_type | solution.py:140
  250.7 1.0 all-to-all-done.1
  251.7 3.4 fusion.14
  255.3 28.5 %all-gather.12.cloned.1.call-done = bf16[4,1408,1408]{2,1,0:T(8,128)(2,1)} async-done(((bf16[4,88,1408]{2,1,0:T(8,128)(2,1)}), bf16[4,1408,1408]{2,1,0:T(8,128)(2,1)}) %all-gather.12.cloned.1.call-update) | async-done | bytes 15859728 | tf_op jit(solution)/shard_map/all_gather | solution.py:197
  283.8 8.8 %fusion.3 = bf16[32,1408]{1,0:T(8,128)(2,1)} fusion(bf16[4,1408,1408]{2,1,0:T(8,128)(2,1)} %all-gather.12.cloned.1.call-done, bf16[1408,32,4]{0,2,1:T(4,128)(2,1)S(1)} %reshape.354), kind=kOutput, calls=%fused_computation.16 | convolution fusion | flops 507555840 | bytes 16310272 | tf_op jit(solution)/shard_map/fgi,ifd->gd/dot_general | solution.py:199
  292.6 0.7 fusion.12
  293.3 0.7 compare_bitcast_fusion
  294.0 41.4 %all-gather.14.cloned.1.call-done = bf16[512,1408]{1,0:T(8,128)(2,1)} async-done(((bf16[32,1408]{1,0:T(8,128)(2,1)}), bf16[512,1408]{1,0:T(8,128)(2,1)}) %all-gather.14.cloned.1.call-update) | async-done | bytes 1441808 | tf_op jit(solution)/shard_map/all_gather | solution.py:200
  335.4 2.5 gather_fusion.1
  337.9 0.8 bitcast_select_fusion
  (74 shorter events, 3.8 us)
Async XLA Ops:
  6.5 26.1 %copy-start = (bf16[2,88,1408]{2,1,0:T(8,128)(2,1)S(1)}, bf16[2,88,1408]{2,1,0:T(8,128)(2,1)}, u32[]{:S(2)}) copy-start(bf16[2,88,1408]{2,1,0:T(8,128)(2,1)} %param.18) | copy-start | bytes 1486852
  6.5 16.5 %copy-start.6 = (s32[3]{0:T(128)S(1)}, s32[3]{0:T(128)}, u32[]{:S(2)}) copy-start(s32[3]{0:T(128)} %constant.158.clone.1) | copy-start | bytes 40
  6.5 17.2 %copy-start.3 = (s32[2048]{0:T(1024)S(1)}, s32[2048]{0:T(1024)}, u32[]{:S(2)}) copy-start(s32[2048]{0:T(1024)} %param.21) | copy-start | bytes 24580
  6.5 66.6 %all-gather.6.cloned.1.call-start = ((), (), s32[]{:S(2)}) async-start(), calls=%async_computation.2 | async-start | bytes 6127616 | tf_op jit(solution)/shard_map/all_gather | solution.py:138
  11.8 20.3 %all-to-all-start = ((bf16[16,88,200]{2,1,0:T(8,128)(2,1)}), bf16[16,88,200]{2,1,0:T(8,128)(2,1)S(1)}, u32[]{:S(2)}, u32[]{:S(2)}) async-start(bf16[16,88,200]{2,1,0:T(8,128)(2,1)} %broadcast_in_dim.58), calls=%async_computation | async-start | bytes 1441792 | tf_op jit(solution)/shard_map/all_to_all | solution.py:155
  19.1 96.5 %all-gather.8.cloned.1.call-start = ((), (), s32[]{:S(2)}) async-start(), calls=%async_computation.3 | async-start | bytes 7077888 | tf_op jit(solution)/shard_map/all_gather | solution.py:175
  19.9 95.7 %copy-start.4 = (bf16[1408]{0:T(1024)(128)(2,1)S(1)}, bf16[1408]{0:T(1024)(128)(2,1)}, u32[]{:S(2)}) copy-start(bf16[1408]{0:T(1024)(128)(2,1)} %param.16) | copy-start | bytes 8452
  44.1 29.0 %copy-start.2 = (bf16[2,96,2048]{2,1,0:T(8,128)(2,1)}, bf16[2,96,2048]{2,1,0:T(8,128)(2,1)S(1)}, u32[]{:S(2)}) copy-start(bf16[2,96,2048]{2,1,0:T(8,128)(2,1)S(1)} %scatter.13) | copy-start | bytes 2359300
  73.2 177.5 %all-gather.10.cloned.1.call-start = ((), (), s32[]{:S(2)}) async-start(), calls=%async_computation.4 | async-start | bytes 4212736 | tf_op jit(solution)/shard_map/all_gather | solution.py:139
  73.9 209.9 %all-gather.12.cloned.1.call-start = ((), (), s32[]{:S(2)}) async-start(), calls=%async_computation.5 | async-start | bytes 16850944 | tf_op jit(solution)/shard_map/all_gather | solution.py:197
  117.5 13.0 %copy-start.7 = (bf16[88,1408]{1,0:T(8,128)(2,1)S(1)}, bf16[88,1408]{1,0:T(8,128)(2,1)}, u32[]{:S(2)}) copy-start(bf16[88,1408]{1,0:T(8,128)(2,1)} %param.17) | copy-start | bytes 743428
  125.9 4.6 %copy-start.1 = (bf16[1408,2048]{0,1:T(8,128)(2,1)S(1)}, bf16[1408,2048]{0,1:T(8,128)(2,1)}, u32[]{:S(2)}) copy-start(bf16[1408,2048]{0,1:T(8,128)(2,1)} %copy.72) | copy-start | bytes 17301508
  143.4 99.5 %copy-start.5 = (bf16[1408]{0:T(1024)(128)(2,1)S(1)}, bf16[1408]{0:T(1024)(128)(2,1)}, u32[]{:S(2)}) copy-start(bf16[1408]{0:T(1024)(128)(2,1)} %param.23) | copy-start | bytes 8452
  235.5 16.2 %all-to-all-start.1 = ((bf16[88,16,128]{2,0,1:T(8,128)(2,1)}), bf16[88,16,128]{2,0,1:T(8,128)(2,1)S(1)}, u32[]{:S(2)}, u32[]{:S(2)}) async-start(bf16[88,16,128]{2,0,1:T(8,128)(2,1)} %copy.88), calls=%async_computation.1 | async-start | bytes 720896 | tf_op jit(solution)/shard_map/all_to_all | solution.py:183
  242.7 92.7 %all-gather.14.cloned.1.call-start = ((), (), s32[]{:S(2)}) async-start(), calls=%async_computation.6 | async-start | bytes 1531904 | tf_op jit(solution)/shard_map/all_gather | solution.py:200
Sparse Core Ops, SparseCore 0:
  9.5 63.5 all-gather.5
  74.8 40.7 all-gather.7
  117.8 50.4 all-gather.9
  170.3 113.4 all-gather.11
  292.7 42.6 all-gather.13

commit v5 on v4

--- a/solution.py
+++ b/solution.py
@@ -136,7 +136,6 @@
     score_scale = HD ** (-0.5)
     col_index = lax.axis_index("col")
     full_rows = lax.all_gather(hidden, "col", axis=0, tiled=True)
-    out_weight = lax.all_gather(w_out, "col", axis=0, tiled=True)
     full_float = full_rows.astype(jnp.float32)
     in_mean = jnp.sum(full_float, axis=0, keepdims=True) / model_width
     in_square = jnp.sum(full_float * full_float, axis=0, keepdims=True) / model_width
@@ -174,6 +173,11 @@
     pair_local, _ = lax.optimization_barrier((pair_local, full_rows))
     pair_all = lax.all_gather(pair_local, "row", axis=2, tiled=True)
     segment_line = pair_all[0, HD].astype(jnp.int32)
+    weight_stack = jnp.concatenate([w_out[None], w_merge], axis=0)
+    weight_stack, _ = lax.optimization_barrier((weight_stack, pair_all))
+    weights_full = lax.all_gather(weight_stack, "col", axis=1, tiled=True)
+    out_weight = weights_full[0]
+    merge_full = weights_full[1:]
     kb_map, flags = block_tables(segment_ids, segment_line, lax.axis_index("row") * tok_rows)
     attended_rows = attention(
         query_rows, segment_ids.astype(jnp.float32)[:, None], pair_all, kb_map, flags, score_scale
@@ -193,8 +197,6 @@
         * lax.rsqrt(row_square - row_mean * row_mean + EPSILON)
         * gain_merge.astype(jnp.float32)[:, None]
     ).astype(jnp.bfloat16)
-    merge_weight, _ = lax.optimization_barrier((w_merge, pair_all))
-    merge_full = lax.all_gather(merge_weight, "col", axis=1, tiled=True)
     grouped = merger_chunk.reshape(model_width, chunk // 4, 4)
     merged_here = jnp.einsum("fgi,ifd->gd", grouped, merge_full, preferred_element_type=jnp.float32)
     merged_all = lax.all_gather(merged_here.astype(jnp.bfloat16), "col", axis=0, tiled=True)

time: 349 us -> 316 us (0.905)
  Pallas kernels: 90.1 us -> 66.5 us
  waiting for transfers between devices: 151 us -> 142 us
    pallas_call x1, Pallas kernels: 90.1 us -> 66.5 us  [attention(): pl.pallas_call(kernel, grid_spec=grid_spec, out_shape=jax.ShapeDtypeStruc...]
    all_gather x2 -> x1, waiting for transfers between devices: 28.5 us -> 20 us  [on_device(): weights_full = lax.all_gather(weight_stack, 'col', axis=1, tiled=True)]
  transfers between devices with their start and end apart: 7 -> 6, of which waited for: 6 -> 6; matrix products, arithmetic and copies ran while one was open for 18% -> 20% of each run, Pallas kernels for 26% -> 21%
where the time goes in v5:
time: 316 us; the launch traced here: 312 us
  waiting for transfers between devices  142 us (45%)
  Pallas kernels  66.5 us (21%)
  local copies, waits for them, and re-layouts  36.9 us (12%)
  other arithmetic  24.9 us (8%)
  starting transfers between devices  14.8 us (5%)
  matrix products  14 us (4%)
  between operations  13.4 us (4%)
    pallas_call x1, Pallas kernels, attention(): pl.pallas_call(kernel, grid_spec=grid_spec, out_shape=jax.ShapeDtypeStruc...  66.5 us
    all_gather x1, waiting for transfers between devices, on_device(): lax.all_gather(merged_here.astype(jnp.bfloat16), 'col', axis=0, tiled=True)  41.4 us
    all_gather x1, waiting for transfers between devices, on_device(): pair_all = lax.all_gather(pair_local, 'row', axis=2, tiled=True)  41.2 us
    all_gather x1, waiting for transfers between devices, on_device(): full_rows = lax.all_gather(hidden, 'col', axis=0, tiled=True)  28.9 us
    all_gather x1, waiting for transfers between devices, on_device(): weights_full = lax.all_gather(weight_stack, 'col', axis=1, tiled=True)  20 us
    all_to_all x1, waiting for transfers between devices, on_device(): picked_full = lax.all_to_all(picked_copies, 'col', 0, 0, tiled=True)  8.42 us
    all_gather x1, local copies, waits for them, and re-layouts, on_device(): full_rows = lax.all_gather(hidden, 'col', axis=0, tiled=True)  8.36 us
    convert_element_type x1, other arithmetic, on_device(): full_float = full_rows.astype(jnp.float32)  7.81 us
  transfers between devices with their start and end apart: 6, of which 6 were waited for; matrix products, arithmetic and copies ran while one was open for 20% of the time, Pallas kernels for 21%

profile of v5, /device:TPU:78, one launch (start us, length us, event | category | flops | bytes accessed | tf_op | source)
XLA Modules:
  0.0 312.3 jit_solution(4229310052682958290)
XLA Ops:
  6.5 0.7 all-gather.5.cloned.1.call-update
  7.3 1.3 copy.73
  8.5 0.7 compare_select_fusion
  9.2 0.8 gather_fusion
  10.0 0.7 compare_and_fusion.2
  10.9 0.9 broadcast_in_dim.61
  11.8 7.4 %all-to-all-start = ((bf16[16,88,200]{2,1,0:T(8,128)(2,1)}), bf16[16,88,200]{2,1,0:T(8,128)(2,1)S(1)}, u32[]{:S(2)}, u32[]{:S(2)}) async-start(bf16[16,88,200]{2,1,0:T(8,128)(2,1)} %broadcast_in_dim.61), calls=%async_computation | async-start | bytes 1441792 | tf_op jit(solution)/shard_map/all_to_all | solution.py:154
  19.3 0.8 mul.104
  20.1 2.4 copy.76
  22.5 0.6 fusion.24
  23.1 0.7 and_reduce_fusion
  23.9 8.4 %all-to-all-done = bf16[16,88,200]{2,1,0:T(8,128)(2,1)S(1)} async-done(((bf16[16,88,200]{2,1,0:T(8,128)(2,1)}), bf16[16,88,200]{2,1,0:T(8,128)(2,1)S(1)}, u32[]{:S(2)}, u32[]{:S(2)}) %all-to-all-start) | async-done | bytes 563232 | tf_op jit(solution)/shard_map/all_to_all | solution.py:154
  32.8 0.3 convolution_convert_fusion
  33.3 6.9 %scatter_fusion = bf16[2,88,2048]{1,0,2:T(2,128)(2,1)S(1)} fusion(bf16[2,88,2048]{1,0,2:T(2,128)(2,1)S(1)} %copy.76, s32[200]{0:T(256)S(1)} %bitcast.77, bf16[200,2,88]{2,1,0:T(2,128)(2,1)S(1)} %bitcast.71), kind=kCustom, calls=%fused_computation.7 | custom fusion | bytes 212000 | tf_op jit(solution)/shard_map/scatter | solution.py:169
  40.2 0.8 copy.77
  41.0 1.9 broadcast_select_fusion
  42.9 1.4 scatter.13
  44.3 28.9 %all-gather.5.cloned.1.call-done = bf16[1408,2048]{1,0:T(8,128)(2,1)} async-done(((bf16[88,2048]{1,0:T(8,128)(2,1)}), bf16[1408,2048]{1,0:T(8,128)(2,1)}) %all-gather.5.cloned.1.call-update) | async-done | bytes 5767184 | tf_op jit(solution)/shard_map/all_gather | solution.py:138
  73.3 1.2 pad_maximum_fusion
  74.4 41.2 %all-gather.7.cloned.1.call-done.k_ref.v_ref = bf16[2,96,16384]{2,1,0:T(8,128)(2,1)} async-done(((bf16[2,96,2048]{2,1,0:T(8,128)(2,1)}), bf16[2,96,16384]{2,1,0:T(8,128)(2,1)}) %all-gather.7.cloned.1.call-update) | async-done | bytes 6291472 | tf_op jit(solution)/shard_map/all_gather | solution.py:174
  115.9 1.3 copy.87.qs_ref
  117.5 8.4 %copy.72 = bf16[1408,2048]{0,1:T(8,128)(2,1)} copy(bf16[1408,2048]{1,0:T(8,128)(2,1)} %all-gather.5.cloned.1.call-done) | data formatting | bytes 11534336 | tf_op jit(solution)/shard_map/all_gather | solution.py:138
  125.9 4.6 %convert_reduce_fusion = (f32[2048]{0:T(1024)S(1)}, f32[2048]{0:T(1024)S(1)}) fusion(bf16[1408,2048]{0,1:T(8,128)(2,1)} %copy.72), kind=kLoop, calls=%fused_computation.12 | loop fusion | flops 11530240 | bytes 5783552 | tf_op jit(solution)/shard_map/reduce_sum | solution.py:140
  130.5 0.5 copy-done.1
  131.0 2.8 fusion.5
  134.0 0.9 pad.12.q_ref
  135.0 1.2 fusion.17
  136.6 0.9 gather_fusion.4
  137.6 0.9 gather_fusion.5
  139.1 0.7 sort.17
  140.0 0.9 gather_fusion.2
  141.0 0.9 gather_fusion.6
  142.0 0.6 select_select_fusion
  142.6 0.6 gather_fusion.3
  143.3 0.6 fusion.19.kb_map
  143.9 66.5 %shard_map.109 = bf16[2048,96]{1,0:T(8,128)(2,1)} custom-call(s32[4,16]{1,0:T(4,128)} %fusion.19.kb_map, s32[4,16]{1,0:T(4,128)} %get-tuple-element.34.flags, bf16[2048,96]{1,0:T(8,128)(2,1)} %pad.12.q_ref, f32[2048,1]{1,0:T(8,128)} %copy.87.qs_ref, bf16[2,96,16384]{2,1,0:T(8,128)(2,1)} %all-gather.7.cloned.1.call-done.k_ref.v_ref, ...), custom_call_target="tpu_custom_call" | custom-call | tf_op jit(solution)/shard_map/pallas_call | solution.py:110
  210.4 2.0 copy.88
  212.4 7.3 %all-to-all-start.1 = ((bf16[88,16,128]{2,0,1:T(8,128)(2,1)}), bf16[88,16,128]{2,0,1:T(8,128)(2,1)S(1)}, u32[]{:S(2)}, u32[]{:S(2)}) async-start(bf16[88,16,128]{2,0,1:T(8,128)(2,1)} %copy.88), calls=%async_computation.1 | async-start | bytes 720896 | tf_op jit(solution)/shard_map/all_to_all | solution.py:187
  219.7 7.8 %convert_element_type.70 = f32[1408,2048]{0,1:T(8,128)} convert(bf16[1408,2048]{0,1:T(8,128)(2,1)} %copy.72) | non-fusion elementwise | flops 2883584 | bytes 17301504 | tf_op jit(solution)/shard_map/convert_element_type | solution.py:139
  227.5 1.1 all-to-all-done.1
  228.6 20.0 %all-gather.9.cloned.1.call-done = bf16[5,1408,1408]{2,1,0:T(8,128)(2,1)} async-done(((bf16[5,88,1408]{2,1,0:T(8,128)(2,1)}), bf16[5,1408,1408]{2,1,0:T(8,128)(2,1)}) %all-gather.9.cloned.1.call-update) | async-done | bytes 19824656 | tf_op jit(solution)/shard_map/all_gather | solution.py:178
  248.6 3.2 %fusion.22 = (f32[128]{0:T(128)S(1)}, f32[128]{0:T(128)S(1)}, f32[1408,128]{0,1:T(8,128)S(1)}) fusion(bf16[1408,128]{1,0:T(8,128)(2,1)S(1)} %bitcast.72, bf16[5,1408,1408]{2,1,0:T(8,128)(2,1)} %all-gather.9.cloned.1.call-done, f32[1408,2048]{0,1:T(8,128)} %convert_element_type.70, s32[]{:T(128)S(6)} %select_n.146), kind=kOutput, calls=%fused_computation.94 | convolution fusion | flops 508231424 | bytes 5768196 | tf_op jit(solution)/shard_map/dot_general | solution.py:189
  252.1 7.5 %fusion.9 = bf16[32,1408]{1,0:T(8,128)(2,1)} fusion(bf16[5,1408,1408]{2,1,0:T(8,128)(2,1)} %all-gather.9.cloned.1.call-done, bf16[1408,32,4]{0,2,1:T(4,128)(2,1)S(1)} %reshape.354), kind=kOutput, calls=%fused_computation.19 | convolution fusion | flops 507555840 | bytes 16310272 | tf_op jit(solution)/shard_map/fgi,ifd->gd/dot_general | solution.py:201
  259.6 0.7 fusion.20
  260.3 0.7 compare_bitcast_fusion
  261.0 41.4 %all-gather.11.cloned.1.call-done = bf16[512,1408]{1,0:T(8,128)(2,1)} async-done(((bf16[32,1408]{1,0:T(8,128)(2,1)}), bf16[512,1408]{1,0:T(8,128)(2,1)}) %all-gather.11.cloned.1.call-update) | async-done | bytes 1441808 | tf_op jit(solution)/shard_map/all_gather | solution.py:202
  302.4 2.5 gather_fusion.1
  305.0 0.8 bitcast_select_fusion
  (76 shorter events, 3.8 us)
Async XLA Ops:
  6.5 26.3 %copy-start = (bf16[2,88,1408]{2,1,0:T(8,128)(2,1)S(1)}, bf16[2,88,1408]{2,1,0:T(8,128)(2,1)}, u32[]{:S(2)}) copy-start(bf16[2,88,1408]{2,1,0:T(8,128)(2,1)} %param.18) | copy-start | bytes 1486852
  6.5 16.6 %copy-start.8 = (s32[3]{0:T(128)S(1)}, s32[3]{0:T(128)}, u32[]{:S(2)}) copy-start(s32[3]{0:T(128)} %constant.156.clone.1) | copy-start | bytes 40
  6.5 17.3 %copy-start.5 = (s32[2048]{0:T(1024)S(1)}, s32[2048]{0:T(1024)}, u32[]{:S(2)}) copy-start(s32[2048]{0:T(1024)} %param.21) | copy-start | bytes 24580
  6.5 66.7 %all-gather.5.cloned.1.call-start = ((), (), s32[]{:S(2)}) async-start(), calls=%async_computation.2 | async-start | bytes 6127616 | tf_op jit(solution)/shard_map/all_gather | solution.py:138
  11.8 61.5 %copy-start.3 = (bf16[4,88,1408]{2,1,0:T(8,128)(2,1)S(1)}, bf16[4,88,1408]{2,1,0:T(8,128)(2,1)}, u32[]{:S(2)}) copy-start(bf16[4,88,1408]{2,1,0:T(8,128)(2,1)} %param.24) | copy-start | bytes 2973700
  11.8 61.5 %copy-start.4 = (bf16[88,1408]{1,0:T(8,128)(2,1)S(1)}, bf16[88,1408]{1,0:T(8,128)(2,1)}, u32[]{:S(2)}) copy-start(bf16[88,1408]{1,0:T(8,128)(2,1)} %param.22) | copy-start | bytes 743428
  11.8 20.5 %all-to-all-start = ((bf16[16,88,200]{2,1,0:T(8,128)(2,1)}), bf16[16,88,200]{2,1,0:T(8,128)(2,1)S(1)}, u32[]{:S(2)}, u32[]{:S(2)}) async-start(bf16[16,88,200]{2,1,0:T(8,128)(2,1)} %broadcast_in_dim.61), calls=%async_computation | async-start | bytes 1441792 | tf_op jit(solution)/shard_map/all_to_all | solution.py:154
  19.3 96.4 %all-gather.7.cloned.1.call-start = ((), (), s32[]{:S(2)}) async-start(), calls=%async_computation.3 | async-start | bytes 7077888 | tf_op jit(solution)/shard_map/all_gather | solution.py:174
  32.5 83.2 %copy-start.6 = (bf16[1408]{0:T(1024)(128)(2,1)S(1)}, bf16[1408]{0:T(1024)(128)(2,1)}, u32[]{:S(2)}) copy-start(bf16[1408]{0:T(1024)(128)(2,1)} %param.16) | copy-start | bytes 8452
  44.3 28.9 %copy-start.2 = (bf16[2,96,2048]{2,1,0:T(8,128)(2,1)}, bf16[2,96,2048]{2,1,0:T(8,128)(2,1)S(1)}, u32[]{:S(2)}) copy-start(bf16[2,96,2048]{2,1,0:T(8,128)(2,1)S(1)} %scatter.13) | copy-start | bytes 2359300
  73.2 175.3 %all-gather.9.cloned.1.call-start = ((), (), s32[]{:S(2)}) async-start(), calls=%async_computation.4 | async-start | bytes 21063680 | tf_op jit(solution)/shard_map/all_gather | solution.py:178
  117.5 13.0 %copy-start.9 = (bf16[88,1408]{1,0:T(8,128)(2,1)S(1)}, bf16[88,1408]{1,0:T(8,128)(2,1)}, u32[]{:S(2)}) copy-start(bf16[88,1408]{1,0:T(8,128)(2,1)} %param.17) | copy-start | bytes 743428
  125.9 5.1 %copy-start.1 = (bf16[1408,2048]{0,1:T(8,128)(2,1)S(1)}, bf16[1408,2048]{0,1:T(8,128)(2,1)}, u32[]{:S(2)}) copy-start(bf16[1408,2048]{0,1:T(8,128)(2,1)} %copy.72) | copy-start | bytes 17301508
  143.9 75.8 %copy-start.7 = (bf16[1408]{0:T(1024)(128)(2,1)S(1)}, bf16[1408]{0:T(1024)(128)(2,1)}, u32[]{:S(2)}) copy-start(bf16[1408]{0:T(1024)(128)(2,1)} %param.23) | copy-start | bytes 8452
  212.4 16.2 %all-to-all-start.1 = ((bf16[88,16,128]{2,0,1:T(8,128)(2,1)}), bf16[88,16,128]{2,0,1:T(8,128)(2,1)S(1)}, u32[]{:S(2)}, u32[]{:S(2)}) async-start(bf16[88,16,128]{2,0,1:T(8,128)(2,1)} %copy.88), calls=%async_computation.1 | async-start | bytes 720896 | tf_op jit(solution)/shard_map/all_to_all | solution.py:187
  219.6 82.8 %all-gather.11.cloned.1.call-start = ((), (), s32[]{:S(2)}) async-start(), calls=%async_computation.5 | async-start | bytes 1531904 | tf_op jit(solution)/shard_map/all_gather | solution.py:202
Sparse Core Ops, SparseCore 0:
  9.5 63.6 all-gather.4
  74.9 40.7 all-gather.6
  117.9 130.6 all-gather.8
  259.7 42.6 all-gather.10

commit v6 on v5

--- a/solution.py
+++ b/solution.py
@@ -57,6 +57,49 @@
     @pl.when(j == n_steps - 1)
     def _():
         o_ref[...] = (acc_ref[...] / l_ref[...]).astype(o_ref.dtype)
+
+
+def _row_gather_kernel(x_ref, o_ref, send_sems, recv_sems, local_sem, *, n_row):
+    me = lax.axis_index("row")
+    col = lax.axis_index("col")
+    barrier = pltpu.get_barrier_semaphore()
+    for k in range(1, n_row):
+        peer = lax.rem(me + k, n_row)
+        pl.semaphore_signal(barrier, inc=1, device_id=(peer, col), device_id_type=pl.DeviceIdType.MESH)
+    pl.semaphore_wait(barrier, n_row - 1)
+    local = pltpu.make_async_copy(x_ref, o_ref.at[me], local_sem)
+    local.start()
+    copies = []
+    for k in range(1, n_row):
+        peer = lax.rem(me + k, n_row)
+        copy = pltpu.make_async_remote_copy(
+            src_ref=x_ref,
+            dst_ref=o_ref.at[me],
+            send_sem=send_sems.at[k],
+            recv_sem=recv_sems.at[k],
+            device_id=(peer, col),
+            device_id_type=pl.DeviceIdType.MESH,
+        )
+        copy.start()
+        copies.append(copy)
+    local.wait()
+    for copy in copies:
+        copy.wait()
+
+
+def row_gather(x, n_row):
+    return pl.pallas_call(
+        functools.partial(_row_gather_kernel, n_row=n_row),
+        out_shape=jax.ShapeDtypeStruct((n_row,) + x.shape, x.dtype),
+        in_specs=[pl.BlockSpec(memory_space=pl.ANY)],
+        out_specs=pl.BlockSpec(memory_space=pl.ANY),
+        scratch_shapes=[
+            pltpu.SemaphoreType.DMA((n_row,)),
+            pltpu.SemaphoreType.DMA((n_row,)),
+            pltpu.SemaphoreType.DMA,
+        ],
+        compiler_params=pltpu.CompilerParams(collective_id=0, has_side_effects=True),
+    )(x)
 
 
 def block_tables(q_seg, k_seg, q_start):
@@ -87,7 +130,8 @@
 
 def attention(q_t, q_seg_f, kv, kb_map, flags, scale, interpret=False):
     n_tok = q_t.shape[0]
-    n_keys = kv.shape[2]
+    per_peer = kv.shape[3] // K_BLOCK
+    n_keys = kv.shape[0] * kv.shape[3]
     n_q = n_tok // Q_BLOCK
     n_k = n_keys // K_BLOCK
     kernel = functools.partial(_attn_kernel, scale=scale, n_steps=n_k)
@@ -97,8 +141,8 @@
         in_specs=[
             pl.BlockSpec((Q_BLOCK, PADW), lambda i, j, km, fl: (i, 0)),
             pl.BlockSpec((Q_BLOCK, 1), lambda i, j, km, fl: (i, 0)),
-            pl.BlockSpec((None, PADW, K_BLOCK), lambda i, j, km, fl: (0, 0, km[i, j])),
-            pl.BlockSpec((None, PADW, K_BLOCK), lambda i, j, km, fl: (1, 0, km[i, j])),
+            pl.BlockSpec((None, None, PADW, K_BLOCK), lambda i, j, km, fl: (km[i, j] // per_peer, 0, 0, km[i, j] % per_peer)),
+            pl.BlockSpec((None, None, PADW, K_BLOCK), lambda i, j, km, fl: (km[i, j] // per_peer, 1, 0, km[i, j] % per_peer)),
         ],
         out_specs=pl.BlockSpec((Q_BLOCK, PADW), lambda i, j, km, fl: (i, 0)),
         scratch_shapes=[
@@ -117,6 +161,7 @@
 
 
 def on_device(
+    n_row,
     hidden,
     gain_in,
     w_query,
@@ -135,19 +180,7 @@
     heads_here = local_width // HD
     score_scale = HD ** (-0.5)
     col_index = lax.axis_index("col")
-    full_rows = lax.all_gather(hidden, "col", axis=0, tiled=True)
-    full_float = full_rows.astype(jnp.float32)
-    in_mean = jnp.sum(full_float, axis=0, keepdims=True) / model_width
-    in_square = jnp.sum(full_float * full_float, axis=0, keepdims=True) / model_width
-    normed = (
-        (full_float - in_mean)
-        * lax.rsqrt(in_square - in_mean * in_mean + EPSILON)
-        * gain_in.astype(jnp.float32)[:, None]
-    ).astype(jnp.bfloat16)
-    query_rows = lax.dot_general(
-        normed, w_query, (((0,), (1,)), ((), ())), preferred_element_type=jnp.float32
-    ).astype(jnp.bfloat16)
-    query_rows = jnp.pad(query_rows, ((0, 0), (0, PADW - HD)))
+    gathered_rows = lax.all_gather(hidden, "col", axis=0, tiled=True)
     picked_rows = recompute_rows[0]
     hidden_picked = jnp.take(hidden, picked_rows, axis=1)
     picked_copies = jnp.broadcast_to(hidden_picked[None], (n_col,) + hidden_picked.shape)
@@ -170,11 +203,23 @@
 
     pair_local = jnp.pad(keys_values, ((0, 0), (0, PADW - HD), (0, 0)))
     pair_local = pair_local.at[0, HD].set(segment_ids.astype(jnp.bfloat16))
-    pair_local, _ = lax.optimization_barrier((pair_local, full_rows))
-    pair_all = lax.all_gather(pair_local, "row", axis=2, tiled=True)
-    segment_line = pair_all[0, HD].astype(jnp.int32)
+    pair_all = row_gather(pair_local, n_row)
+    full_rows, pair_all = lax.optimization_barrier((gathered_rows, pair_all))
+    full_float = full_rows.astype(jnp.float32)
+    in_mean = jnp.sum(full_float, axis=0, keepdims=True) / model_width
+    in_square = jnp.sum(full_float * full_float, axis=0, keepdims=True) / model_width
+    normed = (
+        (full_float - in_mean)
+        * lax.rsqrt(in_square - in_mean * in_mean + EPSILON)
+        * gain_in.astype(jnp.float32)[:, None]
+    ).astype(jnp.bfloat16)
+    query_rows = lax.dot_general(
+        normed, w_query, (((0,), (1,)), ((), ())), preferred_element_type=jnp.float32
+    ).astype(jnp.bfloat16)
+    query_rows = jnp.pad(query_rows, ((0, 0), (0, PADW - HD)))
+    segment_line = pair_all[:, 0, HD].reshape(-1).astype(jnp.int32)
     weight_stack = jnp.concatenate([w_out[None], w_merge], axis=0)
-    weight_stack, _ = lax.optimization_barrier((weight_stack, pair_all))
+    weight_stack, _ = lax.optimization_barrier((weight_stack, full_rows))
     weights_full = lax.all_gather(weight_stack, "col", axis=1, tiled=True)
     out_weight = weights_full[0]
     merge_full = weights_full[1:]
@@ -222,7 +267,7 @@
         P("row", None, None),
     )
     return jax.shard_map(
-        on_device,
+        functools.partial(on_device, mesh.shape["row"]),
         mesh=mesh,
         in_specs=placed,
         out_specs=P("row", "col", None, None),

time: 316 us -> 316 us (level)
  waiting for transfers between devices: 142 us -> 66.9 us
  Pallas kernels: 66.5 us -> 139 us
    pallas_call x0 -> x1, Pallas kernels: none -> 70.3 us  [row_gather(): pl.pallas_call(functools.partial(_row_gather_kernel, n_row=n_row), out_sh...]
    all_gather x2 -> x1, waiting for transfers between devices: 70.1 us -> 0.02 us  [on_device(): gathered_rows = lax.all_gather(hidden, 'col', axis=0, tiled=True)]
    optimization_barrier x0 -> x1, local copies, waits for them, and re-layouts: none -> 8.36 us  [on_device(): full_rows, pair_all = lax.optimization_barrier((gathered_rows, pair_all))]
    all_gather x1 -> x0, local copies, waits for them, and re-layouts: 8.36 us -> none  [on_device(): full_rows = lax.all_gather(hidden, 'col', axis=0, tiled=True)]
  transfers between devices with their start and end apart: 6 -> 5, of which waited for: 6 -> 4; matrix products, arithmetic and copies ran while one was open for 20% -> 20% of each run, Pallas kernels for 21% -> 45%
where the time goes in v6:
time: 316 us; the launch traced here: 312 us
  Pallas kernels  139 us (44%)
  waiting for transfers between devices  66.9 us (21%)
  local copies, waits for them, and re-layouts  37.9 us (12%)
  other arithmetic  25.6 us (8%)
  starting transfers between devices  15.3 us (5%)
  matrix products  14 us (4%)
  between operations  13.5 us (4%)
    pallas_call x1, Pallas kernels, row_gather(): pl.pallas_call(functools.partial(_row_gather_kernel, n_row=n_row), out_sh...  70.3 us
    pallas_call x1, Pallas kernels, attention(): pl.pallas_call(kernel, grid_spec=grid_spec, out_shape=jax.ShapeDtypeStruc...  68.6 us
    all_gather x1, waiting for transfers between devices, on_device(): lax.all_gather(merged_here.astype(jnp.bfloat16), 'col', axis=0, tiled=True)  41.4 us
    all_gather x1, waiting for transfers between devices, on_device(): weights_full = lax.all_gather(weight_stack, 'col', axis=1, tiled=True)  17.1 us
    optimization_barrier x1, local copies, waits for them, and re-layouts, on_device(): full_rows, pair_all = lax.optimization_barrier((gathered_rows, pair_all))  8.36 us
    all_to_all x1, starting transfers between devices, on_device(): attended_chunk = lax.all_to_all(attended, 'col', 1, 0, tiled=True)  7.9 us
    convert_element_type x1, other arithmetic, on_device(): full_float = full_rows.astype(jnp.float32)  7.72 us
    scatter x2, local copies, waits for them, and re-layouts, on_device(): keys_values = kv_cache.at[:, :, picked_rows].set(fresh_pairs)  7.64 us
  transfers between devices with their start and end apart: 5, of which 4 were waited for; matrix products, arithmetic and copies ran while one was open for 20% of the time, Pallas kernels for 45%

profile of v6, /device:TPU:78, one launch (start us, length us, event | category | flops | bytes accessed | tf_op | source)
XLA Modules:
  0.0 312.1 jit_solution(6772071847111193657)
XLA Ops:
  6.6 0.7 all-gather.4.cloned.1.call-update
  7.3 1.3 copy.72
  8.5 0.7 compare_select_fusion
  9.2 0.8 gather_fusion
  10.0 0.7 compare_and_fusion.2
  10.9 0.9 broadcast_in_dim.60
  11.9 7.3 %all-to-all-start = ((bf16[16,88,200]{2,1,0:T(8,128)(2,1)}), bf16[16,88,200]{2,1,0:T(8,128)(2,1)S(1)}, u32[]{:S(2)}, u32[]{:S(2)}) async-start(bf16[16,88,200]{2,1,0:T(8,128)(2,1)} %broadcast_in_dim.60), calls=%async_computation | async-start | bytes 1441792 | tf_op jit(solution)/shard_map/all_to_all | solution.py:187
  19.2 1.4 and_reduce_fusion
  20.6 0.7 fusion.23
  21.3 0.8 mul.103
  22.0 2.4 copy.75
  24.5 1.2 pad_maximum_fusion
  25.6 6.5 %all-to-all-done = bf16[16,88,200]{2,1,0:T(8,128)(2,1)S(1)} async-done(((bf16[16,88,200]{2,1,0:T(8,128)(2,1)}), bf16[16,88,200]{2,1,0:T(8,128)(2,1)S(1)}, u32[]{:S(2)}, u32[]{:S(2)}) %all-to-all-start) | async-done | bytes 563232 | tf_op jit(solution)/shard_map/all_to_all | solution.py:187
  32.7 0.3 convolution_convert_fusion
  33.1 6.9 %scatter_fusion = bf16[2,88,2048]{1,0,2:T(2,128)(2,1)S(1)} fusion(bf16[2,88,2048]{1,0,2:T(2,128)(2,1)S(1)} %copy.75, s32[200]{0:T(256)S(1)} %bitcast.77, bf16[200,2,88]{2,1,0:T(2,128)(2,1)S(1)} %bitcast.71), kind=kCustom, calls=%fused_computation.7 | custom fusion | bytes 212000 | tf_op jit(solution)/shard_map/scatter | solution.py:202
  40.0 0.8 copy.76
  40.9 2.0 broadcast_select_fusion
  42.9 1.4 scatter.13.x_ref
  44.3 0.9 copy-done.2
  45.2 70.3 %shard_map.109.k_ref.v_ref = bf16[8,2,96,2048]{3,2,1,0:T(8,128)(2,1)} custom-call(bf16[2,96,2048]{2,1,0:T(8,128)(2,1)} %copy-done.2), custom_call_target="tpu_custom_call" | custom-call | tf_op jit(solution)/shard_map/pallas_call | solution.py:91
  115.8 1.3 copy.87.qs_ref
  117.4 8.4 %copy.77 = bf16[1408,2048]{0,1:T(8,128)(2,1)} copy(bf16[1408,2048]{1,0:T(8,128)(2,1)} %all-gather.4.cloned.1.call-done) | data formatting | bytes 11534336 | tf_op jit(solution)/shard_map/optimization_barrier | solution.py:207
  125.8 4.6 %convert_reduce_fusion = (f32[2048]{0:T(1024)S(1)}, f32[2048]{0:T(1024)S(1)}) fusion(bf16[1408,2048]{0,1:T(8,128)(2,1)} %copy.77), kind=kLoop, calls=%fused_computation.12 | loop fusion | flops 11530240 | bytes 5783552 | tf_op jit(solution)/shard_map/reduce_sum | solution.py:209
  130.4 0.5 copy-done.1
  130.9 2.8 fusion.5
  134.0 0.9 pad.12.q_ref
  134.9 1.1 convert_reduce_fusion.2
  136.4 0.9 gather_fusion.4
  137.5 0.9 gather_fusion.5
  139.0 0.7 sort.17
  139.9 0.9 gather_fusion.2
  140.9 0.9 gather_fusion.6
  141.9 0.6 select_select_fusion
  142.5 0.6 gather_fusion.3
  143.2 0.6 fusion.18.kb_map
  143.8 68.6 %shard_map.110 = bf16[2048,96]{1,0:T(8,128)(2,1)} custom-call(s32[4,16]{1,0:T(4,128)} %fusion.18.kb_map, s32[4,16]{1,0:T(4,128)} %get-tuple-element.36.flags, bf16[2048,96]{1,0:T(8,128)(2,1)} %pad.12.q_ref, f32[2048,1]{1,0:T(8,128)} %copy.87.qs_ref, bf16[8,2,96,2048]{3,2,1,0:T(8,128)(2,1)} %shard_map.109.k_ref.v_ref, ...), custom_call_target="tpu_custom_call" | custom-call | tf_op jit(solution)/shard_map/pallas_call | solution.py:154
  212.4 2.0 copy.88
  214.4 7.9 %all-to-all-start.1 = ((bf16[88,16,128]{2,0,1:T(8,128)(2,1)}), bf16[88,16,128]{2,0,1:T(8,128)(2,1)S(1)}, u32[]{:S(2)}, u32[]{:S(2)}) async-start(bf16[88,16,128]{2,0,1:T(8,128)(2,1)} %copy.88), calls=%async_computation.1 | async-start | bytes 720896 | tf_op jit(solution)/shard_map/all_to_all | solution.py:232
  222.4 7.7 %convert_element_type.77 = f32[1408,2048]{0,1:T(8,128)} convert(bf16[1408,2048]{0,1:T(8,128)(2,1)} %copy.77) | non-fusion elementwise | flops 2883584 | bytes 17301504 | tf_op jit(solution)/shard_map/convert_element_type | solution.py:208
  230.1 1.2 all-to-all-done.1
  231.3 17.1 %all-gather.6.cloned.1.call-done = bf16[5,1408,1408]{2,1,0:T(8,128)(2,1)} async-done(((bf16[5,88,1408]{2,1,0:T(8,128)(2,1)}), bf16[5,1408,1408]{2,1,0:T(8,128)(2,1)}) %all-gather.6.cloned.1.call-update) | async-done | bytes 19824656 | tf_op jit(solution)/shard_map/all_gather | solution.py:223
  248.4 3.2 %fusion.21 = (f32[128]{0:T(128)S(1)}, f32[128]{0:T(128)S(1)}, f32[1408,128]{0,1:T(8,128)S(1)}) fusion(bf16[1408,128]{1,0:T(8,128)(2,1)S(1)} %bitcast.72, bf16[5,1408,1408]{2,1,0:T(8,128)(2,1)} %all-gather.6.cloned.1.call-done, f32[1408,2048]{0,1:T(8,128)} %convert_element_type.77, s32[]{:T(128)S(6)} %select_n.149), kind=kOutput, calls=%fused_computation.93 | convolution fusion | flops 508231424 | bytes 5768196 | tf_op jit(solution)/shard_map/dot_general | solution.py:234
  251.9 7.5 %fusion.9 = bf16[32,1408]{1,0:T(8,128)(2,1)} fusion(bf16[5,1408,1408]{2,1,0:T(8,128)(2,1)} %all-gather.6.cloned.1.call-done, bf16[1408,32,4]{0,2,1:T(4,128)(2,1)S(1)} %reshape.354), kind=kOutput, calls=%fused_computation.19 | convolution fusion | flops 507555840 | bytes 16310272 | tf_op jit(solution)/shard_map/fgi,ifd->gd/dot_general | solution.py:246
  259.4 0.7 fusion.19
  260.1 0.7 compare_bitcast_fusion
  260.8 41.4 %all-gather.8.cloned.1.call-done = bf16[512,1408]{1,0:T(8,128)(2,1)} async-done(((bf16[32,1408]{1,0:T(8,128)(2,1)}), bf16[512,1408]{1,0:T(8,128)(2,1)}) %all-gather.8.cloned.1.call-update) | async-done | bytes 1441808 | tf_op jit(solution)/shard_map/all_gather | solution.py:247
  302.3 2.5 gather_fusion.1
  304.8 0.8 bitcast_select_fusion
  (72 shorter events, 3.8 us)
Async XLA Ops:
  6.5 26.1 %copy-start = (bf16[2,88,1408]{2,1,0:T(8,128)(2,1)S(1)}, bf16[2,88,1408]{2,1,0:T(8,128)(2,1)}, u32[]{:S(2)}) copy-start(bf16[2,88,1408]{2,1,0:T(8,128)(2,1)} %param.18) | copy-start | bytes 1486852
  6.5 17.9 %copy-start.5 = (s32[2048]{0:T(1024)S(1)}, s32[2048]{0:T(1024)}, u32[]{:S(2)}) copy-start(s32[2048]{0:T(1024)} %param.21) | copy-start | bytes 24580
  6.5 17.9 %copy-start.4 = (bf16[88,1408]{1,0:T(8,128)(2,1)S(1)}, bf16[88,1408]{1,0:T(8,128)(2,1)}, u32[]{:S(2)}) copy-start(bf16[88,1408]{1,0:T(8,128)(2,1)} %param.22) | copy-start | bytes 743428
  6.5 17.9 %copy-start.3 = (bf16[4,88,1408]{2,1,0:T(8,128)(2,1)S(1)}, bf16[4,88,1408]{2,1,0:T(8,128)(2,1)}, u32[]{:S(2)}) copy-start(bf16[4,88,1408]{2,1,0:T(8,128)(2,1)} %param.24) | copy-start | bytes 2973700
  6.5 109.0 %all-gather.4.cloned.1.call-start = ((), (), s32[]{:S(2)}) async-start(), calls=%async_computation.2 | async-start | bytes 6127616 | tf_op jit(solution)/shard_map/all_gather | solution.py:183
  11.9 20.3 %all-to-all-start = ((bf16[16,88,200]{2,1,0:T(8,128)(2,1)}), bf16[16,88,200]{2,1,0:T(8,128)(2,1)S(1)}, u32[]{:S(2)}, u32[]{:S(2)}) async-start(bf16[16,88,200]{2,1,0:T(8,128)(2,1)} %broadcast_in_dim.60), calls=%async_computation | async-start | bytes 1441792 | tf_op jit(solution)/shard_map/all_to_all | solution.py:187
  19.2 229.2 %all-gather.6.cloned.1.call-start = ((), (), s32[]{:S(2)}) async-start(), calls=%async_computation.3 | async-start | bytes 21063680 | tf_op jit(solution)/shard_map/all_gather | solution.py:223
  40.0 75.6 %copy-start.6 = (bf16[1408]{0:T(1024)(128)(2,1)S(1)}, bf16[1408]{0:T(1024)(128)(2,1)}, u32[]{:S(2)}) copy-start(bf16[1408]{0:T(1024)(128)(2,1)} %param.16) | copy-start | bytes 8452
  44.3 0.9 copy-start.2
  117.4 13.0 %copy-start.8 = (bf16[88,1408]{1,0:T(8,128)(2,1)S(1)}, bf16[88,1408]{1,0:T(8,128)(2,1)}, u32[]{:S(2)}) copy-start(bf16[88,1408]{1,0:T(8,128)(2,1)} %param.17) | copy-start | bytes 743428
  125.8 5.1 %copy-start.1 = (bf16[1408,2048]{0,1:T(8,128)(2,1)S(1)}, bf16[1408,2048]{0,1:T(8,128)(2,1)}, u32[]{:S(2)}) copy-start(bf16[1408,2048]{0,1:T(8,128)(2,1)} %copy.77) | copy-start | bytes 17301508
  143.8 78.6 %copy-start.7 = (bf16[1408]{0:T(1024)(128)(2,1)S(1)}, bf16[1408]{0:T(1024)(128)(2,1)}, u32[]{:S(2)}) copy-start(bf16[1408]{0:T(1024)(128)(2,1)} %param.23) | copy-start | bytes 8452
  214.4 16.9 %all-to-all-start.1 = ((bf16[88,16,128]{2,0,1:T(8,128)(2,1)}), bf16[88,16,128]{2,0,1:T(8,128)(2,1)S(1)}, u32[]{:S(2)}, u32[]{:S(2)}) async-start(bf16[88,16,128]{2,0,1:T(8,128)(2,1)} %copy.88), calls=%async_computation.1 | async-start | bytes 720896 | tf_op jit(solution)/shard_map/all_to_all | solution.py:232
  222.3 79.9 %all-gather.8.cloned.1.call-start = ((), (), s32[]{:S(2)}) async-start(), calls=%async_computation.4 | async-start | bytes 1531904 | tf_op jit(solution)/shard_map/all_gather | solution.py:247
Sparse Core Ops, SparseCore 0:
  9.5 63.5 all-gather.3
  115.7 132.6 all-gather.5
  259.6 42.6 all-gather.7

commit v7 on v6

--- a/solution.py
+++ b/solution.py
@@ -59,43 +59,66 @@
         o_ref[...] = (acc_ref[...] / l_ref[...]).astype(o_ref.dtype)
 
 
-def _row_gather_kernel(x_ref, o_ref, send_sems, recv_sems, local_sem, *, n_row):
+def _row_gather_kernel(x_ref, o_ref, send_far, recv_far, send_pair, recv_pair, send_fwd, recv_fwd, local_sem, *, n_row):
+    mesh_ids = pl.DeviceIdType.MESH
+    n_chip = n_row // 2
     me = lax.axis_index("row")
     col = lax.axis_index("col")
+    chip = me // 2
+    core = me % 2
+    sibling = chip * 2 + 1 - core
+    far = [lax.rem(chip + k, n_chip) * 2 + core for k in range(1, n_chip)]
     barrier = pltpu.get_barrier_semaphore()
-    for k in range(1, n_row):
-        peer = lax.rem(me + k, n_row)
-        pl.semaphore_signal(barrier, inc=1, device_id=(peer, col), device_id_type=pl.DeviceIdType.MESH)
-    pl.semaphore_wait(barrier, n_row - 1)
+    for peer in far + [sibling]:
+        pl.semaphore_signal(barrier, inc=1, device_id=(peer, col), device_id_type=mesh_ids)
+    pl.semaphore_wait(barrier, n_chip)
     local = pltpu.make_async_copy(x_ref, o_ref.at[me], local_sem)
     local.start()
-    copies = []
-    for k in range(1, n_row):
-        peer = lax.rem(me + k, n_row)
+    pair = pltpu.make_async_remote_copy(
+        src_ref=x_ref, dst_ref=o_ref.at[me], send_sem=send_pair, recv_sem=recv_pair,
+        device_id=(sibling, col), device_id_type=mesh_ids,
+    )
+    pair.start()
+    outgoing = []
+    for k in range(1, n_chip):
         copy = pltpu.make_async_remote_copy(
-            src_ref=x_ref,
-            dst_ref=o_ref.at[me],
-            send_sem=send_sems.at[k],
-            recv_sem=recv_sems.at[k],
-            device_id=(peer, col),
-            device_id_type=pl.DeviceIdType.MESH,
+            src_ref=x_ref, dst_ref=o_ref.at[me], send_sem=send_far.at[k], recv_sem=recv_far.at[k],
+            device_id=(far[k - 1], col), device_id_type=mesh_ids,
         )
         copy.start()
-        copies.append(copy)
+        outgoing.append(copy)
+    forwards = []
+    for k in range(1, n_chip):
+        outgoing[k - 1].wait_recv()
+        source = lax.rem(chip + n_chip - k, n_chip) * 2 + core
+        forward = pltpu.make_async_remote_copy(
+            src_ref=o_ref.at[source], dst_ref=o_ref.at[source], send_sem=send_fwd.at[k],
+            recv_sem=recv_fwd.at[k], device_id=(sibling, col), device_id_type=mesh_ids,
+        )
+        forward.start()
+        forwards.append(forward)
     local.wait()
-    for copy in copies:
-        copy.wait()
+    pair.wait()
+    for copy in outgoing:
+        copy.wait_send()
+    for forward in forwards:
+        forward.wait()
 
 
 def row_gather(x, n_row):
+    n_chip = n_row // 2
     return pl.pallas_call(
         functools.partial(_row_gather_kernel, n_row=n_row),
         out_shape=jax.ShapeDtypeStruct((n_row,) + x.shape, x.dtype),
         in_specs=[pl.BlockSpec(memory_space=pl.ANY)],
         out_specs=pl.BlockSpec(memory_space=pl.ANY),
         scratch_shapes=[
-            pltpu.SemaphoreType.DMA((n_row,)),
-            pltpu.SemaphoreType.DMA((n_row,)),
+            pltpu.SemaphoreType.DMA((n_chip,)),
+            pltpu.SemaphoreType.DMA((n_chip,)),
+            pltpu.SemaphoreType.DMA,
+            pltpu.SemaphoreType.DMA,
+            pltpu.SemaphoreType.DMA((n_chip,)),
+            pltpu.SemaphoreType.DMA((n_chip,)),
             pltpu.SemaphoreType.DMA,
         ],
         compiler_params=pltpu.CompilerParams(collective_id=0, has_side_effects=True),

time: 316 us -> 300 us (0.949)
  waiting for transfers between devices: 66.9 us -> 48.8 us
    pallas_call x1, Pallas kernels: 68.6 us -> 99.8 us  [attention(): pl.pallas_call(kernel, grid_spec=grid_spec, out_shape=jax.ShapeDtypeStruc...]
    pallas_call x1, Pallas kernels: 70.3 us -> 39.9 us  [row_gather(): pl.pallas_call(functools.partial(_row_gather_kernel, n_row=n_row), out_sh...]
    all_gather x1, waiting for transfers between devices: 17.1 us -> 0.01 us  [on_device(): weights_full = lax.all_gather(weight_stack, 'col', axis=1, tiled=True)]
  transfers between devices with their start and end apart: 5 -> 5, of which waited for: 4 -> 2; matrix products, arithmetic and copies ran while one was open for 20% -> 21% of each run, Pallas kernels for 45% -> 47%
where the time goes in v7:
time: 300 us; the launch traced here: 296 us
  Pallas kernels  140 us (47%)
  waiting for transfers between devices  48.8 us (16%)
  local copies, waits for them, and re-layouts  37.8 us (13%)
  other arithmetic  25.7 us (9%)
  starting transfers between devices  16.6 us (6%)
  matrix products  14 us (5%)
  between operations  13.5 us (4%)
    pallas_call x1, Pallas kernels, attention(): pl.pallas_call(kernel, grid_spec=grid_spec, out_shape=jax.ShapeDtypeStruc...  99.8 us
    all_gather x1, waiting for transfers between devices, on_device(): lax.all_gather(merged_here.astype(jnp.bfloat16), 'col', axis=0, tiled=True)  41.7 us
    pallas_call x1, Pallas kernels, row_gather(): pl.pallas_call(functools.partial(_row_gather_kernel, n_row=n_row), out_sh...  39.9 us
    all_to_all x1, starting transfers between devices, on_device(): attended_chunk = lax.all_to_all(attended, 'col', 1, 0, tiled=True)  9.14 us
    optimization_barrier x1, local copies, waits for them, and re-layouts, on_device(): full_rows, pair_all = lax.optimization_barrier((gathered_rows, pair_all))  8.36 us
    scatter x2, local copies, waits for them, and re-layouts, on_device(): keys_values = kv_cache.at[:, :, picked_rows].set(fresh_pairs)  7.64 us
    convert_element_type x1, other arithmetic, on_device(): full_float = full_rows.astype(jnp.float32)  7.63 us
    dot_general x1, matrix products, on_device(): jnp.einsum('fgi,ifd->gd', grouped, merge_full, preferred_element_type=jnp...  7.51 us
  transfers between devices with their start and end apart: 5, of which 2 were waited for; matrix products, arithmetic and copies ran while one was open for 21% of the time, Pallas kernels for 47%

profile of v7, /device:TPU:78, one launch (start us, length us, event | category | flops | bytes accessed | tf_op | source)
XLA Modules:
  0.0 295.9 jit_solution(14953753056332026316)
XLA Ops:
  6.6 0.7 all-gather.4.cloned.1.call-update
  7.3 1.3 copy.72
  8.5 0.7 compare_select_fusion
  9.2 0.8 gather_fusion
  10.0 0.7 compare_and_fusion.2
  10.9 0.9 broadcast_in_dim.60
  11.9 7.3 %all-to-all-start = ((bf16[16,88,200]{2,1,0:T(8,128)(2,1)}), bf16[16,88,200]{2,1,0:T(8,128)(2,1)S(1)}, u32[]{:S(2)}, u32[]{:S(2)}) async-start(bf16[16,88,200]{2,1,0:T(8,128)(2,1)} %broadcast_in_dim.60), calls=%async_computation | async-start | bytes 1441792 | tf_op jit(solution)/shard_map/all_to_all | solution.py:210
  19.2 1.4 and_reduce_fusion
  20.6 0.7 fusion.23
  21.3 0.8 mul.103
  22.0 2.4 copy.75
  24.5 1.2 pad_maximum_fusion
  25.6 6.4 %all-to-all-done = bf16[16,88,200]{2,1,0:T(8,128)(2,1)S(1)} async-done(((bf16[16,88,200]{2,1,0:T(8,128)(2,1)}), bf16[16,88,200]{2,1,0:T(8,128)(2,1)S(1)}, u32[]{:S(2)}, u32[]{:S(2)}) %all-to-all-start) | async-done | bytes 563232 | tf_op jit(solution)/shard_map/all_to_all | solution.py:210
  32.0 0.3 convert_reduce_fusion.1
  32.6 0.3 convolution_convert_fusion
  33.0 6.9 %scatter_fusion = bf16[2,88,2048]{1,0,2:T(2,128)(2,1)S(1)} fusion(bf16[2,88,2048]{1,0,2:T(2,128)(2,1)S(1)} %copy.75, s32[200]{0:T(256)S(1)} %bitcast.77, bf16[200,2,88]{2,1,0:T(2,128)(2,1)S(1)} %bitcast.71), kind=kCustom, calls=%fused_computation.7 | custom fusion | bytes 212000 | tf_op jit(solution)/shard_map/scatter | solution.py:225
  39.9 0.8 copy.76
  40.8 2.0 broadcast_select_fusion
  42.8 1.4 scatter.13.x_ref
  44.2 0.9 copy-done.2
  45.1 39.9 %shard_map.109.k_ref.v_ref = bf16[8,2,96,2048]{3,2,1,0:T(8,128)(2,1)} custom-call(bf16[2,96,2048]{2,1,0:T(8,128)(2,1)} %copy-done.2), custom_call_target="tpu_custom_call" | custom-call | tf_op jit(solution)/shard_map/pallas_call | solution.py:110
  85.3 1.3 copy.87.qs_ref
  86.8 8.4 %copy.77 = bf16[1408,2048]{0,1:T(8,128)(2,1)} copy(bf16[1408,2048]{1,0:T(8,128)(2,1)} %all-gather.4.cloned.1.call-done) | data formatting | bytes 11534336 | tf_op jit(solution)/shard_map/optimization_barrier | solution.py:230
  95.2 4.8 %convert_reduce_fusion = (f32[2048]{0:T(1024)S(1)}, f32[2048]{0:T(1024)S(1)}) fusion(bf16[1408,2048]{0,1:T(8,128)(2,1)} %copy.77), kind=kLoop, calls=%fused_computation.12 | loop fusion | flops 11530240 | bytes 5783552 | tf_op jit(solution)/shard_map/reduce_sum | solution.py:232
  100.0 0.4 copy-done.1
  100.4 2.8 fusion.5
  103.2 0.3 copy.86
  103.5 0.9 pad.12.q_ref
  104.4 1.1 convert_reduce_fusion.2
  106.0 0.9 gather_fusion.4
  107.1 0.9 gather_fusion.5
  108.6 0.7 sort.17
  109.5 0.9 gather_fusion.2
  110.4 0.9 gather_fusion.6
  111.4 0.6 select_select_fusion
  112.1 0.6 gather_fusion.3
  112.7 0.6 fusion.18.kb_map
  113.3 99.8 %shard_map.110 = bf16[2048,96]{1,0:T(8,128)(2,1)} custom-call(s32[4,16]{1,0:T(4,128)} %fusion.18.kb_map, s32[4,16]{1,0:T(4,128)} %get-tuple-element.36.flags, bf16[2048,96]{1,0:T(8,128)(2,1)} %pad.12.q_ref, f32[2048,1]{1,0:T(8,128)} %copy.87.qs_ref, bf16[8,2,96,2048]{3,2,1,0:T(8,128)(2,1)} %shard_map.109.k_ref.v_ref, ...), custom_call_target="tpu_custom_call" | custom-call | tf_op jit(solution)/shard_map/pallas_call | solution.py:177
  213.1 2.0 copy.88
  215.1 9.1 %all-to-all-start.1 = ((bf16[88,16,128]{2,0,1:T(8,128)(2,1)}), bf16[88,16,128]{2,0,1:T(8,128)(2,1)S(1)}, u32[]{:S(2)}, u32[]{:S(2)}) async-start(bf16[88,16,128]{2,0,1:T(8,128)(2,1)} %copy.88), calls=%async_computation.1 | async-start | bytes 720896 | tf_op jit(solution)/shard_map/all_to_all | solution.py:255
  224.3 7.6 %convert_element_type.77 = f32[1408,2048]{0,1:T(8,128)} convert(bf16[1408,2048]{0,1:T(8,128)(2,1)} %copy.77) | non-fusion elementwise | flops 2883584 | bytes 17301504 | tf_op jit(solution)/shard_map/convert_element_type | solution.py:231
  232.0 3.2 %fusion.21 = (f32[128]{0:T(128)S(1)}, f32[128]{0:T(128)S(1)}, f32[1408,128]{0,1:T(8,128)S(1)}) fusion(bf16[1408,128]{1,0:T(8,128)(2,1)S(1)} %bitcast.72, bf16[5,1408,1408]{2,1,0:T(8,128)(2,1)} %all-gather.6.cloned.1.call-done, f32[1408,2048]{0,1:T(8,128)} %convert_element_type.77, s32[]{:T(128)S(6)} %select_n.149), kind=kOutput, calls=%fused_computation.93 | convolution fusion | flops 508231424 | bytes 5768196 | tf_op jit(solution)/shard_map/dot_general | solution.py:257
  235.5 7.5 %fusion.9 = bf16[32,1408]{1,0:T(8,128)(2,1)} fusion(bf16[5,1408,1408]{2,1,0:T(8,128)(2,1)} %all-gather.6.cloned.1.call-done, bf16[1408,32,4]{0,2,1:T(4,128)(2,1)S(1)} %reshape.354), kind=kOutput, calls=%fused_computation.19 | convolution fusion | flops 507555840 | bytes 16310272 | tf_op jit(solution)/shard_map/fgi,ifd->gd/dot_general | solution.py:269
  243.0 0.7 fusion.19
  243.7 0.7 compare_bitcast_fusion
  244.4 41.7 %all-gather.8.cloned.1.call-done = bf16[512,1408]{1,0:T(8,128)(2,1)} async-done(((bf16[32,1408]{1,0:T(8,128)(2,1)}), bf16[512,1408]{1,0:T(8,128)(2,1)}) %all-gather.8.cloned.1.call-update) | async-done | bytes 1441808 | tf_op jit(solution)/shard_map/all_gather | solution.py:270
  286.1 2.5 gather_fusion.1
  288.6 0.8 bitcast_select_fusion
  (72 shorter events, 3.3 us)
Async XLA Ops:
  6.5 26.0 %copy-start = (bf16[2,88,1408]{2,1,0:T(8,128)(2,1)S(1)}, bf16[2,88,1408]{2,1,0:T(8,128)(2,1)}, u32[]{:S(2)}) copy-start(bf16[2,88,1408]{2,1,0:T(8,128)(2,1)} %param.18) | copy-start | bytes 1486852
  6.5 17.9 %copy-start.5 = (s32[2048]{0:T(1024)S(1)}, s32[2048]{0:T(1024)}, u32[]{:S(2)}) copy-start(s32[2048]{0:T(1024)} %param.21) | copy-start | bytes 24580
  6.5 17.9 %copy-start.4 = (bf16[88,1408]{1,0:T(8,128)(2,1)S(1)}, bf16[88,1408]{1,0:T(8,128)(2,1)}, u32[]{:S(2)}) copy-start(bf16[88,1408]{1,0:T(8,128)(2,1)} %param.22) | copy-start | bytes 743428
  6.5 17.9 %copy-start.3 = (bf16[4,88,1408]{2,1,0:T(8,128)(2,1)S(1)}, bf16[4,88,1408]{2,1,0:T(8,128)(2,1)}, u32[]{:S(2)}) copy-start(bf16[4,88,1408]{2,1,0:T(8,128)(2,1)} %param.24) | copy-start | bytes 2973700
  6.5 78.5 %all-gather.4.cloned.1.call-start = ((), (), s32[]{:S(2)}) async-start(), calls=%async_computation.2 | async-start | bytes 6127616 | tf_op jit(solution)/shard_map/all_gather | solution.py:206
  11.9 20.2 %all-to-all-start = ((bf16[16,88,200]{2,1,0:T(8,128)(2,1)}), bf16[16,88,200]{2,1,0:T(8,128)(2,1)S(1)}, u32[]{:S(2)}, u32[]{:S(2)}) async-start(bf16[16,88,200]{2,1,0:T(8,128)(2,1)} %broadcast_in_dim.60), calls=%async_computation | async-start | bytes 1441792 | tf_op jit(solution)/shard_map/all_to_all | solution.py:210
  19.2 212.8 %all-gather.6.cloned.1.call-start = ((), (), s32[]{:S(2)}) async-start(), calls=%async_computation.3 | async-start | bytes 21063680 | tf_op jit(solution)/shard_map/all_gather | solution.py:246
  39.9 45.1 %copy-start.6 = (bf16[1408]{0:T(1024)(128)(2,1)S(1)}, bf16[1408]{0:T(1024)(128)(2,1)}, u32[]{:S(2)}) copy-start(bf16[1408]{0:T(1024)(128)(2,1)} %param.16) | copy-start | bytes 8452
  44.2 0.9 copy-start.2
  86.8 13.2 %copy-start.8 = (bf16[88,1408]{1,0:T(8,128)(2,1)S(1)}, bf16[88,1408]{1,0:T(8,128)(2,1)}, u32[]{:S(2)}) copy-start(bf16[88,1408]{1,0:T(8,128)(2,1)} %param.17) | copy-start | bytes 743428
  95.2 5.2 %copy-start.1 = (bf16[1408,2048]{0,1:T(8,128)(2,1)S(1)}, bf16[1408,2048]{0,1:T(8,128)(2,1)}, u32[]{:S(2)}) copy-start(bf16[1408,2048]{0,1:T(8,128)(2,1)} %copy.77) | copy-start | bytes 17301508
  113.3 111.0 %copy-start.7 = (bf16[1408]{0:T(1024)(128)(2,1)S(1)}, bf16[1408]{0:T(1024)(128)(2,1)}, u32[]{:S(2)}) copy-start(bf16[1408]{0:T(1024)(128)(2,1)} %param.23) | copy-start | bytes 8452
  215.1 16.8 %all-to-all-start.1 = ((bf16[88,16,128]{2,0,1:T(8,128)(2,1)}), bf16[88,16,128]{2,0,1:T(8,128)(2,1)S(1)}, u32[]{:S(2)}, u32[]{:S(2)}) async-start(bf16[88,16,128]{2,0,1:T(8,128)(2,1)} %copy.88), calls=%async_computation.1 | async-start | bytes 720896 | tf_op jit(solution)/shard_map/all_to_all | solution.py:255
  224.2 61.9 %all-gather.8.cloned.1.call-start = ((), (), s32[]{:S(2)}) async-start(), calls=%async_computation.4 | async-start | bytes 1531904 | tf_op jit(solution)/shard_map/all_gather | solution.py:270
Sparse Core Ops, SparseCore 0:
  9.5 63.5 all-gather.3
  85.2 128.3 all-gather.5
  243.1 42.9 all-gather.7

commit v8 on v7

--- a/solution.py
+++ b/solution.py
@@ -122,6 +122,46 @@
             pltpu.SemaphoreType.DMA,
         ],
         compiler_params=pltpu.CompilerParams(collective_id=0, has_side_effects=True),
+    )(x)
+
+
+def _col_gather_kernel(x_ref, o_ref, send_sems, recv_sems, local_sem, *, n_col):
+    mesh_ids = pl.DeviceIdType.MESH
+    me = lax.axis_index("col")
+    row = lax.axis_index("row")
+    barrier = pltpu.get_barrier_semaphore()
+    for k in range(1, n_col):
+        peer = lax.rem(me + k, n_col)
+        pl.semaphore_signal(barrier, inc=1, device_id=(row, peer), device_id_type=mesh_ids)
+    pl.semaphore_wait(barrier, n_col - 1)
+    local = pltpu.make_async_copy(x_ref, o_ref.at[me], local_sem)
+    local.start()
+    copies = []
+    for k in range(1, n_col):
+        peer = lax.rem(me + k, n_col)
+        copy = pltpu.make_async_remote_copy(
+            src_ref=x_ref, dst_ref=o_ref.at[me], send_sem=send_sems.at[k], recv_sem=recv_sems.at[k],
+            device_id=(row, peer), device_id_type=mesh_ids,
+        )
+        copy.start()
+        copies.append(copy)
+    local.wait()
+    for copy in copies:
+        copy.wait()
+
+
+def col_gather(x, n_col):
+    return pl.pallas_call(
+        functools.partial(_col_gather_kernel, n_col=n_col),
+        out_shape=jax.ShapeDtypeStruct((n_col,) + x.shape, x.dtype),
+        in_specs=[pl.BlockSpec(memory_space=pl.ANY)],
+        out_specs=pl.BlockSpec(memory_space=pl.ANY),
+        scratch_shapes=[
+            pltpu.SemaphoreType.DMA((n_col,)),
+            pltpu.SemaphoreType.DMA((n_col,)),
+            pltpu.SemaphoreType.DMA,
+        ],
+        compiler_params=pltpu.CompilerParams(collective_id=1, has_side_effects=True),
     )(x)
 
 
@@ -253,7 +293,7 @@
     attended = attended_rows[:, :HD].T
     chunk = tok_rows // n_col
     attended_chunk = lax.all_to_all(attended, "col", 1, 0, tiled=True)
-    x_chunk = lax.dynamic_slice_in_dim(full_float, col_index * chunk, chunk, 1)
+    x_chunk = lax.dynamic_slice_in_dim(full_rows, col_index * chunk, chunk, 1).astype(jnp.float32)
     projected = lax.dot_general(
         out_weight, attended_chunk, (((0,), (0,)), ((), ())), preferred_element_type=jnp.float32
     )
@@ -267,7 +307,7 @@
     ).astype(jnp.bfloat16)
     grouped = merger_chunk.reshape(model_width, chunk // 4, 4)
     merged_here = jnp.einsum("fgi,ifd->gd", grouped, merge_full, preferred_element_type=jnp.float32)
-    merged_all = lax.all_gather(merged_here.astype(jnp.bfloat16), "col", axis=0, tiled=True)
+    merged_all = col_gather(merged_here.astype(jnp.bfloat16), n_col).reshape(-1, model_width)
     wanted_rows = lax.dynamic_index_in_dim(requests[0], col_index, 0, keepdims=False)
     is_valid = wanted_rows >= 0
     safe_index = jnp.where(is_valid, wanted_rows, 0)

time: 300 us -> 266 us (0.89)
  waiting for transfers between devices: 48.8 us -> 17.1 us
  other arithmetic: 25.7 us -> 17.6 us
  Pallas kernels: 140 us -> 148 us
    all_gather x1 -> x0, waiting for transfers between devices: 41.7 us -> none  [on_device(): lax.all_gather(merged_here.astype(jnp.bfloat16), 'col', axis=0, tiled=True)]
    pallas_call x0 -> x1, Pallas kernels: none -> 25 us  [col_gather(): pl.pallas_call(functools.partial(_col_gather_kernel, n_col=n_col), out_sh...]
    pallas_call x1, Pallas kernels: 99.8 us -> 83.3 us  [attention(): pl.pallas_call(kernel, grid_spec=grid_spec, out_shape=jax.ShapeDtypeStruc...]
    all_gather x1, waiting for transfers between devices: 0.01 us -> 9.89 us  [on_device(): weights_full = lax.all_gather(weight_stack, 'col', axis=1, tiled=True)]
    convert_element_type x1 -> x0, other arithmetic: 7.63 us -> none  [on_device(): full_float = full_rows.astype(jnp.float32)]
  transfers between devices with their start and end apart: 5 -> 4, of which waited for: 2 -> 2; matrix products, arithmetic and copies ran while one was open for 21% -> 20% of each run, Pallas kernels for 47% -> 47%
where the time goes in v8:
time: 266 us; the launch traced here: 263 us
  Pallas kernels  148 us (56%)
  local copies, waits for them, and re-layouts  37.6 us (14%)
  other arithmetic  17.6 us (7%)
  waiting for transfers between devices  17.1 us (6%)
  starting transfers between devices  16.2 us (6%)
  between operations  13.7 us (5%)
  matrix products  13.1 us (5%)
    pallas_call x1, Pallas kernels, attention(): pl.pallas_call(kernel, grid_spec=grid_spec, out_shape=jax.ShapeDtypeStruc...  83.3 us
    pallas_call x1, Pallas kernels, row_gather(): pl.pallas_call(functools.partial(_row_gather_kernel, n_row=n_row), out_sh...  39.8 us
    pallas_call x1, Pallas kernels, col_gather(): pl.pallas_call(functools.partial(_col_gather_kernel, n_col=n_col), out_sh...  25 us
    all_gather x1, waiting for transfers between devices, on_device(): weights_full = lax.all_gather(weight_stack, 'col', axis=1, tiled=True)  9.89 us
    all_to_all x1, starting transfers between devices, on_device(): attended_chunk = lax.all_to_all(attended, 'col', 1, 0, tiled=True)  8.86 us
    optimization_barrier x1, local copies, waits for them, and re-layouts, on_device(): full_rows, pair_all = lax.optimization_barrier((gathered_rows, pair_all))  8.45 us
    scatter x2, local copies, waits for them, and re-layouts, on_device(): keys_values = kv_cache.at[:, :, picked_rows].set(fresh_pairs)  7.64 us
    dot_general x1, matrix products, on_device(): jnp.einsum('fgi,ifd->gd', grouped, merge_full, preferred_element_type=jnp...  7.51 us
  transfers between devices with their start and end apart: 4, of which 2 were waited for; matrix products, arithmetic and copies ran while one was open for 20% of the time, Pallas kernels for 47%

profile of v8, /device:TPU:78, one launch (start us, length us, event | category | flops | bytes accessed | tf_op | source)
XLA Modules:
  0.0 263.4 jit_solution(8563878314290415532)
XLA Ops:
  6.6 0.7 all-gather.3.cloned.1.call-update
  7.3 1.3 copy.72
  8.5 0.7 compare_select_fusion
  9.2 0.8 gather_fusion
  10.0 0.7 compare_and_fusion.2
  10.9 0.9 broadcast_in_dim.60
  11.8 7.3 %all-to-all-start = ((bf16[16,88,200]{2,1,0:T(8,128)(2,1)}), bf16[16,88,200]{2,1,0:T(8,128)(2,1)S(1)}, u32[]{:S(2)}, u32[]{:S(2)}) async-start(bf16[16,88,200]{2,1,0:T(8,128)(2,1)} %broadcast_in_dim.60), calls=%async_computation | async-start | bytes 1441792 | tf_op jit(solution)/shard_map/all_to_all | solution.py:250
  19.2 1.4 and_reduce_fusion
  20.6 0.6 fusion.30
  21.2 0.8 mul.103
  22.0 2.4 copy.75
  24.4 1.2 pad_maximum_fusion
  25.6 6.5 %all-to-all-done = bf16[16,88,200]{2,1,0:T(8,128)(2,1)S(1)} async-done(((bf16[16,88,200]{2,1,0:T(8,128)(2,1)}), bf16[16,88,200]{2,1,0:T(8,128)(2,1)S(1)}, u32[]{:S(2)}, u32[]{:S(2)}) %all-to-all-start) | async-done | bytes 563232 | tf_op jit(solution)/shard_map/all_to_all | solution.py:250
  32.1 0.3 convert_reduce_fusion.1
  32.3 0.3 fusion.21
  32.6 0.3 convolution_convert_fusion
  33.1 6.9 %scatter_fusion = bf16[2,88,2048]{1,0,2:T(2,128)(2,1)S(1)} fusion(bf16[2,88,2048]{1,0,2:T(2,128)(2,1)S(1)} %copy.75, s32[200]{0:T(256)S(1)} %bitcast.79, bf16[200,2,88]{2,1,0:T(2,128)(2,1)S(1)} %bitcast.73), kind=kCustom, calls=%fused_computation.7 | custom fusion | bytes 212000 | tf_op jit(solution)/shard_map/scatter | solution.py:265
  40.0 0.8 copy.76
  40.8 1.9 broadcast_select_fusion
  42.7 1.5 scatter.13.x_ref
  44.3 0.9 copy-done.2
  45.2 39.8 %shard_map.109.k_ref.v_ref = bf16[8,2,96,2048]{3,2,1,0:T(8,128)(2,1)} custom-call(bf16[2,96,2048]{2,1,0:T(8,128)(2,1)} %copy-done.2), custom_call_target="tpu_custom_call" | custom-call | tf_op jit(solution)/shard_map/pallas_call | solution.py:110
  85.2 1.4 copy.87.qs_ref
  86.9 4.4 %convert_reduce_fusion = (f32[2048]{0:T(1024)S(1)}, f32[2048]{0:T(1024)S(1)}) fusion(bf16[1408,2048]{1,0:T(8,128)(2,1)} %all-gather.3.cloned.1.call-done), kind=kLoop, calls=%fused_computation.10 | loop fusion | flops 11530240 | bytes 5783552 | tf_op jit(solution)/shard_map/reduce_sum | solution.py:272
  91.3 2.0 fusion.10
  93.3 0.3 copy.86
  93.6 0.9 pad.12.q_ref
  94.5 1.1 convert_reduce_fusion.2
  96.1 0.9 gather_fusion.4
  97.1 0.9 gather_fusion.5
  98.7 0.7 sort.17
  99.5 0.9 gather_fusion.2
  100.5 0.9 gather_fusion.6
  101.5 0.6 select_select_fusion
  102.2 0.6 gather_fusion.3
  102.8 0.7 fusion.25.kb_map
  103.5 83.3 %shard_map.110 = bf16[2048,96]{1,0:T(8,128)(2,1)} custom-call(s32[4,16]{1,0:T(4,128)} %fusion.25.kb_map, s32[4,16]{1,0:T(4,128)} %get-tuple-element.36.flags, bf16[2048,96]{1,0:T(8,128)(2,1)} %pad.12.q_ref, f32[2048,1]{1,0:T(8,128)} %copy.87.qs_ref, bf16[8,2,96,2048]{3,2,1,0:T(8,128)(2,1)} %shard_map.109.k_ref.v_ref, ...), custom_call_target="tpu_custom_call" | custom-call | tf_op jit(solution)/shard_map/pallas_call | solution.py:217
  186.7 2.0 copy.88
  188.7 8.9 %all-to-all-start.1 = ((bf16[88,16,128]{2,0,1:T(8,128)(2,1)}), bf16[88,16,128]{2,0,1:T(8,128)(2,1)S(1)}, u32[]{:S(2)}, u32[]{:S(2)}) async-start(bf16[88,16,128]{2,0,1:T(8,128)(2,1)} %copy.88), calls=%async_computation.1 | async-start | bytes 720896 | tf_op jit(solution)/shard_map/all_to_all | solution.py:295
  197.6 0.7 fusion.26
  198.3 0.7 compare_bitcast_fusion
  199.0 8.5 %copy.77 = bf16[1408,2048]{0,1:T(8,128)(2,1)} copy(bf16[1408,2048]{1,0:T(8,128)(2,1)} %all-gather.3.cloned.1.call-done) | data formatting | bytes 11534336 | tf_op jit(solution)/shard_map/optimization_barrier | solution.py:270
  207.5 9.9 %all-gather.5.cloned.1.call-done = bf16[5,1408,1408]{2,1,0:T(8,128)(2,1)} async-done(((bf16[5,88,1408]{2,1,0:T(8,128)(2,1)}), bf16[5,1408,1408]{2,1,0:T(8,128)(2,1)}) %all-gather.5.cloned.1.call-update) | async-done | bytes 19824656 | tf_op jit(solution)/shard_map/all_gather | solution.py:286
  217.4 3.1 %fusion.28 = (f32[128]{0:T(128)S(1)}, f32[128]{0:T(128)S(1)}, f32[1408,128]{0,1:T(8,128)S(1)}) fusion(bf16[1408,128]{1,0:T(8,128)(2,1)S(1)} %bitcast.74, bf16[5,1408,1408]{2,1,0:T(8,128)(2,1)} %all-gather.5.cloned.1.call-done, bf16[1408,2048]{0,1:T(8,128)(2,1)} %copy.77, s32[]{:T(128)S(6)} %select_n.149), kind=kOutput, calls=%fused_computation.97 | convolution fusion | flops 508411648 | bytes 5407748 | tf_op jit(solution)/shard_map/dot_general | solution.py:297
  220.8 7.5 %fusion.16.x_ref = bf16[32,1408]{1,0:T(8,128)(2,1)} fusion(bf16[5,1408,1408]{2,1,0:T(8,128)(2,1)} %all-gather.5.cloned.1.call-done, bf16[1408,32,4]{0,2,1:T(4,128)(2,1)S(1)} %reshape.357), kind=kOutput, calls=%fused_computation.23 | convolution fusion | flops 507555840 | bytes 16310272 | tf_op jit(solution)/shard_map/fgi,ifd->gd/dot_general | solution.py:309
  228.3 25.0 %shard_map.111 = bf16[16,32,1408]{2,1,0:T(8,128)(2,1)} custom-call(bf16[32,1408]{1,0:T(8,128)(2,1)} %fusion.16.x_ref), custom_call_target="tpu_custom_call" | custom-call | tf_op jit(solution)/shard_map/pallas_call | solution.py:154
  253.3 2.5 gather_fusion.1
  255.8 0.8 bitcast_select_fusion
  (69 shorter events, 2.9 us)
Async XLA Ops:
  6.5 26.1 %copy-start = (bf16[2,88,1408]{2,1,0:T(8,128)(2,1)S(1)}, bf16[2,88,1408]{2,1,0:T(8,128)(2,1)}, u32[]{:S(2)}) copy-start(bf16[2,88,1408]{2,1,0:T(8,128)(2,1)} %param.18) | copy-start | bytes 1486852
  6.5 17.8 %copy-start.5 = (s32[2048]{0:T(1024)S(1)}, s32[2048]{0:T(1024)}, u32[]{:S(2)}) copy-start(s32[2048]{0:T(1024)} %param.21) | copy-start | bytes 24580
  6.5 17.8 %copy-start.4 = (bf16[88,1408]{1,0:T(8,128)(2,1)S(1)}, bf16[88,1408]{1,0:T(8,128)(2,1)}, u32[]{:S(2)}) copy-start(bf16[88,1408]{1,0:T(8,128)(2,1)} %param.22) | copy-start | bytes 743428
  6.5 17.9 %copy-start.3 = (bf16[4,88,1408]{2,1,0:T(8,128)(2,1)S(1)}, bf16[4,88,1408]{2,1,0:T(8,128)(2,1)}, u32[]{:S(2)}) copy-start(bf16[4,88,1408]{2,1,0:T(8,128)(2,1)} %param.24) | copy-start | bytes 2973700
  6.5 78.4 %all-gather.3.cloned.1.call-start = ((), (), s32[]{:S(2)}) async-start(), calls=%async_computation.2 | async-start | bytes 6127616 | tf_op jit(solution)/shard_map/all_gather | solution.py:246
  11.8 20.2 %all-to-all-start = ((bf16[16,88,200]{2,1,0:T(8,128)(2,1)}), bf16[16,88,200]{2,1,0:T(8,128)(2,1)S(1)}, u32[]{:S(2)}, u32[]{:S(2)}) async-start(bf16[16,88,200]{2,1,0:T(8,128)(2,1)} %broadcast_in_dim.60), calls=%async_computation | async-start | bytes 1441792 | tf_op jit(solution)/shard_map/all_to_all | solution.py:250
  19.1 198.2 %all-gather.5.cloned.1.call-start = ((), (), s32[]{:S(2)}) async-start(), calls=%async_computation.3 | async-start | bytes 21063680 | tf_op jit(solution)/shard_map/all_gather | solution.py:286
  39.9 45.0 %copy-start.6 = (bf16[1408]{0:T(1024)(128)(2,1)S(1)}, bf16[1408]{0:T(1024)(128)(2,1)}, u32[]{:S(2)}) copy-start(bf16[1408]{0:T(1024)(128)(2,1)} %param.16) | copy-start | bytes 8452
  44.3 0.9 copy-start.2
  84.9 6.3 %copy-start.8 = (bf16[88,1408]{1,0:T(8,128)(2,1)S(1)}, bf16[88,1408]{1,0:T(8,128)(2,1)}, u32[]{:S(2)}) copy-start(bf16[88,1408]{1,0:T(8,128)(2,1)} %param.17) | copy-start | bytes 743428
  86.6 4.6 %copy-start.1 = (bf16[1408,2048]{1,0:T(8,128)(2,1)S(1)}, bf16[1408,2048]{1,0:T(8,128)(2,1)}, u32[]{:S(2)}) copy-start(bf16[1408,2048]{1,0:T(8,128)(2,1)} %all-gather.3.cloned.1.call-done) | copy-start | bytes 17301508
  103.5 94.1 %copy-start.7 = (bf16[1408]{0:T(1024)(128)(2,1)S(1)}, bf16[1408]{0:T(1024)(128)(2,1)}, u32[]{:S(2)}) copy-start(bf16[1408]{0:T(1024)(128)(2,1)} %param.23) | copy-start | bytes 8452
  188.7 18.7 %all-to-all-start.1 = ((bf16[88,16,128]{2,0,1:T(8,128)(2,1)}), bf16[88,16,128]{2,0,1:T(8,128)(2,1)S(1)}, u32[]{:S(2)}, u32[]{:S(2)}) async-start(bf16[88,16,128]{2,0,1:T(8,128)(2,1)} %copy.88), calls=%async_computation.1 | async-start | bytes 720896 | tf_op jit(solution)/shard_map/all_to_all | solution.py:295
Sparse Core Ops, SparseCore 0:
  9.5 63.5 all-gather.2
  85.1 132.2 all-gather.4

commit v9 on v8

--- a/solution.py
+++ b/solution.py
@@ -12,8 +12,8 @@
 EPSILON = 1e-06
 MASKED = -1e30
 PADW = 96
-Q_BLOCK = 512
-K_BLOCK = 1024
+Q_BLOCK = 1024
+K_BLOCK = 2048
 
 
 def _attn_kernel(kb_map, flags, q_ref, qs_ref, k_ref, v_ref, o_ref, m_ref, l_ref, acc_ref, *, scale, n_steps):

time: 266 us -> 266 us (level)
  waiting for transfers between devices: 17.1 us -> 43.9 us
  Pallas kernels: 148 us -> 122 us
    all_gather x1, waiting for transfers between devices: 9.89 us -> 36.7 us  [on_device(): weights_full = lax.all_gather(weight_stack, 'col', axis=1, tiled=True)]
    pallas_call x1, Pallas kernels: 83.3 us -> 57.1 us  [attention(): pl.pallas_call(kernel, grid_spec=grid_spec, out_shape=jax.ShapeDtypeStruc...]
  transfers between devices with their start and end apart: 4 -> 4, of which waited for: 2 -> 2; matrix products, arithmetic and copies ran while one was open for 20% -> 20% of each run, Pallas kernels for 47% -> 37%
where the time goes in v9:
time: 266 us; the launch traced here: 263 us
  Pallas kernels  122 us (46%)
  waiting for transfers between devices  43.9 us (17%)
  local copies, waits for them, and re-layouts  36.8 us (14%)
  other arithmetic  17.6 us (7%)
  starting transfers between devices  16.1 us (6%)
  between operations  13.8 us (5%)
  matrix products  13.1 us (5%)
    pallas_call x1, Pallas kernels, attention(): pl.pallas_call(kernel, grid_spec=grid_spec, out_shape=jax.ShapeDtypeStruc...  57.1 us
    pallas_call x1, Pallas kernels, row_gather(): pl.pallas_call(functools.partial(_row_gather_kernel, n_row=n_row), out_sh...  39.8 us
    all_gather x1, waiting for transfers between devices, on_device(): weights_full = lax.all_gather(weight_stack, 'col', axis=1, tiled=True)  36.7 us
    pallas_call x1, Pallas kernels, col_gather(): pl.pallas_call(functools.partial(_col_gather_kernel, n_col=n_col), out_sh...  25 us
    all_to_all x1, starting transfers between devices, on_device(): attended_chunk = lax.all_to_all(attended, 'col', 1, 0, tiled=True)  8.75 us
    optimization_barrier x1, local copies, waits for them, and re-layouts, on_device(): full_rows, pair_all = lax.optimization_barrier((gathered_rows, pair_all))  8.51 us
    scatter x2, local copies, waits for them, and re-layouts, on_device(): keys_values = kv_cache.at[:, :, picked_rows].set(fresh_pairs)  7.64 us
    dot_general x1, matrix products, on_device(): jnp.einsum('fgi,ifd->gd', grouped, merge_full, preferred_element_type=jnp...  7.51 us
  transfers between devices with their start and end apart: 4, of which 2 were waited for; matrix products, arithmetic and copies ran while one was open for 20% of the time, Pallas kernels for 37%

profile of v9, /device:TPU:78, one launch (start us, length us, event | category | flops | bytes accessed | tf_op | source)
XLA Modules:
  0.0 263.2 jit_solution(17741690032913603715)
XLA Ops:
  6.6 0.7 all-gather.3.cloned.1.call-update
  7.3 1.3 copy.75
  8.5 0.7 compare_select_fusion
  9.2 0.8 gather_fusion
  10.0 0.7 compare_and_fusion.2
  10.9 0.9 broadcast_in_dim.53
  11.8 7.3 %all-to-all-start = ((bf16[16,88,200]{2,1,0:T(8,128)(2,1)}), bf16[16,88,200]{2,1,0:T(8,128)(2,1)S(1)}, u32[]{:S(2)}, u32[]{:S(2)}) async-start(bf16[16,88,200]{2,1,0:T(8,128)(2,1)} %broadcast_in_dim.53), calls=%async_computation | async-start | bytes 1441792 | tf_op jit(solution)/shard_map/all_to_all | solution.py:250
  19.2 1.4 and_reduce_fusion
  20.6 0.6 fusion.31
  21.2 0.8 mul.103
  22.0 2.4 copy.78
  24.4 1.2 pad_maximum_fusion
  25.6 6.5 %all-to-all-done = bf16[16,88,200]{2,1,0:T(8,128)(2,1)S(1)} async-done(((bf16[16,88,200]{2,1,0:T(8,128)(2,1)}), bf16[16,88,200]{2,1,0:T(8,128)(2,1)S(1)}, u32[]{:S(2)}, u32[]{:S(2)}) %all-to-all-start) | async-done | bytes 563232 | tf_op jit(solution)/shard_map/all_to_all | solution.py:250
  32.1 0.3 convert_reduce_fusion.1
  32.3 0.3 fusion.21
  32.6 0.3 convolution_convert_fusion
  33.1 6.9 %scatter_fusion = bf16[2,88,2048]{1,0,2:T(2,128)(2,1)S(1)} fusion(bf16[2,88,2048]{1,0,2:T(2,128)(2,1)S(1)} %copy.78, s32[200]{0:T(256)S(1)} %bitcast.80, bf16[200,2,88]{2,1,0:T(2,128)(2,1)S(1)} %bitcast.73), kind=kCustom, calls=%fused_computation.7 | custom fusion | bytes 212000 | tf_op jit(solution)/shard_map/scatter | solution.py:265
  40.0 0.8 copy.79
  40.8 1.9 broadcast_select_fusion
  42.7 1.4 scatter.13.x_ref
  44.1 0.9 copy-done.2
  45.0 39.8 %shard_map.109.k_ref.v_ref = bf16[8,2,96,2048]{3,2,1,0:T(8,128)(2,1)} custom-call(bf16[2,96,2048]{2,1,0:T(8,128)(2,1)} %copy-done.2), custom_call_target="tpu_custom_call" | custom-call | tf_op jit(solution)/shard_map/pallas_call | solution.py:110
  85.0 1.4 copy.90.qs_ref
  86.8 4.4 %convert_reduce_fusion = (f32[2048]{0:T(1024)S(1)}, f32[2048]{0:T(1024)S(1)}) fusion(bf16[1408,2048]{1,0:T(8,128)(2,1)} %all-gather.3.cloned.1.call-done), kind=kLoop, calls=%fused_computation.10 | loop fusion | flops 11530240 | bytes 5783552 | tf_op jit(solution)/shard_map/reduce_sum | solution.py:272
  91.2 2.0 fusion.10
  93.2 0.3 copy.89
  93.5 0.9 pad.12.q_ref
  94.4 1.0 slice_convert_fusion
  95.8 0.7 gather_fusion.4
  96.7 0.7 gather_fusion.5
  98.0 0.7 sort.17
  98.8 0.7 gather_fusion.2
  99.6 0.7 gather_fusion.6
  100.7 0.6 fusion.24
  101.3 0.6 gather_fusion.3
  102.0 0.7 fusion.26.kb_map
  102.6 57.1 %shard_map.110 = bf16[2048,96]{1,0:T(8,128)(2,1)} custom-call(s32[2,8]{1,0:T(2,128)} %fusion.26.kb_map, s32[2,8]{1,0:T(2,128)} %get-tuple-element.36.flags, bf16[2048,96]{1,0:T(8,128)(2,1)} %pad.12.q_ref, f32[2048,1]{1,0:T(8,128)} %copy.90.qs_ref, bf16[8,2,96,2048]{3,2,1,0:T(8,128)(2,1)} %shard_map.109.k_ref.v_ref, ...), custom_call_target="tpu_custom_call" | custom-call | tf_op jit(solution)/shard_map/pallas_call | solution.py:217
  159.7 2.0 copy.91
  161.7 8.8 %all-to-all-start.1 = ((bf16[88,16,128]{2,0,1:T(8,128)(2,1)}), bf16[88,16,128]{2,0,1:T(8,128)(2,1)S(1)}, u32[]{:S(2)}, u32[]{:S(2)}) async-start(bf16[88,16,128]{2,0,1:T(8,128)(2,1)} %copy.91), calls=%async_computation.1 | async-start | bytes 720896 | tf_op jit(solution)/shard_map/all_to_all | solution.py:295
  170.5 0.7 fusion.27
  171.2 0.7 compare_bitcast_fusion
  171.9 8.5 %copy.80 = bf16[1408,2048]{0,1:T(8,128)(2,1)} copy(bf16[1408,2048]{1,0:T(8,128)(2,1)} %all-gather.3.cloned.1.call-done) | data formatting | bytes 11534336 | tf_op jit(solution)/shard_map/optimization_barrier | solution.py:270
  180.4 36.7 %all-gather.5.cloned.1.call-done = bf16[5,1408,1408]{2,1,0:T(8,128)(2,1)} async-done(((bf16[5,88,1408]{2,1,0:T(8,128)(2,1)}), bf16[5,1408,1408]{2,1,0:T(8,128)(2,1)}) %all-gather.5.cloned.1.call-update) | async-done | bytes 19824656 | tf_op jit(solution)/shard_map/all_gather | solution.py:286
  217.1 3.1 %fusion.29 = (f32[128]{0:T(128)S(1)}, f32[128]{0:T(128)S(1)}, f32[1408,128]{0,1:T(8,128)S(1)}) fusion(bf16[1408,128]{1,0:T(8,128)(2,1)S(1)} %bitcast.74, bf16[5,1408,1408]{2,1,0:T(8,128)(2,1)} %all-gather.5.cloned.1.call-done, bf16[1408,2048]{0,1:T(8,128)(2,1)} %copy.80, s32[]{:T(128)S(6)} %select_n.149), kind=kOutput, calls=%fused_computation.99 | convolution fusion | flops 508411648 | bytes 5407748 | tf_op jit(solution)/shard_map/dot_general | solution.py:297
  220.5 7.5 %fusion.16.x_ref = bf16[32,1408]{1,0:T(8,128)(2,1)} fusion(bf16[5,1408,1408]{2,1,0:T(8,128)(2,1)} %all-gather.5.cloned.1.call-done, bf16[1408,32,4]{0,2,1:T(4,128)(2,1)S(1)} %reshape.357), kind=kOutput, calls=%fused_computation.23 | convolution fusion | flops 507555840 | bytes 16310272 | tf_op jit(solution)/shard_map/fgi,ifd->gd/dot_general | solution.py:309
  228.0 25.0 %shard_map.111 = bf16[16,32,1408]{2,1,0:T(8,128)(2,1)} custom-call(bf16[32,1408]{1,0:T(8,128)(2,1)} %fusion.16.x_ref), custom_call_target="tpu_custom_call" | custom-call | tf_op jit(solution)/shard_map/pallas_call | solution.py:154
  253.0 2.5 gather_fusion.1
  255.6 0.8 bitcast_select_fusion
  (70 shorter events, 3.2 us)
Async XLA Ops:
  6.5 26.1 %copy-start = (bf16[2,88,1408]{2,1,0:T(8,128)(2,1)S(1)}, bf16[2,88,1408]{2,1,0:T(8,128)(2,1)}, u32[]{:S(2)}) copy-start(bf16[2,88,1408]{2,1,0:T(8,128)(2,1)} %param.18) | copy-start | bytes 1486852
  6.5 17.8 %copy-start.5 = (s32[2048]{0:T(1024)S(1)}, s32[2048]{0:T(1024)}, u32[]{:S(2)}) copy-start(s32[2048]{0:T(1024)} %param.21) | copy-start | bytes 24580
  6.5 17.8 %copy-start.4 = (bf16[88,1408]{1,0:T(8,128)(2,1)S(1)}, bf16[88,1408]{1,0:T(8,128)(2,1)}, u32[]{:S(2)}) copy-start(bf16[88,1408]{1,0:T(8,128)(2,1)} %param.22) | copy-start | bytes 743428
  6.5 17.9 %copy-start.3 = (bf16[4,88,1408]{2,1,0:T(8,128)(2,1)S(1)}, bf16[4,88,1408]{2,1,0:T(8,128)(2,1)}, u32[]{:S(2)}) copy-start(bf16[4,88,1408]{2,1,0:T(8,128)(2,1)} %param.24) | copy-start | bytes 2973700
  6.5 78.2 %all-gather.3.cloned.1.call-start = ((), (), s32[]{:S(2)}) async-start(), calls=%async_computation.2 | async-start | bytes 6127616 | tf_op jit(solution)/shard_map/all_gather | solution.py:246
  11.8 20.2 %all-to-all-start = ((bf16[16,88,200]{2,1,0:T(8,128)(2,1)}), bf16[16,88,200]{2,1,0:T(8,128)(2,1)S(1)}, u32[]{:S(2)}, u32[]{:S(2)}) async-start(bf16[16,88,200]{2,1,0:T(8,128)(2,1)} %broadcast_in_dim.53), calls=%async_computation | async-start | bytes 1441792 | tf_op jit(solution)/shard_map/all_to_all | solution.py:250
  19.1 198.0 %all-gather.5.cloned.1.call-start = ((), (), s32[]{:S(2)}) async-start(), calls=%async_computation.3 | async-start | bytes 21063680 | tf_op jit(solution)/shard_map/all_gather | solution.py:286
  39.9 44.9 %copy-start.6 = (bf16[1408]{0:T(1024)(128)(2,1)S(1)}, bf16[1408]{0:T(1024)(128)(2,1)}, u32[]{:S(2)}) copy-start(bf16[1408]{0:T(1024)(128)(2,1)} %param.16) | copy-start | bytes 8452
  44.1 0.9 copy-start.2
  84.8 6.4 %copy-start.8 = (bf16[88,1408]{1,0:T(8,128)(2,1)S(1)}, bf16[88,1408]{1,0:T(8,128)(2,1)}, u32[]{:S(2)}) copy-start(bf16[88,1408]{1,0:T(8,128)(2,1)} %param.17) | copy-start | bytes 743428
  86.4 4.7 %copy-start.1 = (bf16[1408,2048]{1,0:T(8,128)(2,1)S(1)}, bf16[1408,2048]{1,0:T(8,128)(2,1)}, u32[]{:S(2)}) copy-start(bf16[1408,2048]{1,0:T(8,128)(2,1)} %all-gather.3.cloned.1.call-done) | copy-start | bytes 17301508
  102.6 67.8 %copy-start.7 = (bf16[1408]{0:T(1024)(128)(2,1)S(1)}, bf16[1408]{0:T(1024)(128)(2,1)}, u32[]{:S(2)}) copy-start(bf16[1408]{0:T(1024)(128)(2,1)} %param.23) | copy-start | bytes 8452
  161.7 18.7 %all-to-all-start.1 = ((bf16[88,16,128]{2,0,1:T(8,128)(2,1)}), bf16[88,16,128]{2,0,1:T(8,128)(2,1)S(1)}, u32[]{:S(2)}, u32[]{:S(2)}) async-start(bf16[88,16,128]{2,0,1:T(8,128)(2,1)} %copy.91), calls=%async_computation.1 | async-start | bytes 720896 | tf_op jit(solution)/shard_map/all_to_all | solution.py:295
Sparse Core Ops, SparseCore 0:
  9.5 63.5 all-gather.2
  84.9 132.1 all-gather.4

commit v10 on v9

--- a/solution.py
+++ b/solution.py
@@ -282,7 +282,7 @@
     query_rows = jnp.pad(query_rows, ((0, 0), (0, PADW - HD)))
     segment_line = pair_all[:, 0, HD].reshape(-1).astype(jnp.int32)
     weight_stack = jnp.concatenate([w_out[None], w_merge], axis=0)
-    weight_stack, _ = lax.optimization_barrier((weight_stack, full_rows))
+    weight_stack, _ = lax.optimization_barrier((weight_stack, picked_full))
     weights_full = lax.all_gather(weight_stack, "col", axis=1, tiled=True)
     out_weight = weights_full[0]
     merge_full = weights_full[1:]

time: 266 us -> 254 us (0.955)
  waiting for transfers between devices: 43.9 us -> 34.4 us
    all_gather x1, waiting for transfers between devices: 36.7 us -> 23.2 us  [on_device(): weights_full = lax.all_gather(weight_stack, 'col', axis=1, tiled=True)]
    all_to_all x1, waiting for transfers between devices: 6.48 us -> 10.4 us  [on_device(): picked_full = lax.all_to_all(picked_copies, 'col', 0, 0, tiled=True)]
  transfers between devices with their start and end apart: 4 -> 4, of which waited for: 2 -> 2; matrix products, arithmetic and copies ran while one was open for 20% -> 20% of each run, Pallas kernels for 37% -> 38%
where the time goes in v10:
time: 254 us; the launch traced here: 252 us
  Pallas kernels  121 us (48%)
  local copies, waits for them, and re-layouts  34.6 us (14%)
  waiting for transfers between devices  34.4 us (14%)
  other arithmetic  18.3 us (7%)
  starting transfers between devices  16.3 us (6%)
  between operations  13.7 us (5%)
  matrix products  13.1 us (5%)
    pallas_call x1, Pallas kernels, attention(): pl.pallas_call(kernel, grid_spec=grid_spec, out_shape=jax.ShapeDtypeStruc...  56.6 us
    pallas_call x1, Pallas kernels, row_gather(): pl.pallas_call(functools.partial(_row_gather_kernel, n_row=n_row), out_sh...  39.8 us
    pallas_call x1, Pallas kernels, col_gather(): pl.pallas_call(functools.partial(_col_gather_kernel, n_col=n_col), out_sh...  25 us
    all_gather x1, waiting for transfers between devices, on_device(): weights_full = lax.all_gather(weight_stack, 'col', axis=1, tiled=True)  23.2 us
    all_to_all x1, waiting for transfers between devices, on_device(): picked_full = lax.all_to_all(picked_copies, 'col', 0, 0, tiled=True)  10.4 us
    all_to_all x1, starting transfers between devices, on_device(): attended_chunk = lax.all_to_all(attended, 'col', 1, 0, tiled=True)  8.94 us
    optimization_barrier x1, local copies, waits for them, and re-layouts, on_device(): full_rows, pair_all = lax.optimization_barrier((gathered_rows, pair_all))  8.47 us
    scatter x2, local copies, waits for them, and re-layouts, on_device(): keys_values = kv_cache.at[:, :, picked_rows].set(fresh_pairs)  7.64 us
  transfers between devices with their start and end apart: 4, of which 2 were waited for; matrix products, arithmetic and copies ran while one was open for 20% of the time, Pallas kernels for 38%

profile of v10, /device:TPU:78, one launch (start us, length us, event | category | flops | bytes accessed | tf_op | source)
XLA Modules:
  0.0 251.8 jit_solution(1071301289946228476)
XLA Ops:
  6.6 0.7 all-gather.3.cloned.1.call-update
  7.3 1.3 copy.75
  8.6 0.7 compare_select_fusion
  9.3 0.8 gather_fusion
  10.1 0.7 compare_and_fusion.2
  10.9 0.9 broadcast_in_dim.53
  11.8 7.3 %all-to-all-start = ((bf16[16,88,200]{2,1,0:T(8,128)(2,1)}), bf16[16,88,200]{2,1,0:T(8,128)(2,1)S(1)}, u32[]{:S(2)}, u32[]{:S(2)}) async-start(bf16[16,88,200]{2,1,0:T(8,128)(2,1)} %broadcast_in_dim.53), calls=%async_computation | async-start | bytes 1441792 | tf_op jit(solution)/shard_map/all_to_all | solution.py:250
  19.2 2.5 pad_maximum_fusion
  21.7 10.4 %all-to-all-done = bf16[16,88,200]{2,1,0:T(8,128)(2,1)S(1)} async-done(((bf16[16,88,200]{2,1,0:T(8,128)(2,1)}), bf16[16,88,200]{2,1,0:T(8,128)(2,1)S(1)}, u32[]{:S(2)}, u32[]{:S(2)}) %all-to-all-start) | async-done | bytes 563232 | tf_op jit(solution)/shard_map/all_to_all | solution.py:250
  32.3 0.8 copy.78
  33.3 1.4 copy.90.qs_ref
  35.0 0.7 fusion.31
  35.6 0.7 and_reduce_fusion
  36.4 0.3 convert_reduce_fusion.1
  36.6 0.3 fusion.21
  36.9 0.3 convolution_convert_fusion
  37.4 6.9 %scatter_fusion = bf16[2,88,2048]{1,0,2:T(2,128)(2,1)S(1)} fusion(bf16[2,88,2048]{1,0,2:T(2,128)(2,1)S(1)} %copy.78, s32[200]{0:T(256)S(1)} %bitcast.80, bf16[200,2,88]{2,1,0:T(2,128)(2,1)S(1)} %bitcast.73), kind=kCustom, calls=%fused_computation.7 | custom fusion | bytes 212000 | tf_op jit(solution)/shard_map/scatter | solution.py:265
  44.2 0.8 copy.79
  45.1 1.9 broadcast_select_fusion
  47.0 1.4 scatter.13.x_ref
  48.4 0.9 copy-done.2
  49.3 39.8 %shard_map.109.k_ref.v_ref = bf16[8,2,96,2048]{3,2,1,0:T(8,128)(2,1)} custom-call(bf16[2,96,2048]{2,1,0:T(8,128)(2,1)} %copy-done.2), custom_call_target="tpu_custom_call" | custom-call | tf_op jit(solution)/shard_map/pallas_call | solution.py:110
  89.1 4.4 %convert_reduce_fusion = (f32[2048]{0:T(1024)S(1)}, f32[2048]{0:T(1024)S(1)}) fusion(bf16[1408,2048]{1,0:T(8,128)(2,1)} %all-gather.3.cloned.1.call-done), kind=kLoop, calls=%fused_computation.10 | loop fusion | flops 11530240 | bytes 5783552 | tf_op jit(solution)/shard_map/reduce_sum | solution.py:272
  93.5 2.0 fusion.10
  95.6 0.3 copy.89
  95.9 0.9 pad.12.q_ref
  96.8 1.0 slice_convert_fusion
  97.8 0.2 compare_reduce_fusion
  98.2 0.7 gather_fusion.4
  99.1 0.7 gather_fusion.5
  100.4 0.7 sort.17
  101.2 0.7 gather_fusion.2
  102.0 0.7 gather_fusion.6
  103.1 0.6 fusion.24
  103.7 0.6 gather_fusion.3
  104.4 0.7 fusion.26.kb_map
  105.0 56.6 %shard_map.110 = bf16[2048,96]{1,0:T(8,128)(2,1)} custom-call(s32[2,8]{1,0:T(2,128)} %fusion.26.kb_map, s32[2,8]{1,0:T(2,128)} %get-tuple-element.36.flags, bf16[2048,96]{1,0:T(8,128)(2,1)} %pad.12.q_ref, f32[2048,1]{1,0:T(8,128)} %copy.90.qs_ref, bf16[8,2,96,2048]{3,2,1,0:T(8,128)(2,1)} %shard_map.109.k_ref.v_ref, ...), custom_call_target="tpu_custom_call" | custom-call | tf_op jit(solution)/shard_map/pallas_call | solution.py:217
  161.6 2.0 copy.91
  163.6 8.9 %all-to-all-start.1 = ((bf16[88,16,128]{2,0,1:T(8,128)(2,1)}), bf16[88,16,128]{2,0,1:T(8,128)(2,1)S(1)}, u32[]{:S(2)}, u32[]{:S(2)}) async-start(bf16[88,16,128]{2,0,1:T(8,128)(2,1)} %copy.91), calls=%async_computation.1 | async-start | bytes 720896 | tf_op jit(solution)/shard_map/all_to_all | solution.py:295
  172.6 0.7 fusion.27
  173.3 0.7 compare_bitcast_fusion
  174.0 8.5 %copy.80 = bf16[1408,2048]{0,1:T(8,128)(2,1)} copy(bf16[1408,2048]{1,0:T(8,128)(2,1)} %all-gather.3.cloned.1.call-done) | data formatting | bytes 11534336 | tf_op jit(solution)/shard_map/optimization_barrier | solution.py:270
  182.5 23.2 %all-gather.5.cloned.1.call-done = bf16[5,1408,1408]{2,1,0:T(8,128)(2,1)} async-done(((bf16[5,88,1408]{2,1,0:T(8,128)(2,1)}), bf16[5,1408,1408]{2,1,0:T(8,128)(2,1)}) %all-gather.5.cloned.1.call-update) | async-done | bytes 19824656 | tf_op jit(solution)/shard_map/all_gather | solution.py:286
  205.7 3.1 %fusion.29 = (f32[128]{0:T(128)S(1)}, f32[128]{0:T(128)S(1)}, f32[1408,128]{0,1:T(8,128)S(1)}) fusion(bf16[1408,128]{1,0:T(8,128)(2,1)S(1)} %bitcast.74, bf16[5,1408,1408]{2,1,0:T(8,128)(2,1)} %all-gather.5.cloned.1.call-done, bf16[1408,2048]{0,1:T(8,128)(2,1)} %copy.80, s32[]{:T(128)S(6)} %select_n.149), kind=kOutput, calls=%fused_computation.99 | convolution fusion | flops 508411648 | bytes 5407748 | tf_op jit(solution)/shard_map/dot_general | solution.py:297
  209.1 7.5 %fusion.16.x_ref = bf16[32,1408]{1,0:T(8,128)(2,1)} fusion(bf16[5,1408,1408]{2,1,0:T(8,128)(2,1)} %all-gather.5.cloned.1.call-done, bf16[1408,32,4]{0,2,1:T(4,128)(2,1)S(1)} %reshape.357), kind=kOutput, calls=%fused_computation.23 | convolution fusion | flops 507555840 | bytes 16310272 | tf_op jit(solution)/shard_map/fgi,ifd->gd/dot_general | solution.py:309
  216.6 25.0 %shard_map.111 = bf16[16,32,1408]{2,1,0:T(8,128)(2,1)} custom-call(bf16[32,1408]{1,0:T(8,128)(2,1)} %fusion.16.x_ref), custom_call_target="tpu_custom_call" | custom-call | tf_op jit(solution)/shard_map/pallas_call | solution.py:154
  241.6 2.5 %gather_fusion.1 = bf16[85,1408]{1,0:T(8,128)(2,1)S(1)} fusion(bf16[512,1408]{1,0:T(8,128)(2,1)} %bitcast.70, s32[1024]{0:T(1024)S(1)} %pad_clamp_fusion), kind=kCustom, calls=%fused_computation.4 | custom fusion | bytes 479060 | tf_op jit(solution)/shard_map/gather | solution.py:314
  244.2 0.8 bitcast_select_fusion
  (70 shorter events, 3.1 us)
Async XLA Ops:
  6.5 30.4 %copy-start = (bf16[2,88,1408]{2,1,0:T(8,128)(2,1)S(1)}, bf16[2,88,1408]{2,1,0:T(8,128)(2,1)}, u32[]{:S(2)}) copy-start(bf16[2,88,1408]{2,1,0:T(8,128)(2,1)} %param.18) | copy-start | bytes 1486852
  6.5 29.1 %copy-start.7 = (s32[3]{0:T(128)S(1)}, s32[3]{0:T(128)}, u32[]{:S(2)}) copy-start(s32[3]{0:T(128)} %constant.154.clone.1) | copy-start | bytes 40
  6.5 25.6 %copy-start.5 = (bf16[1408]{0:T(1024)(128)(2,1)S(1)}, bf16[1408]{0:T(1024)(128)(2,1)}, u32[]{:S(2)}) copy-start(bf16[1408]{0:T(1024)(128)(2,1)} %param.16) | copy-start | bytes 8452
  6.5 25.7 %copy-start.3 = (bf16[2,88,2048]{2,1,0:T(8,128)(2,1)S(1)}, bf16[2,88,2048]{2,1,0:T(8,128)(2,1)}, u32[]{:S(2)}) copy-start(bf16[2,88,2048]{2,1,0:T(8,128)(2,1)} %param.19) | copy-start | bytes 2162692
  6.5 26.5 %copy-start.4 = (s32[2048]{0:T(1024)S(1)}, s32[2048]{0:T(1024)}, u32[]{:S(2)}) copy-start(s32[2048]{0:T(1024)} %param.21) | copy-start | bytes 24580
  6.5 82.6 %all-gather.3.cloned.1.call-start = ((), (), s32[]{:S(2)}) async-start(), calls=%async_computation.2 | async-start | bytes 6127616 | tf_op jit(solution)/shard_map/all_gather | solution.py:246
  11.8 20.3 %all-to-all-start = ((bf16[16,88,200]{2,1,0:T(8,128)(2,1)}), bf16[16,88,200]{2,1,0:T(8,128)(2,1)S(1)}, u32[]{:S(2)}, u32[]{:S(2)}) async-start(bf16[16,88,200]{2,1,0:T(8,128)(2,1)} %broadcast_in_dim.53), calls=%async_computation | async-start | bytes 1441792 | tf_op jit(solution)/shard_map/all_to_all | solution.py:250
  19.2 186.6 %all-gather.5.cloned.1.call-start = ((), (), s32[]{:S(2)}) async-start(), calls=%async_computation.3 | async-start | bytes 21063680 | tf_op jit(solution)/shard_map/all_gather | solution.py:286
  48.4 0.9 copy-start.2
  49.3 44.2 %copy-start.8 = (bf16[88,1408]{1,0:T(8,128)(2,1)S(1)}, bf16[88,1408]{1,0:T(8,128)(2,1)}, u32[]{:S(2)}) copy-start(bf16[88,1408]{1,0:T(8,128)(2,1)} %param.17) | copy-start | bytes 743428
  89.1 4.4 %copy-start.1 = (bf16[1408,2048]{1,0:T(8,128)(2,1)S(1)}, bf16[1408,2048]{1,0:T(8,128)(2,1)}, u32[]{:S(2)}) copy-start(bf16[1408,2048]{1,0:T(8,128)(2,1)} %all-gather.3.cloned.1.call-done) | copy-start | bytes 17301508
  105.0 67.5 %copy-start.6 = (bf16[1408]{0:T(1024)(128)(2,1)S(1)}, bf16[1408]{0:T(1024)(128)(2,1)}, u32[]{:S(2)}) copy-start(bf16[1408]{0:T(1024)(128)(2,1)} %param.23) | copy-start | bytes 8452
  163.6 18.8 %all-to-all-start.1 = ((bf16[88,16,128]{2,0,1:T(8,128)(2,1)}), bf16[88,16,128]{2,0,1:T(8,128)(2,1)S(1)}, u32[]{:S(2)}, u32[]{:S(2)}) async-start(bf16[88,16,128]{2,0,1:T(8,128)(2,1)} %copy.91), calls=%async_computation.1 | async-start | bytes 720896 | tf_op jit(solution)/shard_map/all_to_all | solution.py:295
Sparse Core Ops, SparseCore 0:
  9.5 63.5 all-gather.2
  75.3 130.3 all-gather.4

commit v11 on v10

--- a/solution.py
+++ b/solution.py
@@ -150,7 +150,7 @@
         copy.wait()
 
 
-def col_gather(x, n_col):
+def col_gather(x, n_col, kernel_id):
     return pl.pallas_call(
         functools.partial(_col_gather_kernel, n_col=n_col),
         out_shape=jax.ShapeDtypeStruct((n_col,) + x.shape, x.dtype),
@@ -161,7 +161,7 @@
             pltpu.SemaphoreType.DMA((n_col,)),
             pltpu.SemaphoreType.DMA,
         ],
-        compiler_params=pltpu.CompilerParams(collective_id=1, has_side_effects=True),
+        compiler_params=pltpu.CompilerParams(collective_id=kernel_id, has_side_effects=True),
     )(x)
 
 
@@ -243,31 +243,7 @@
     heads_here = local_width // HD
     score_scale = HD ** (-0.5)
     col_index = lax.axis_index("col")
-    gathered_rows = lax.all_gather(hidden, "col", axis=0, tiled=True)
-    picked_rows = recompute_rows[0]
-    hidden_picked = jnp.take(hidden, picked_rows, axis=1)
-    picked_copies = jnp.broadcast_to(hidden_picked[None], (n_col,) + hidden_picked.shape)
-    picked_full = lax.all_to_all(picked_copies, "col", 0, 0, tiled=True)
-    picked_float = picked_full.reshape(model_width, -1).astype(jnp.float32)
-    picked_mean = jnp.sum(picked_float, axis=0, keepdims=True) / model_width
-    picked_square = jnp.sum(picked_float * picked_float, axis=0, keepdims=True) / model_width
-    normed_picked = (
-        (picked_float - picked_mean)
-        * lax.rsqrt(picked_square - picked_mean * picked_mean + EPSILON)
-        * gain_in.astype(jnp.float32)[:, None]
-    ).astype(jnp.bfloat16)
-    fresh_pairs = jnp.dot(
-        w_pair.reshape(2 * local_width, model_width),
-        normed_picked,
-        preferred_element_type=jnp.float32,
-    )
-    fresh_pairs = fresh_pairs.astype(jnp.bfloat16).reshape(2, local_width, -1)
-    keys_values = kv_cache.at[:, :, picked_rows].set(fresh_pairs)
-
-    pair_local = jnp.pad(keys_values, ((0, 0), (0, PADW - HD), (0, 0)))
-    pair_local = pair_local.at[0, HD].set(segment_ids.astype(jnp.bfloat16))
-    pair_all = row_gather(pair_local, n_row)
-    full_rows, pair_all = lax.optimization_barrier((gathered_rows, pair_all))
+    full_rows = col_gather(hidden, n_col, 2).reshape(model_width, tok_rows)
     full_float = full_rows.astype(jnp.float32)
     in_mean = jnp.sum(full_float, axis=0, keepdims=True) / model_width
     in_square = jnp.sum(full_float * full_float, axis=0, keepdims=True) / model_width
@@ -280,9 +256,21 @@
         normed, w_query, (((0,), (1,)), ((), ())), preferred_element_type=jnp.float32
     ).astype(jnp.bfloat16)
     query_rows = jnp.pad(query_rows, ((0, 0), (0, PADW - HD)))
+    picked_rows = recompute_rows[0]
+    normed_picked = jnp.take(normed, picked_rows, axis=1)
+    fresh_pairs = jnp.dot(
+        w_pair.reshape(2 * local_width, model_width),
+        normed_picked,
+        preferred_element_type=jnp.float32,
+    )
+    fresh_pairs = fresh_pairs.astype(jnp.bfloat16).reshape(2, local_width, -1)
+    keys_values = kv_cache.at[:, :, picked_rows].set(fresh_pairs)
+
+    pair_local = jnp.pad(keys_values, ((0, 0), (0, PADW - HD), (0, 0)))
+    pair_local = pair_local.at[0, HD].set(segment_ids.astype(jnp.bfloat16))
+    pair_all = row_gather(pair_local, n_row)
     segment_line = pair_all[:, 0, HD].reshape(-1).astype(jnp.int32)
     weight_stack = jnp.concatenate([w_out[None], w_merge], axis=0)
-    weight_stack, _ = lax.optimization_barrier((weight_stack, picked_full))
     weights_full = lax.all_gather(weight_stack, "col", axis=1, tiled=True)
     out_weight = weights_full[0]
     merge_full = weights_full[1:]
@@ -307,7 +295,7 @@
     ).astype(jnp.bfloat16)
     grouped = merger_chunk.reshape(model_width, chunk // 4, 4)
     merged_here = jnp.einsum("fgi,ifd->gd", grouped, merge_full, preferred_element_type=jnp.float32)
-    merged_all = col_gather(merged_here.astype(jnp.bfloat16), n_col).reshape(-1, model_width)
+    merged_all = col_gather(merged_here.astype(jnp.bfloat16), n_col, 1).reshape(-1, model_width)
     wanted_rows = lax.dynamic_index_in_dim(requests[0], col_index, 0, keepdims=False)
     is_valid = wanted_rows >= 0
     safe_index = jnp.where(is_valid, wanted_rows, 0)

time: 254 us -> 331 us (1.30)
  the two profiles are of different devices: /device:TPU:78 before, /device:TPU:14 now
where the time goes in v11:
time: 331 us; the launch traced here: 330 us
  Pallas kernels  226 us (68%)
  local copies, waits for them, and re-layouts  36.9 us (11%)
  other arithmetic  20.2 us (6%)
  matrix products  15.8 us (5%)
  between operations  13.7 us (4%)
  starting transfers between devices  11.4 us (3%)
  waiting for transfers between devices  5.39 us (2%)
    pallas_call x2, Pallas kernels, col_gather(): pl.pallas_call(functools.partial(_col_gather_kernel, n_col=n_col), out_sh...  126 us
    pallas_call x1, Pallas kernels, attention(): pl.pallas_call(kernel, grid_spec=grid_spec, out_shape=jax.ShapeDtypeStruc...  56.4 us
    pallas_call x1, Pallas kernels, row_gather(): pl.pallas_call(functools.partial(_row_gather_kernel, n_row=n_row), out_sh...  43.7 us
    all_to_all x1, starting transfers between devices, on_device(): attended_chunk = lax.all_to_all(attended, 'col', 1, 0, tiled=True)  11.4 us
    reshape x1, local copies, waits for them, and re-layouts, on_device(): full_rows = col_gather(hidden, n_col, 2).reshape(model_width, tok_rows)  8.39 us
    scatter x2, local copies, waits for them, and re-layouts, on_device(): keys_values = kv_cache.at[:, :, picked_rows].set(fresh_pairs)  7.64 us
    dot_general x1, matrix products, on_device(): jnp.einsum('fgi,ifd->gd', grouped, merge_full, preferred_element_type=jnp...  7.51 us
  transfers between devices with their start and end apart: 2, of which 1 were waited for; matrix products, arithmetic and copies ran while one was open for 17% of the time, Pallas kernels for 61%

profile of v11, /device:TPU:14, one launch (start us, length us, event | category | flops | bytes accessed | tf_op | source)
XLA Modules:
  0.0 329.8 jit_solution(41254593290226964)
XLA Ops:
  6.5 2.5 pad_maximum_fusion
  9.0 101.1 %shard_map.109 = bf16[16,88,2048]{2,1,0:T(8,128)(2,1)} custom-call(bf16[88,2048]{1,0:T(8,128)(2,1)} %x_ref.1), custom_call_target="tpu_custom_call" | custom-call | tf_op jit(solution)/shard_map/pallas_call | solution.py:154
  110.2 8.4 %copy.54 = bf16[1408,2048]{0,1:T(8,128)(2,1)} copy(bf16[1408,2048]{1,0:T(8,128)(2,1)} %bitcast.68) | data formatting | bytes 11534336 | tf_op jit(solution)/shard_map/reshape | solution.py:246
  118.6 4.4 %convert_reduce_fusion = (f32[2048]{0:T(1024)S(1)}, f32[2048]{0:T(1024)S(1)}) fusion(bf16[16,88,2048]{2,1,0:T(8,128)(2,1)} %shard_map.109), kind=kLoop, calls=%fused_computation.11 | loop fusion | flops 11530240 | bytes 5783552 | tf_op jit(solution)/shard_map/reduce_sum | solution.py:248
  123.0 4.0 %multiply_convert_fusion = bf16[1408,2048]{0,1:T(8,128)(2,1)} fusion(bf16[1408,2048]{0,1:T(8,128)(2,1)S(1)} %copy-done.1, f32[1408]{0:T(1024)S(1)} %convert_element_type.67, f32[2048]{0:T(1024)S(1)} %get-tuple-element.27, f32[2048]{0:T(1024)S(1)} %get-tuple-element.26), kind=kLoop, calls=%fused_computation.13 | loop fusion | flops 14417920 | bytes 11556352 | tf_op jit(solution)/shard_map/convert_element_type | solution.py:254
  127.0 5.5 %gather_fusion = bf16[200,1408]{1,0:T(8,128)(2,1)S(1)} fusion(bf16[1408,2048]{0,1:T(8,128)(2,1)} %multiply_convert_fusion, s32[1024]{0:T(1024)S(1)} %pad_clamp_fusion.1), kind=kCustom, calls=%fused_computation.3 | custom fusion | bytes 1127200 | tf_op jit(solution)/shard_map/jit(_take)/gather | solution.py:260
  132.5 0.4 convolution_convert_fusion.1
  133.1 0.8 copy.57
  133.8 6.9 %scatter_fusion = bf16[2,88,2048]{1,0,2:T(2,128)(2,1)S(1)} fusion(bf16[2,88,2048]{1,0,2:T(2,128)(2,1)S(1)} %copy.57, s32[200]{0:T(256)S(1)} %bitcast.78, bf16[200,2,88]{2,1,0:T(2,128)(2,1)S(1)} %bitcast.71), kind=kCustom, calls=%fused_computation.7 | custom fusion | bytes 212000 | tf_op jit(solution)/shard_map/scatter | solution.py:267
  140.7 0.8 copy.58
  141.6 0.7 fusion.23
  142.3 0.7 and_reduce_fusion
  143.0 1.9 broadcast_select_fusion
  144.9 1.5 scatter.13.x_ref
  146.5 0.9 copy-done.2
  147.3 43.7 %shard_map.110.k_ref.v_ref = bf16[8,2,96,2048]{3,2,1,0:T(8,128)(2,1)} custom-call(bf16[2,96,2048]{2,1,0:T(8,128)(2,1)} %copy-done.2), custom_call_target="tpu_custom_call" | custom-call | tf_op jit(solution)/shard_map/pallas_call | solution.py:110
  191.1 1.0 slice_convert_fusion
  192.3 0.2 compare_reduce_fusion.1
  192.5 0.2 compare_reduce_fusion
  192.8 0.1 convolution_compare_fusion
  192.9 0.7 gather_fusion.4
  193.7 0.1 convert_reduce_fusion.2
  193.9 0.7 gather_fusion.5
  194.7 0.2 reduce_window_sum.11
  194.9 0.2 convert_reduce_fusion.3
  195.2 0.7 sort.17
  196.1 0.7 gather_fusion.2
  196.8 0.7 gather_fusion.6
  197.7 4.7 %convolution_convert_fusion = bf16[2048,88]{0,1:T(8,128)(2,1)S(1)} fusion(bf16[1408,2048]{0,1:T(8,128)(2,1)} %multiply_convert_fusion, bf16[88,1408]{1,0:T(8,128)(2,1)S(1)} %copy-done.4), kind=kOutput, calls=%fused_computation.17 | convolution fusion | flops 507691008 | bytes 6375424 | tf_op jit(solution)/shard_map/dot_general | solution.py:255
  202.4 0.3 copy.67
  202.7 0.9 pad.12.q_ref
  203.6 1.4 copy.68.qs_ref
  205.0 0.2 or_reduce_fusion
  205.2 0.6 fusion.15
  205.8 0.6 gather_fusion.3
  206.4 0.6 fusion.17.kb_map
  207.0 56.4 %shard_map.111 = bf16[2048,96]{1,0:T(8,128)(2,1)} custom-call(s32[2,8]{1,0:T(2,128)} %fusion.17.kb_map, s32[2,8]{1,0:T(2,128)} %get-tuple-element.28.flags, bf16[2048,96]{1,0:T(8,128)(2,1)} %pad.12.q_ref, f32[2048,1]{1,0:T(8,128)} %copy.68.qs_ref, bf16[8,2,96,2048]{3,2,1,0:T(8,128)(2,1)} %shard_map.110.k_ref.v_ref, ...), custom_call_target="tpu_custom_call" | custom-call | tf_op jit(solution)/shard_map/pallas_call | solution.py:217
  263.4 2.0 copy.69
  265.4 11.4 %all-to-all-start = ((bf16[88,16,128]{2,0,1:T(8,128)(2,1)}), bf16[88,16,128]{2,0,1:T(8,128)(2,1)S(1)}, u32[]{:S(2)}, u32[]{:S(2)}) async-start(bf16[88,16,128]{2,0,1:T(8,128)(2,1)} %copy.69), calls=%async_computation | async-start | bytes 720896 | tf_op jit(solution)/shard_map/all_to_all | solution.py:283
  276.9 0.7 fusion.18
  277.6 0.7 compare_bitcast_fusion
  278.3 5.4 %all-to-all-done = bf16[88,16,128]{2,0,1:T(8,128)(2,1)S(1)} async-done(((bf16[88,16,128]{2,0,1:T(8,128)(2,1)}), bf16[88,16,128]{2,0,1:T(8,128)(2,1)S(1)}, u32[]{:S(2)}, u32[]{:S(2)}) %all-to-all-start) | async-done | bytes 360480 | tf_op jit(solution)/shard_map/all_to_all | solution.py:283
  283.7 3.1 fusion.21
  286.8 0.2 multiply_convert_fusion.1
  287.1 7.5 %fusion.8.x_ref = bf16[32,1408]{1,0:T(8,128)(2,1)} fusion(bf16[5,1408,1408]{2,1,0:T(8,128)(2,1)} %all-gather.2.cloned.1.call-done, bf16[1408,32,4]{0,2,1:T(4,128)(2,1)S(1)} %reshape.310), kind=kOutput, calls=%fused_computation.19 | convolution fusion | flops 507555840 | bytes 16310272 | tf_op jit(solution)/shard_map/fgi,ifd->gd/dot_general | solution.py:297
  294.6 25.1 %shard_map.112 = bf16[16,32,1408]{2,1,0:T(8,128)(2,1)} custom-call(bf16[32,1408]{1,0:T(8,128)(2,1)} %fusion.8.x_ref), custom_call_target="tpu_custom_call" | custom-call | tf_op jit(solution)/shard_map/pallas_call | solution.py:154
  319.7 2.5 gather_fusion.1
  322.2 0.8 bitcast_select_fusion
  (61 shorter events, 1.5 us)
Async XLA Ops:
  6.5 125.9 %copy-start = (bf16[2,88,1408]{2,1,0:T(8,128)(2,1)S(1)}, bf16[2,88,1408]{2,1,0:T(8,128)(2,1)}, u32[]{:S(2)}) copy-start(bf16[2,88,1408]{2,1,0:T(8,128)(2,1)} %param.18) | copy-start | bytes 1486852
  6.5 277.1 %all-gather.2.cloned.1.call-start = ((), (), s32[]{:S(2)}) async-start(), calls=%async_computation.1 | async-start | bytes 21063680 | tf_op jit(solution)/shard_map/all_gather | solution.py:274
  110.1 8.4 %copy-start.6 = (bf16[1408]{0:T(1024)(128)(2,1)S(1)}, bf16[1408]{0:T(1024)(128)(2,1)}, u32[]{:S(2)}) copy-start(bf16[1408]{0:T(1024)(128)(2,1)} %param.16) | copy-start | bytes 8452
  110.2 8.4 %copy-start.8 = (s32[1,200]{1,0:T(1,128)S(1)}, s32[1,200]{1,0:T(1,128)}, u32[]{:S(2)}) copy-start(s32[1,200]{1,0:T(1,128)} %param.20) | copy-start | bytes 2404
  118.6 4.4 %copy-start.1 = (bf16[1408,2048]{0,1:T(8,128)(2,1)S(1)}, bf16[1408,2048]{0,1:T(8,128)(2,1)}, u32[]{:S(2)}) copy-start(bf16[1408,2048]{0,1:T(8,128)(2,1)} %copy.54) | copy-start | bytes 17301508
  127.0 6.1 %copy-start.3 = (bf16[2,88,2048]{2,1,0:T(8,128)(2,1)S(1)}, bf16[2,88,2048]{2,1,0:T(8,128)(2,1)}, u32[]{:S(2)}) copy-start(bf16[2,88,2048]{2,1,0:T(8,128)(2,1)} %param.19) | copy-start | bytes 2162692
  127.0 14.5 %copy-start.5 = (s32[2048]{0:T(1024)S(1)}, s32[2048]{0:T(1024)}, u32[]{:S(2)}) copy-start(s32[2048]{0:T(1024)} %param.21) | copy-start | bytes 24580
  127.0 15.3 %copy-start.9 = (s32[3]{0:T(128)S(1)}, s32[3]{0:T(128)}, u32[]{:S(2)}) copy-start(s32[3]{0:T(128)} %constant.153.clone.1) | copy-start | bytes 40
  141.6 56.1 %copy-start.4 = (bf16[88,1408]{1,0:T(8,128)(2,1)S(1)}, bf16[88,1408]{1,0:T(8,128)(2,1)}, u32[]{:S(2)}) copy-start(bf16[88,1408]{1,0:T(8,128)(2,1)} %param.17) | copy-start | bytes 743428
  146.5 0.9 copy-start.2
  207.0 69.8 %copy-start.7 = (bf16[1408]{0:T(1024)(128)(2,1)S(1)}, bf16[1408]{0:T(1024)(128)(2,1)}, u32[]{:S(2)}) copy-start(bf16[1408]{0:T(1024)(128)(2,1)} %param.23) | copy-start | bytes 8452
  265.4 18.2 %all-to-all-start = ((bf16[88,16,128]{2,0,1:T(8,128)(2,1)}), bf16[88,16,128]{2,0,1:T(8,128)(2,1)S(1)}, u32[]{:S(2)}, u32[]{:S(2)}) async-start(bf16[88,16,128]{2,0,1:T(8,128)(2,1)} %copy.69), calls=%async_computation | async-start | bytes 720896 | tf_op jit(solution)/shard_map/all_to_all | solution.py:283
Sparse Core Ops, SparseCore 0:
  9.6 197.5 all-gather.1

commit v12 on v10

--- a/solution.py
+++ b/solution.py
@@ -282,10 +282,10 @@
     query_rows = jnp.pad(query_rows, ((0, 0), (0, PADW - HD)))
     segment_line = pair_all[:, 0, HD].reshape(-1).astype(jnp.int32)
     weight_stack = jnp.concatenate([w_out[None], w_merge], axis=0)
-    weight_stack, _ = lax.optimization_barrier((weight_stack, picked_full))
-    weights_full = lax.all_gather(weight_stack, "col", axis=1, tiled=True)
-    out_weight = weights_full[0]
-    merge_full = weights_full[1:]
+    weight_copies = jnp.broadcast_to(weight_stack[None], (n_col,) + weight_stack.shape)
+    weights_full = lax.all_to_all(weight_copies, "col", 0, 0, tiled=True)
+    out_weight = weights_full[:, 0].reshape(model_width, model_width)
+    merge_parts = weights_full[:, 1:]
     kb_map, flags = block_tables(segment_ids, segment_line, lax.axis_index("row") * tok_rows)
     attended_rows = attention(
         query_rows, segment_ids.astype(jnp.float32)[:, None], pair_all, kb_map, flags, score_scale
@@ -305,8 +305,8 @@
         * lax.rsqrt(row_square - row_mean * row_mean + EPSILON)
         * gain_merge.astype(jnp.float32)[:, None]
     ).astype(jnp.bfloat16)
-    grouped = merger_chunk.reshape(model_width, chunk // 4, 4)
-    merged_here = jnp.einsum("fgi,ifd->gd", grouped, merge_full, preferred_element_type=jnp.float32)
+    grouped = merger_chunk.reshape(n_col, local_width, chunk // 4, 4)
+    merged_here = jnp.einsum("cfgi,cifd->gd", grouped, merge_parts, preferred_element_type=jnp.float32)
     merged_all = col_gather(merged_here.astype(jnp.bfloat16), n_col).reshape(-1, model_width)
     wanted_rows = lax.dynamic_index_in_dim(requests[0], col_index, 0, keepdims=False)
     is_valid = wanted_rows >= 0

time: 254 us -> 484 us (1.91); the launches traced: 252 us -> 476 us
  waiting for transfers between devices: 34.4 us -> 243 us
  starting transfers between devices: 16.3 us -> 36.1 us
  Pallas kernels: 121 us -> 114 us
    all_gather x1, waiting for transfers between devices: 0.02 us -> 233 us  [on_device(): gathered_rows = lax.all_gather(hidden, 'col', axis=0, tiled=True)]
    all_gather x1 -> x0, waiting for transfers between devices: 23.2 us -> none  [on_device(): weights_full = lax.all_gather(weight_stack, 'col', axis=1, tiled=True)]
    all_to_all x1, starting transfers between devices: 8.94 us -> 20.2 us  [on_device(): attended_chunk = lax.all_to_all(attended, 'col', 1, 0, tiled=True)]
    all_to_all x0 -> x1, starting transfers between devices: none -> 8.62 us  [on_device(): weights_full = lax.all_to_all(weight_copies, 'col', 0, 0, tiled=True)]
    optimization_barrier x1 -> x0, local copies, waits for them, and re-layouts: 8.47 us -> none  [on_device(): full_rows, pair_all = lax.optimization_barrier((gathered_rows, pair_all))]
    pallas_call x1, Pallas kernels: 25 us -> 17.7 us  [col_gather(): pl.pallas_call(functools.partial(_col_gather_kernel, n_col=n_col), out_sh...]
    broadcast_in_dim x0 -> x1, local copies, waits for them, and re-layouts: none -> 6.86 us  [on_device(): jnp.broadcast_to(weight_stack[None], (n_col,) + weight_stack.shape)]
  transfers between devices with their start and end apart: 4 -> 4, of which waited for: 2 -> 2; matrix products, arithmetic and copies ran while one was open for 20% -> 9% of each run, Pallas kernels for 38% -> 20%
where the time goes in v12:
time: 484 us; the launch traced here: 476 us
  waiting for transfers between devices  243 us (50%)
  Pallas kernels  114 us (24%)
  local copies, waits for them, and re-layouts  38.3 us (8%)
  starting transfers between devices  36.1 us (7%)
  other arithmetic  17.2 us (4%)
  matrix products  13.7 us (3%)
  between operations  13.7 us (3%)
    all_gather x1, waiting for transfers between devices, on_device(): gathered_rows = lax.all_gather(hidden, 'col', axis=0, tiled=True)  233 us
    pallas_call x1, Pallas kernels, attention(): pl.pallas_call(kernel, grid_spec=grid_spec, out_shape=jax.ShapeDtypeStruc...  56.6 us
    pallas_call x1, Pallas kernels, row_gather(): pl.pallas_call(functools.partial(_row_gather_kernel, n_row=n_row), out_sh...  39.9 us
    all_to_all x1, starting transfers between devices, on_device(): attended_chunk = lax.all_to_all(attended, 'col', 1, 0, tiled=True)  20.2 us
    pallas_call x1, Pallas kernels, col_gather(): pl.pallas_call(functools.partial(_col_gather_kernel, n_col=n_col), out_sh...  17.7 us
  transfers between devices with their start and end apart: 4, of which 2 were waited for; matrix products, arithmetic and copies ran while one was open for 9% of the time, Pallas kernels for 20%

profile of v12, /device:TPU:78, one launch (start us, length us, event | category | flops | bytes accessed | tf_op | source)
XLA Modules:
  0.0 475.9 jit_solution(7101633860663693487)
XLA Ops:
  6.5 0.7 compare_select_fusion
  7.3 1.3 copy.56
  8.6 0.7 compare_and_fusion.2
  9.2 0.8 gather_fusion
  10.2 0.9 broadcast_in_dim.54
  11.1 7.3 %all-to-all-start = ((bf16[16,88,200]{2,1,0:T(8,128)(2,1)}), bf16[16,88,200]{2,1,0:T(8,128)(2,1)S(1)}, u32[]{:S(2)}, u32[]{:S(2)}) async-start(bf16[16,88,200]{2,1,0:T(8,128)(2,1)} %broadcast_in_dim.54), calls=%async_computation | async-start | bytes 1441792 | tf_op jit(solution)/shard_map/all_to_all | solution.py:250
  18.5 1.4 pad_maximum_fusion
  19.8 9.0 %all-to-all-done = bf16[16,88,200]{2,1,0:T(8,128)(2,1)S(1)} async-done(((bf16[16,88,200]{2,1,0:T(8,128)(2,1)}), bf16[16,88,200]{2,1,0:T(8,128)(2,1)S(1)}, u32[]{:S(2)}, u32[]{:S(2)}) %all-to-all-start) | async-done | bytes 563232 | tf_op jit(solution)/shard_map/all_to_all | solution.py:250
  28.8 6.9 %broadcast_in_dim.57 = bf16[16,5,88,1408]{3,2,1,0:T(8,128)(2,1)} broadcast(bf16[5,88,1408]{2,1,0:T(8,128)(2,1)S(1)} %pad_maximum_fusion), dimensions={1,2,3} | broadcast | bytes 21063680 | tf_op jit(solution)/shard_map/broadcast_in_dim | solution.py:285
  35.7 8.6 %all-to-all-start.1 = ((bf16[16,5,88,1408]{3,2,1,0:T(8,128)(2,1)}), bf16[16,5,88,1408]{3,2,1,0:T(8,128)(2,1)}, u32[]{:S(2)}, u32[]{:S(2)}) async-start(bf16[16,5,88,1408]{3,2,1,0:T(8,128)(2,1)} %broadcast_in_dim.57), calls=%async_computation.1 | async-start | bytes 39649280 | tf_op jit(solution)/shard_map/all_to_all | solution.py:286
  44.4 0.7 all-gather.2.cloned.1.call-update
  45.2 0.8 copy.59
  46.2 1.4 copy.70.qs_ref
  47.9 0.6 fusion.29
  48.5 0.7 and_reduce_fusion
  49.7 0.3 convolution_convert_fusion
  50.2 6.9 %scatter_fusion = bf16[2,88,2048]{1,0,2:T(2,128)(2,1)S(1)} fusion(bf16[2,88,2048]{1,0,2:T(2,128)(2,1)S(1)} %copy.59, s32[200]{0:T(256)S(1)} %bitcast.78, bf16[200,2,88]{2,1,0:T(2,128)(2,1)S(1)} %bitcast.71), kind=kCustom, calls=%fused_computation.7 | custom fusion | bytes 212000 | tf_op jit(solution)/shard_map/scatter | solution.py:265
  57.1 0.8 copy.60
  57.9 1.9 broadcast_select_fusion
  59.8 1.3 scatter.13.x_ref
  61.1 0.9 copy-done.3
  62.0 39.9 %shard_map.109.k_ref.v_ref = bf16[8,2,96,2048]{3,2,1,0:T(8,128)(2,1)} custom-call(bf16[2,96,2048]{2,1,0:T(8,128)(2,1)} %copy-done.3), custom_call_target="tpu_custom_call" | custom-call | tf_op jit(solution)/shard_map/pallas_call | solution.py:110
  101.9 232.9 %all-gather.2.cloned.1.call-done = bf16[1408,2048]{1,0:T(8,128)(2,1)} async-done(((bf16[88,2048]{1,0:T(8,128)(2,1)}), bf16[1408,2048]{1,0:T(8,128)(2,1)}) %all-gather.2.cloned.1.call-update) | async-done | bytes 5767184 | tf_op jit(solution)/shard_map/all_gather | solution.py:246
  334.8 1.0 slice_convert_fusion
  336.1 0.7 gather_fusion.5
  337.0 0.7 gather_fusion.4
  338.4 0.7 sort.17
  339.2 0.7 gather_fusion.6
  340.0 0.7 gather_fusion.2
  340.9 4.4 convert_reduce_fusion
  345.3 2.0 fusion.8
  347.3 0.3 copy.69
  347.6 0.9 pad.12.q_ref
  348.7 0.6 fusion.22
  349.3 0.6 gather_fusion.3
  350.0 0.7 fusion.24.kb_map
  350.6 56.6 %shard_map.110 = bf16[2048,96]{1,0:T(8,128)(2,1)} custom-call(s32[2,8]{1,0:T(2,128)} %fusion.24.kb_map, s32[2,8]{1,0:T(2,128)} %get-tuple-element.34.flags, bf16[2048,96]{1,0:T(8,128)(2,1)} %pad.12.q_ref, f32[2048,1]{1,0:T(8,128)} %copy.70.qs_ref, bf16[8,2,96,2048]{3,2,1,0:T(8,128)(2,1)} %shard_map.109.k_ref.v_ref, ...), custom_call_target="tpu_custom_call" | custom-call | tf_op jit(solution)/shard_map/pallas_call | solution.py:217
  407.2 2.0 copy.71
  409.2 20.2 %all-to-all-start.2 = ((bf16[88,16,128]{2,0,1:T(8,128)(2,1)}), bf16[88,16,128]{2,0,1:T(8,128)(2,1)S(1)}, u32[]{:S(2)}, u32[]{:S(2)}) async-start(bf16[88,16,128]{2,0,1:T(8,128)(2,1)} %copy.71), calls=%async_computation.2 | async-start | bytes 720896 | tf_op jit(solution)/shard_map/all_to_all | solution.py:295
  429.4 0.7 fusion.25
  430.1 0.7 compare_bitcast_fusion
  430.8 4.4 slice.57
  435.2 3.4 fusion.27
  439.1 1.1 reshape.358
  440.2 7.8 %fusion.14.x_ref = bf16[32,1408]{1,0:T(8,128)(2,1)} fusion(bf16[16,5,88,1408]{3,2,1,0:T(8,128)(2,1)} %all-to-all-done.1, bf16[16,88,32,4]{1,0,3,2:T(8,128)(2,1)S(1)} %reshape.358), kind=kOutput, calls=%fused_computation.21 | convolution fusion | flops 507555840 | bytes 16310272 | tf_op jit(solution)/shard_map/cfgi,cifd->gd/dot_general | solution.py:309
  448.0 17.7 %shard_map.111 = bf16[16,32,1408]{2,1,0:T(8,128)(2,1)} custom-call(bf16[32,1408]{1,0:T(8,128)(2,1)} %fusion.14.x_ref), custom_call_target="tpu_custom_call" | custom-call | tf_op jit(solution)/shard_map/pallas_call | solution.py:154
  465.7 2.5 gather_fusion.1
  468.3 0.8 bitcast_select_fusion
  (73 shorter events, 4.0 us)
Async XLA Ops:
  6.5 43.2 %copy-start = (bf16[2,88,1408]{2,1,0:T(8,128)(2,1)S(1)}, bf16[2,88,1408]{2,1,0:T(8,128)(2,1)}, u32[]{:S(2)}) copy-start(bf16[2,88,1408]{2,1,0:T(8,128)(2,1)} %param.18) | copy-start | bytes 1486852
  11.1 17.7 %all-to-all-start = ((bf16[16,88,200]{2,1,0:T(8,128)(2,1)}), bf16[16,88,200]{2,1,0:T(8,128)(2,1)S(1)}, u32[]{:S(2)}, u32[]{:S(2)}) async-start(bf16[16,88,200]{2,1,0:T(8,128)(2,1)} %broadcast_in_dim.54), calls=%async_computation | async-start | bytes 1441792 | tf_op jit(solution)/shard_map/all_to_all | solution.py:250
  35.7 9.4 %copy-start.6 = (bf16[1408]{0:T(1024)(128)(2,1)S(1)}, bf16[1408]{0:T(1024)(128)(2,1)}, u32[]{:S(2)}) copy-start(bf16[1408]{0:T(1024)(128)(2,1)} %param.16) | copy-start | bytes 8452
  35.7 9.5 %copy-start.4 = (bf16[2,88,2048]{2,1,0:T(8,128)(2,1)S(1)}, bf16[2,88,2048]{2,1,0:T(8,128)(2,1)}, u32[]{:S(2)}) copy-start(bf16[2,88,2048]{2,1,0:T(8,128)(2,1)} %param.19) | copy-start | bytes 2162692
  35.7 10.3 %copy-start.5 = (s32[2048]{0:T(1024)S(1)}, s32[2048]{0:T(1024)}, u32[]{:S(2)}) copy-start(s32[2048]{0:T(1024)} %param.21) | copy-start | bytes 24580
  35.7 12.8 %copy-start.8 = (s32[3]{0:T(128)S(1)}, s32[3]{0:T(128)}, u32[]{:S(2)}) copy-start(s32[3]{0:T(128)} %constant.154.clone.1) | copy-start | bytes 40
  35.7 373.5 %all-to-all-start.1 = ((bf16[16,5,88,1408]{3,2,1,0:T(8,128)(2,1)}), bf16[16,5,88,1408]{3,2,1,0:T(8,128)(2,1)}, u32[]{:S(2)}, u32[]{:S(2)}) async-start(bf16[16,5,88,1408]{3,2,1,0:T(8,128)(2,1)} %broadcast_in_dim.57), calls=%async_computation.1 | async-start | bytes 39649280 | tf_op jit(solution)/shard_map/all_to_all | solution.py:286
  44.3 290.4 %all-gather.2.cloned.1.call-start = ((), (), s32[]{:S(2)}) async-start(), calls=%async_computation.3 | async-start | bytes 6127616 | tf_op jit(solution)/shard_map/all_gather | solution.py:246
  61.1 0.9 copy-start.3
  101.8 243.4 %copy-start.9 = (bf16[88,1408]{1,0:T(8,128)(2,1)S(1)}, bf16[88,1408]{1,0:T(8,128)(2,1)}, u32[]{:S(2)}) copy-start(bf16[88,1408]{1,0:T(8,128)(2,1)} %param.17) | copy-start | bytes 743428
  340.9 4.4 copy-start.2
  350.6 78.8 %copy-start.7 = (bf16[1408]{0:T(1024)(128)(2,1)S(1)}, bf16[1408]{0:T(1024)(128)(2,1)}, u32[]{:S(2)}) copy-start(bf16[1408]{0:T(1024)(128)(2,1)} %param.23) | copy-start | bytes 8452
  409.2 26.0 %all-to-all-start.2 = ((bf16[88,16,128]{2,0,1:T(8,128)(2,1)}), bf16[88,16,128]{2,0,1:T(8,128)(2,1)S(1)}, u32[]{:S(2)}, u32[]{:S(2)}) async-start(bf16[88,16,128]{2,0,1:T(8,128)(2,1)} %copy.71), calls=%async_computation.2 | async-start | bytes 720896 | tf_op jit(solution)/shard_map/all_to_all | solution.py:295
  440.2 28.8 %copy-start.1 = (bf16[2,88,1408]{2,1,0:T(8,128)(2,1)S(1)}, bf16[2,88,1408]{2,1,0:T(8,128)(2,1)}, u32[]{:S(2)}) copy-start(bf16[2,88,1408]{2,1,0:T(8,128)(2,1)} %param.18) | copy-start | bytes 1486852
Sparse Core Ops, SparseCore 0:
  47.3 287.4 all-gather.1

commit v13 on v10

--- a/solution.py
+++ b/solution.py
@@ -281,21 +281,37 @@
     ).astype(jnp.bfloat16)
     query_rows = jnp.pad(query_rows, ((0, 0), (0, PADW - HD)))
     segment_line = pair_all[:, 0, HD].reshape(-1).astype(jnp.int32)
+    half = model_width // 2
+    core = lax.axis_index("row") % 2
     weight_stack = jnp.concatenate([w_out[None], w_merge], axis=0)
-    weight_stack, _ = lax.optimization_barrier((weight_stack, picked_full))
-    weights_full = lax.all_gather(weight_stack, "col", axis=1, tiled=True)
-    out_weight = weights_full[0]
-    merge_full = weights_full[1:]
+    weight_half = lax.dynamic_slice_in_dim(weight_stack, core * half, half, 2)
+    weight_half, _ = lax.optimization_barrier((weight_half, full_rows))
+    weights_mine = lax.all_gather(weight_half, "col", axis=1, tiled=True)
+
+    def in_order(mine, other, axis):
+        return jnp.where(
+            core == 0,
+            jnp.concatenate([mine, other], axis=axis),
+            jnp.concatenate([other, mine], axis=axis),
+        )
     kb_map, flags = block_tables(segment_ids, segment_line, lax.axis_index("row") * tok_rows)
     attended_rows = attention(
         query_rows, segment_ids.astype(jnp.float32)[:, None], pair_all, kb_map, flags, score_scale
     )
     attended = attended_rows[:, :HD].T
+    weights_mine, _ = lax.optimization_barrier((weights_mine, attended_rows))
+    weights_other = lax.ppermute(weights_mine, "row", [(i, i ^ 1) for i in range(n_row)])
     chunk = tok_rows // n_col
     attended_chunk = lax.all_to_all(attended, "col", 1, 0, tiled=True)
     x_chunk = lax.dynamic_slice_in_dim(full_rows, col_index * chunk, chunk, 1).astype(jnp.float32)
-    projected = lax.dot_general(
-        out_weight, attended_chunk, (((0,), (0,)), ((), ())), preferred_element_type=jnp.float32
+    projected = in_order(
+        *[
+            lax.dot_general(
+                part[0], attended_chunk, (((0,), (0,)), ((), ())), preferred_element_type=jnp.float32
+            )
+            for part in (weights_mine, weights_other)
+        ],
+        0,
     )
     updated = x_chunk + projected
     row_mean = jnp.sum(updated, axis=0, keepdims=True) / model_width
@@ -306,7 +322,13 @@
         * gain_merge.astype(jnp.float32)[:, None]
     ).astype(jnp.bfloat16)
     grouped = merger_chunk.reshape(model_width, chunk // 4, 4)
-    merged_here = jnp.einsum("fgi,ifd->gd", grouped, merge_full, preferred_element_type=jnp.float32)
+    merged_here = in_order(
+        *[
+            jnp.einsum("fgi,ifd->gd", grouped, part[1:], preferred_element_type=jnp.float32)
+            for part in (weights_mine, weights_other)
+        ],
+        1,
+    )
     merged_all = col_gather(merged_here.astype(jnp.bfloat16), n_col).reshape(-1, model_width)
     wanted_rows = lax.dynamic_index_in_dim(requests[0], col_index, 0, keepdims=False)
     is_valid = wanted_rows >= 0

time: 254 us -> 254 us (level)
  waiting for transfers between devices: 34.4 us -> 22.7 us
  local copies, waits for them, and re-layouts: 34.6 us -> 41.8 us
  matrix products: 13.1 us -> 18.2 us
    all_gather x1, waiting for transfers between devices: 23.2 us -> 9.36 us  [on_device(): weights_mine = lax.all_gather(weight_half, 'col', axis=1, tiled=True)]
    optimization_barrier x1, local copies, waits for them, and re-layouts: 8.47 us -> 14.2 us  [on_device(): weights_mine, _ = lax.optimization_barrier((weights_mine, attended_rows))]
    all_to_all x1, waiting for transfers between devices: 0.01 us -> 5.51 us  [on_device(): attended_chunk = lax.all_to_all(attended, 'col', 1, 0, tiled=True)]
    dot_general x2 -> x4, matrix products: 10.6 us -> 15.8 us  [the longest x2 11.1 us: on_device(): jnp.einsum('fgi,ifd->gd', grouped, part[1:], preferred_element_type=jnp.f...]
    all_to_all x1, waiting for transfers between devices: 10.4 us -> 7.15 us  [on_device(): picked_full = lax.all_to_all(picked_copies, 'col', 0, 0, tiled=True)]
  transfers between devices with their start and end apart: 4 -> 5, of which waited for: 2 -> 3; matrix products, arithmetic and copies ran while one was open for 20% -> 18% of each run, Pallas kernels for 38% -> 38%
where the time goes in v13:
time: 254 us; the launch traced here: 253 us
  Pallas kernels  122 us (48%)
  local copies, waits for them, and re-layouts  41.8 us (16%)
  waiting for transfers between devices  22.7 us (9%)
  other arithmetic  20 us (8%)
  matrix products  18.2 us (7%)
  starting transfers between devices  14.3 us (6%)
  between operations  13.8 us (5%)
    pallas_call x1, Pallas kernels, attention(): pl.pallas_call(kernel, grid_spec=grid_spec, out_shape=jax.ShapeDtypeStruc...  56.5 us
    pallas_call x1, Pallas kernels, row_gather(): pl.pallas_call(functools.partial(_row_gather_kernel, n_row=n_row), out_sh...  39.8 us
    pallas_call x1, Pallas kernels, col_gather(): pl.pallas_call(functools.partial(_col_gather_kernel, n_col=n_col), out_sh...  25.3 us
    optimization_barrier x1, local copies, waits for them, and re-layouts, on_device(): weights_mine, _ = lax.optimization_barrier((weights_mine, attended_rows))  14.2 us
    dot_general x2, matrix products, on_device(): jnp.einsum('fgi,ifd->gd', grouped, part[1:], preferred_element_type=jnp.f...  11.1 us
    all_gather x1, waiting for transfers between devices, on_device(): weights_mine = lax.all_gather(weight_half, 'col', axis=1, tiled=True)  9.36 us
    scatter x2, local copies, waits for them, and re-layouts, on_device(): keys_values = kv_cache.at[:, :, picked_rows].set(fresh_pairs)  7.74 us
    all_to_all x1, starting transfers between devices, on_device(): picked_full = lax.all_to_all(picked_copies, 'col', 0, 0, tiled=True)  7.31 us
  transfers between devices with their start and end apart: 5, of which 3 were waited for; matrix products, arithmetic and copies ran while one was open for 18% of the time, Pallas kernels for 38%

profile of v13, /device:TPU:78, one launch (start us, length us, event | category | flops | bytes accessed | tf_op | source)
XLA Modules:
  0.0 252.5 jit_solution(12860829835894091416)
XLA Ops:
  6.6 0.7 all-gather.3.cloned.1.call-update
  7.3 1.3 copy.86
  8.5 0.7 compare_select_fusion
  9.2 0.8 gather_fusion
  10.0 0.7 compare_and_fusion.2
  10.9 0.9 broadcast_in_dim.53
  11.8 7.3 %all-to-all-start = ((bf16[16,88,200]{2,1,0:T(8,128)(2,1)}), bf16[16,88,200]{2,1,0:T(8,128)(2,1)S(1)}, u32[]{:S(2)}, u32[]{:S(2)}) async-start(bf16[16,88,200]{2,1,0:T(8,128)(2,1)} %broadcast_in_dim.53), calls=%async_computation | async-start | bytes 1441792 | tf_op jit(solution)/shard_map/all_to_all | solution.py:250
  19.2 0.8 mul.106
  20.0 2.4 copy.89
  23.0 0.7 and_reduce_fusion
  23.7 1.2 fusion.28
  24.9 7.2 %all-to-all-done = bf16[16,88,200]{2,1,0:T(8,128)(2,1)S(1)} async-done(((bf16[16,88,200]{2,1,0:T(8,128)(2,1)}), bf16[16,88,200]{2,1,0:T(8,128)(2,1)S(1)}, u32[]{:S(2)}, u32[]{:S(2)}) %all-to-all-start) | async-done | bytes 563232 | tf_op jit(solution)/shard_map/all_to_all | solution.py:250
  33.1 7.0 %scatter_fusion = bf16[2,88,2048]{1,0,2:T(2,128)(2,1)S(1)} fusion(bf16[2,88,2048]{1,0,2:T(2,128)(2,1)S(1)} %copy.89, s32[200]{0:T(256)S(1)} %bitcast.82, bf16[200,2,88]{2,1,0:T(2,128)(2,1)S(1)} %bitcast.74), kind=kCustom, calls=%fused_computation.7 | custom fusion | bytes 212000 | tf_op jit(solution)/shard_map/scatter | solution.py:265
  40.1 0.8 copy.90
  40.9 1.9 broadcast_select_fusion
  42.9 1.4 scatter.13.x_ref
  44.3 0.9 copy-done.2
  45.1 39.8 %shard_map.109.k_ref.v_ref = bf16[8,2,96,2048]{3,2,1,0:T(8,128)(2,1)} custom-call(bf16[2,96,2048]{2,1,0:T(8,128)(2,1)} %copy-done.2), custom_call_target="tpu_custom_call" | custom-call | tf_op jit(solution)/shard_map/pallas_call | solution.py:110
  85.2 1.4 copy.100.qs_ref
  86.9 1.0 slice_convert_fusion
  88.2 0.7 gather_fusion.5
  89.1 0.7 gather_fusion.4
  90.6 0.7 sort.17
  91.4 0.7 gather_fusion.2
  92.1 0.7 gather_fusion.6
  93.0 4.4 %convert_reduce_fusion = (f32[2048]{0:T(1024)S(1)}, f32[2048]{0:T(1024)S(1)}) fusion(bf16[1408,2048]{1,0:T(8,128)(2,1)} %all-gather.3.cloned.1.call-done), kind=kLoop, calls=%fused_computation.10 | loop fusion | flops 11530240 | bytes 5783552 | tf_op jit(solution)/shard_map/reduce_sum | solution.py:272
  97.4 2.0 fusion.10
  99.7 0.9 pad.12.q_ref
  101.4 0.6 gather_fusion.3
  102.0 0.7 fusion.34.kb_map
  102.7 56.5 %shard_map.110 = bf16[2048,96]{1,0:T(8,128)(2,1)} custom-call(s32[2,8]{1,0:T(2,128)} %fusion.34.kb_map, s32[2,8]{1,0:T(2,128)} %get-tuple-element.38.flags, bf16[2048,96]{1,0:T(8,128)(2,1)} %pad.12.q_ref, f32[2048,1]{1,0:T(8,128)} %copy.100.qs_ref, bf16[8,2,96,2048]{3,2,1,0:T(8,128)(2,1)} %shard_map.109.k_ref.v_ref, ...), custom_call_target="tpu_custom_call" | custom-call | tf_op jit(solution)/shard_map/pallas_call | solution.py:217
  159.2 9.4 %all-gather.5.cloned.1.call-done = bf16[5,1408,704]{2,1,0:T(8,128)(2,1)} async-done(((bf16[5,88,704]{2,1,0:T(8,128)(2,1)}), bf16[5,1408,704]{2,1,0:T(8,128)(2,1)}) %all-gather.5.cloned.1.call-update) | async-done | bytes 9912336 | tf_op jit(solution)/shard_map/all_gather | solution.py:289
  168.6 14.2 %copy.102 = bf16[5,1408,704]{1,2,0:T(8,128)(2,1)} copy(bf16[5,1408,704]{2,1,0:T(8,128)(2,1)} %all-gather.5.cloned.1.call-done) | data formatting | bytes 19824640 | tf_op jit(solution)/shard_map/optimization_barrier | solution.py:302
  182.8 1.0 copy.101
  183.8 6.9 %all-to-all-start.1 = ((bf16[88,16,128]{2,0,1:T(8,128)(2,1)}), bf16[88,16,128]{2,0,1:T(8,128)(2,1)S(1)}, u32[]{:S(2)}, u32[]{:S(2)}) async-start(bf16[88,16,128]{2,0,1:T(8,128)(2,1)} %copy.101), calls=%async_computation.1 | async-start | bytes 720896 | tf_op jit(solution)/shard_map/all_to_all | solution.py:305
  190.7 0.7 fusion.35
  191.4 0.7 compare_bitcast_fusion
  192.1 5.5 %all-to-all-done.1 = bf16[88,16,128]{2,0,1:T(8,128)(2,1)S(1)} async-done(((bf16[88,16,128]{2,0,1:T(8,128)(2,1)}), bf16[88,16,128]{2,0,1:T(8,128)(2,1)S(1)}, u32[]{:S(2)}, u32[]{:S(2)}) %all-to-all-start.1) | async-done | bytes 360480 | tf_op jit(solution)/shard_map/all_to_all | solution.py:305
  197.6 2.4 fusion.13
  200.1 2.2 fusion.16
  202.3 1.2 fusion.37
  203.5 1.2 multiply_convert_fusion
  205.1 5.6 %fusion.21 = bf16[32,704]{1,0:T(8,128)(2,1)S(1)} fusion(bf16[5,1408,704]{1,2,0:T(8,128)(2,1)} %copy.102, bf16[1408,32,4]{0,2,1:T(4,128)(2,1)S(1)} %reshape.357), kind=kOutput, calls=%fused_computation.36 | convolution fusion | flops 253755392 | bytes 8335360 | tf_op jit(solution)/shard_map/fgi,ifd->gd/dot_general | solution.py:327
  210.6 5.6 %fusion.24 = bf16[32,704]{1,0:T(8,128)(2,1)S(1)} fusion(bf16[5,1408,704]{1,2,0:T(8,128)(2,1)} %collective-permute-done, bf16[1408,32,4]{0,2,1:T(4,128)(2,1)S(1)} %reshape.357), kind=kOutput, calls=%fused_computation.37 | convolution fusion | flops 253755392 | bytes 8335360 | tf_op jit(solution)/shard_map/fgi,ifd->gd/dot_general | solution.py:327
  216.2 0.8 fusion.31.x_ref
  217.0 25.3 %shard_map.111 = bf16[16,32,1408]{2,1,0:T(8,128)(2,1)} custom-call(bf16[32,1408]{1,0:T(8,128)(2,1)} %fusion.31.x_ref), custom_call_target="tpu_custom_call" | custom-call | tf_op jit(solution)/shard_map/pallas_call | solution.py:154
  242.4 2.5 %gather_fusion.1 = bf16[85,1408]{1,0:T(8,128)(2,1)S(1)} fusion(bf16[512,1408]{1,0:T(8,128)(2,1)} %bitcast.71, s32[1024]{0:T(1024)S(1)} %pad_clamp_fusion), kind=kCustom, calls=%fused_computation.4 | custom fusion | bytes 479060 | tf_op jit(solution)/shard_map/gather | solution.py:336
  244.9 0.8 bitcast_select_fusion
  (81 shorter events, 5.6 us)
Async XLA Ops:
  6.5 26.1 %copy-start = (bf16[2,88,1408]{2,1,0:T(8,128)(2,1)S(1)}, bf16[2,88,1408]{2,1,0:T(8,128)(2,1)}, u32[]{:S(2)}) copy-start(bf16[2,88,1408]{2,1,0:T(8,128)(2,1)} %param.18) | copy-start | bytes 1486852
  6.5 16.5 %copy-start.9 = (s32[3]{0:T(128)S(1)}, s32[3]{0:T(128)}, u32[]{:S(2)}) copy-start(s32[3]{0:T(128)} %constant.169.clone.1) | copy-start | bytes 40
  6.5 17.2 %copy-start.4 = (bf16[4,88,1408]{2,1,0:T(8,128)(2,1)S(1)}, bf16[4,88,1408]{2,1,0:T(8,128)(2,1)}, u32[]{:S(2)}) copy-start(bf16[4,88,1408]{2,1,0:T(8,128)(2,1)} %param.24) | copy-start | bytes 2973700
  6.5 17.2 %copy-start.5 = (bf16[88,1408]{1,0:T(8,128)(2,1)S(1)}, bf16[88,1408]{1,0:T(8,128)(2,1)}, u32[]{:S(2)}) copy-start(bf16[88,1408]{1,0:T(8,128)(2,1)} %param.22) | copy-start | bytes 743428
  6.5 18.4 %copy-start.6 = (s32[2048]{0:T(1024)S(1)}, s32[2048]{0:T(1024)}, u32[]{:S(2)}) copy-start(s32[2048]{0:T(1024)} %param.21) | copy-start | bytes 24580
  6.5 78.4 %all-gather.3.cloned.1.call-start = ((), (), s32[]{:S(2)}) async-start(), calls=%async_computation.2 | async-start | bytes 6127616 | tf_op jit(solution)/shard_map/all_gather | solution.py:246
  11.8 20.3 %all-to-all-start = ((bf16[16,88,200]{2,1,0:T(8,128)(2,1)}), bf16[16,88,200]{2,1,0:T(8,128)(2,1)S(1)}, u32[]{:S(2)}, u32[]{:S(2)}) async-start(bf16[16,88,200]{2,1,0:T(8,128)(2,1)} %broadcast_in_dim.53), calls=%async_computation | async-start | bytes 1441792 | tf_op jit(solution)/shard_map/all_to_all | solution.py:250
  19.1 149.4 %all-gather.5.cloned.1.call-start = ((), (), s32[]{:S(2)}) async-start(), calls=%async_computation.3 | async-start | bytes 11489280 | tf_op jit(solution)/shard_map/all_gather | solution.py:289
  40.1 44.9 %copy-start.7 = (bf16[1408]{0:T(1024)(128)(2,1)S(1)}, bf16[1408]{0:T(1024)(128)(2,1)}, u32[]{:S(2)}) copy-start(bf16[1408]{0:T(1024)(128)(2,1)} %param.16) | copy-start | bytes 8452
  44.2 0.9 copy-start.2
  84.9 12.5 %copy-start.10 = (bf16[88,1408]{1,0:T(8,128)(2,1)S(1)}, bf16[88,1408]{1,0:T(8,128)(2,1)}, u32[]{:S(2)}) copy-start(bf16[88,1408]{1,0:T(8,128)(2,1)} %param.17) | copy-start | bytes 743428
  93.0 4.4 %copy-start.1 = (bf16[1408,2048]{1,0:T(8,128)(2,1)S(1)}, bf16[1408,2048]{1,0:T(8,128)(2,1)}, u32[]{:S(2)}) copy-start(bf16[1408,2048]{1,0:T(8,128)(2,1)} %all-gather.3.cloned.1.call-done) | copy-start | bytes 17301508
  159.2 23.6 %copy-start.3 = (bf16[2048,96]{1,0:T(8,128)(2,1)S(1)}, bf16[2048,96]{1,0:T(8,128)(2,1)}, u32[]{:S(2)}) copy-start(bf16[2048,96]{1,0:T(8,128)(2,1)} %shard_map.110) | copy-start | bytes 1179652
  159.2 31.5 %copy-start.8 = (bf16[1408]{0:T(1024)(128)(2,1)S(1)}, bf16[1408]{0:T(1024)(128)(2,1)}, u32[]{:S(2)}) copy-start(bf16[1408]{0:T(1024)(128)(2,1)} %param.23) | copy-start | bytes 8452
  182.8 17.3 %collective-permute-start = (bf16[5,1408,704]{1,2,0:T(8,128)(2,1)}, bf16[5,1408,704]{1,2,0:T(8,128)(2,1)}, u32[]{:S(2)}, u32[]{:S(2)}) collective-permute-start(bf16[5,1408,704]{1,2,0:T(8,128)(2,1)} %copy.102), channel_id=1, source_target_pairs={{0,16},{16,0},{32,48},{48,32},{64,80},{80,64},{96,112},{112,96},{1... | collective-permute-start | bytes 29736968 | tf_op jit(solution)/shard_map/ppermute | solution.py:303
  183.8 13.9 %all-to-all-start.1 = ((bf16[88,16,128]{2,0,1:T(8,128)(2,1)}), bf16[88,16,128]{2,0,1:T(8,128)(2,1)S(1)}, u32[]{:S(2)}, u32[]{:S(2)}) async-start(bf16[88,16,128]{2,0,1:T(8,128)(2,1)} %copy.101), calls=%async_computation.1 | async-start | bytes 720896 | tf_op jit(solution)/shard_map/all_to_all | solution.py:305
Sparse Core Ops, SparseCore 0:
  9.5 63.5 all-gather.2
  85.1 83.4 all-gather.4

commit v14 on v13

--- a/solution.py
+++ b/solution.py
@@ -285,7 +285,7 @@
     core = lax.axis_index("row") % 2
     weight_stack = jnp.concatenate([w_out[None], w_merge], axis=0)
     weight_half = lax.dynamic_slice_in_dim(weight_stack, core * half, half, 2)
-    weight_half, _ = lax.optimization_barrier((weight_half, full_rows))
+    weight_half, _ = lax.optimization_barrier((weight_half, picked_full))
     weights_mine = lax.all_gather(weight_half, "col", axis=1, tiled=True)
 
     def in_order(mine, other, axis):

time: 254 us -> 252 us (level); the launches traced: 253 us -> 247 us
  waiting for transfers between devices: 22.7 us -> 16.8 us
    all_gather x1, waiting for transfers between devices: 9.36 us -> 0.02 us  [on_device(): weights_mine = lax.all_gather(weight_half, 'col', axis=1, tiled=True)]
    all_to_all x1, waiting for transfers between devices: 7.15 us -> 10.5 us  [on_device(): picked_full = lax.all_to_all(picked_copies, 'col', 0, 0, tiled=True)]
  transfers between devices with their start and end apart: 5 -> 5, of which waited for: 3 -> 2; matrix products, arithmetic and copies ran while one was open for 18% -> 18% of each run, Pallas kernels for 38% -> 39%
where the time goes in v14:
time: 252 us; the launch traced here: 247 us
  Pallas kernels  122 us (48%)
  local copies, waits for them, and re-layouts  39.7 us (16%)
  other arithmetic  21.4 us (8%)
  matrix products  18.2 us (7%)
  waiting for transfers between devices  16.8 us (7%)
  starting transfers between devices  16 us (6%)
  between operations  13.8 us (5%)
    pallas_call x1, Pallas kernels, attention(): pl.pallas_call(kernel, grid_spec=grid_spec, out_shape=jax.ShapeDtypeStruc...  56.5 us
    pallas_call x1, Pallas kernels, row_gather(): pl.pallas_call(functools.partial(_row_gather_kernel, n_row=n_row), out_sh...  39.8 us
    pallas_call x1, Pallas kernels, col_gather(): pl.pallas_call(functools.partial(_col_gather_kernel, n_col=n_col), out_sh...  25.3 us
    optimization_barrier x1, local copies, waits for them, and re-layouts, on_device(): weights_mine, _ = lax.optimization_barrier((weights_mine, attended_rows))  14.3 us
    dot_general x2, matrix products, on_device(): jnp.einsum('fgi,ifd->gd', grouped, part[1:], preferred_element_type=jnp.f...  11.1 us
    all_to_all x1, waiting for transfers between devices, on_device(): picked_full = lax.all_to_all(picked_copies, 'col', 0, 0, tiled=True)  10.5 us
    all_to_all x1, starting transfers between devices, on_device(): attended_chunk = lax.all_to_all(attended, 'col', 1, 0, tiled=True)  8.59 us
    scatter x2, local copies, waits for them, and re-layouts, on_device(): keys_values = kv_cache.at[:, :, picked_rows].set(fresh_pairs)  7.74 us
  transfers between devices with their start and end apart: 5, of which 2 were waited for; matrix products, arithmetic and copies ran while one was open for 18% of the time, Pallas kernels for 39%

profile of v14, /device:TPU:78, one launch (start us, length us, event | category | flops | bytes accessed | tf_op | source)
XLA Modules:
  0.0 247.4 jit_solution(10127461535159423020)
XLA Ops:
  6.6 0.7 all-gather.3.cloned.1.call-update
  7.3 1.3 copy.86
  8.5 0.7 compare_select_fusion
  9.2 0.8 gather_fusion
  10.0 0.7 compare_and_fusion.2
  10.9 0.9 broadcast_in_dim.53
  11.8 7.3 %all-to-all-start = ((bf16[16,88,200]{2,1,0:T(8,128)(2,1)}), bf16[16,88,200]{2,1,0:T(8,128)(2,1)S(1)}, u32[]{:S(2)}, u32[]{:S(2)}) async-start(bf16[16,88,200]{2,1,0:T(8,128)(2,1)} %broadcast_in_dim.53), calls=%async_computation | async-start | bytes 1441792 | tf_op jit(solution)/shard_map/all_to_all | solution.py:250
  19.2 2.4 fusion.28
  21.6 10.5 %all-to-all-done = bf16[16,88,200]{2,1,0:T(8,128)(2,1)S(1)} async-done(((bf16[16,88,200]{2,1,0:T(8,128)(2,1)}), bf16[16,88,200]{2,1,0:T(8,128)(2,1)S(1)}, u32[]{:S(2)}, u32[]{:S(2)}) %all-to-all-start) | async-done | bytes 563232 | tf_op jit(solution)/shard_map/all_to_all | solution.py:250
  32.4 1.4 copy.100.qs_ref
  33.8 0.8 copy.89
  34.9 0.7 fusion.39
  35.6 0.7 and_reduce_fusion
  37.3 7.0 %scatter_fusion = bf16[2,88,2048]{1,0,2:T(2,128)(2,1)S(1)} fusion(bf16[2,88,2048]{1,0,2:T(2,128)(2,1)S(1)} %copy.89, s32[200]{0:T(256)S(1)} %bitcast.82, bf16[200,2,88]{2,1,0:T(2,128)(2,1)S(1)} %bitcast.74), kind=kCustom, calls=%fused_computation.7 | custom fusion | bytes 212000 | tf_op jit(solution)/shard_map/scatter | solution.py:265
  44.3 0.8 copy.90
  45.1 1.9 broadcast_select_fusion
  47.1 1.4 scatter.13.x_ref
  48.5 0.9 copy-done.2
  49.4 39.8 %shard_map.109.k_ref.v_ref = bf16[8,2,96,2048]{3,2,1,0:T(8,128)(2,1)} custom-call(bf16[2,96,2048]{2,1,0:T(8,128)(2,1)} %copy-done.2), custom_call_target="tpu_custom_call" | custom-call | tf_op jit(solution)/shard_map/pallas_call | solution.py:110
  89.2 1.1 slice_convert_fusion
  90.6 0.7 gather_fusion.5
  91.4 0.7 gather_fusion.4
  93.0 0.7 sort.17
  93.8 0.7 gather_fusion.2
  94.5 0.7 gather_fusion.6
  95.4 4.5 %convert_reduce_fusion = (f32[2048]{0:T(1024)S(1)}, f32[2048]{0:T(1024)S(1)}) fusion(bf16[1408,2048]{1,0:T(8,128)(2,1)} %all-gather.3.cloned.1.call-done), kind=kLoop, calls=%fused_computation.10 | loop fusion | flops 11530240 | bytes 5783552 | tf_op jit(solution)/shard_map/reduce_sum | solution.py:272
  99.9 2.0 fusion.10
  102.2 0.9 pad.12.q_ref
  103.3 0.6 fusion.32
  103.9 0.6 gather_fusion.3
  104.6 0.7 fusion.34.kb_map
  105.2 56.5 %shard_map.110 = bf16[2048,96]{1,0:T(8,128)(2,1)} custom-call(s32[2,8]{1,0:T(2,128)} %fusion.34.kb_map, s32[2,8]{1,0:T(2,128)} %get-tuple-element.38.flags, bf16[2048,96]{1,0:T(8,128)(2,1)} %pad.12.q_ref, f32[2048,1]{1,0:T(8,128)} %copy.100.qs_ref, bf16[8,2,96,2048]{3,2,1,0:T(8,128)(2,1)} %shard_map.109.k_ref.v_ref, ...), custom_call_target="tpu_custom_call" | custom-call | tf_op jit(solution)/shard_map/pallas_call | solution.py:217
  161.8 14.3 %copy.102 = bf16[5,1408,704]{1,2,0:T(8,128)(2,1)} copy(bf16[5,1408,704]{2,1,0:T(8,128)(2,1)} %all-gather.5.cloned.1.call-done) | data formatting | bytes 19824640 | tf_op jit(solution)/shard_map/optimization_barrier | solution.py:302
  176.1 1.0 copy.101
  177.0 8.6 %all-to-all-start.1 = ((bf16[88,16,128]{2,0,1:T(8,128)(2,1)}), bf16[88,16,128]{2,0,1:T(8,128)(2,1)S(1)}, u32[]{:S(2)}, u32[]{:S(2)}) async-start(bf16[88,16,128]{2,0,1:T(8,128)(2,1)} %copy.101), calls=%async_computation.1 | async-start | bytes 720896 | tf_op jit(solution)/shard_map/all_to_all | solution.py:305
  185.6 0.7 fusion.35
  186.3 0.7 compare_bitcast_fusion
  187.0 5.5 %all-to-all-done.1 = bf16[88,16,128]{2,0,1:T(8,128)(2,1)S(1)} async-done(((bf16[88,16,128]{2,0,1:T(8,128)(2,1)}), bf16[88,16,128]{2,0,1:T(8,128)(2,1)S(1)}, u32[]{:S(2)}, u32[]{:S(2)}) %all-to-all-start.1) | async-done | bytes 360480 | tf_op jit(solution)/shard_map/all_to_all | solution.py:305
  192.6 2.4 fusion.13
  195.0 2.2 fusion.16
  197.2 1.2 fusion.37
  198.4 1.2 multiply_convert_fusion
  200.0 5.6 %fusion.21 = bf16[32,704]{1,0:T(8,128)(2,1)S(1)} fusion(bf16[5,1408,704]{1,2,0:T(8,128)(2,1)} %copy.102, bf16[1408,32,4]{0,2,1:T(4,128)(2,1)S(1)} %reshape.357), kind=kOutput, calls=%fused_computation.36 | convolution fusion | flops 253755392 | bytes 8335360 | tf_op jit(solution)/shard_map/fgi,ifd->gd/dot_general | solution.py:327
  205.6 5.6 %fusion.24 = bf16[32,704]{1,0:T(8,128)(2,1)S(1)} fusion(bf16[5,1408,704]{1,2,0:T(8,128)(2,1)} %collective-permute-done, bf16[1408,32,4]{0,2,1:T(4,128)(2,1)S(1)} %reshape.357), kind=kOutput, calls=%fused_computation.37 | convolution fusion | flops 253755392 | bytes 8335360 | tf_op jit(solution)/shard_map/fgi,ifd->gd/dot_general | solution.py:327
  211.2 0.8 fusion.31.x_ref
  211.9 25.3 %shard_map.111 = bf16[16,32,1408]{2,1,0:T(8,128)(2,1)} custom-call(bf16[32,1408]{1,0:T(8,128)(2,1)} %fusion.31.x_ref), custom_call_target="tpu_custom_call" | custom-call | tf_op jit(solution)/shard_map/pallas_call | solution.py:154
  237.3 2.5 %gather_fusion.1 = bf16[85,1408]{1,0:T(8,128)(2,1)S(1)} fusion(bf16[512,1408]{1,0:T(8,128)(2,1)} %bitcast.71, s32[1024]{0:T(1024)S(1)} %pad_clamp_fusion), kind=kCustom, calls=%fused_computation.4 | custom fusion | bytes 479060 | tf_op jit(solution)/shard_map/gather | solution.py:336
  239.8 0.8 bitcast_select_fusion
  (79 shorter events, 4.5 us)
Async XLA Ops:
  6.5 30.3 %copy-start = (bf16[2,88,1408]{2,1,0:T(8,128)(2,1)S(1)}, bf16[2,88,1408]{2,1,0:T(8,128)(2,1)}, u32[]{:S(2)}) copy-start(bf16[2,88,1408]{2,1,0:T(8,128)(2,1)} %param.18) | copy-start | bytes 1486852
  6.5 29.0 %copy-start.8 = (s32[3]{0:T(128)S(1)}, s32[3]{0:T(128)}, u32[]{:S(2)}) copy-start(s32[3]{0:T(128)} %constant.169.clone.1) | copy-start | bytes 40
  6.5 25.6 %copy-start.6 = (bf16[1408]{0:T(1024)(128)(2,1)S(1)}, bf16[1408]{0:T(1024)(128)(2,1)}, u32[]{:S(2)}) copy-start(bf16[1408]{0:T(1024)(128)(2,1)} %param.16) | copy-start | bytes 8452
  6.5 25.9 %copy-start.5 = (s32[2048]{0:T(1024)S(1)}, s32[2048]{0:T(1024)}, u32[]{:S(2)}) copy-start(s32[2048]{0:T(1024)} %param.21) | copy-start | bytes 24580
  6.5 27.2 %copy-start.4 = (bf16[2,88,2048]{2,1,0:T(8,128)(2,1)S(1)}, bf16[2,88,2048]{2,1,0:T(8,128)(2,1)}, u32[]{:S(2)}) copy-start(bf16[2,88,2048]{2,1,0:T(8,128)(2,1)} %param.19) | copy-start | bytes 2162692
  6.5 82.6 %all-gather.3.cloned.1.call-start = ((), (), s32[]{:S(2)}) async-start(), calls=%async_computation.2 | async-start | bytes 6127616 | tf_op jit(solution)/shard_map/all_gather | solution.py:246
  11.8 20.3 %all-to-all-start = ((bf16[16,88,200]{2,1,0:T(8,128)(2,1)}), bf16[16,88,200]{2,1,0:T(8,128)(2,1)S(1)}, u32[]{:S(2)}, u32[]{:S(2)}) async-start(bf16[16,88,200]{2,1,0:T(8,128)(2,1)} %broadcast_in_dim.53), calls=%async_computation | async-start | bytes 1441792 | tf_op jit(solution)/shard_map/all_to_all | solution.py:250
  19.1 142.6 %all-gather.5.cloned.1.call-start = ((), (), s32[]{:S(2)}) async-start(), calls=%async_computation.3 | async-start | bytes 11489280 | tf_op jit(solution)/shard_map/all_gather | solution.py:289
  48.5 0.9 copy-start.2
  89.1 10.7 %copy-start.9 = (bf16[88,1408]{1,0:T(8,128)(2,1)S(1)}, bf16[88,1408]{1,0:T(8,128)(2,1)}, u32[]{:S(2)}) copy-start(bf16[88,1408]{1,0:T(8,128)(2,1)} %param.17) | copy-start | bytes 743428
  95.4 4.5 %copy-start.1 = (bf16[1408,2048]{1,0:T(8,128)(2,1)S(1)}, bf16[1408,2048]{1,0:T(8,128)(2,1)}, u32[]{:S(2)}) copy-start(bf16[1408,2048]{1,0:T(8,128)(2,1)} %all-gather.3.cloned.1.call-done) | copy-start | bytes 17301508
  161.7 14.3 %copy-start.3 = (bf16[2048,96]{1,0:T(8,128)(2,1)S(1)}, bf16[2048,96]{1,0:T(8,128)(2,1)}, u32[]{:S(2)}) copy-start(bf16[2048,96]{1,0:T(8,128)(2,1)} %shard_map.110) | copy-start | bytes 1179652
  161.7 23.9 %copy-start.7 = (bf16[1408]{0:T(1024)(128)(2,1)S(1)}, bf16[1408]{0:T(1024)(128)(2,1)}, u32[]{:S(2)}) copy-start(bf16[1408]{0:T(1024)(128)(2,1)} %param.23) | copy-start | bytes 8452
  176.1 18.9 %collective-permute-start = (bf16[5,1408,704]{1,2,0:T(8,128)(2,1)}, bf16[5,1408,704]{1,2,0:T(8,128)(2,1)}, u32[]{:S(2)}, u32[]{:S(2)}) collective-permute-start(bf16[5,1408,704]{1,2,0:T(8,128)(2,1)} %copy.102), channel_id=1, source_target_pairs={{0,16},{16,0},{32,48},{48,32},{64,80},{80,64},{96,112},{112,96},{1... | collective-permute-start | bytes 29736968 | tf_op jit(solution)/shard_map/ppermute | solution.py:303
  177.0 15.5 %all-to-all-start.1 = ((bf16[88,16,128]{2,0,1:T(8,128)(2,1)}), bf16[88,16,128]{2,0,1:T(8,128)(2,1)S(1)}, u32[]{:S(2)}, u32[]{:S(2)}) async-start(bf16[88,16,128]{2,0,1:T(8,128)(2,1)} %copy.101), calls=%async_computation.1 | async-start | bytes 720896 | tf_op jit(solution)/shard_map/all_to_all | solution.py:305
Sparse Core Ops, SparseCore 0:
  9.5 63.5 all-gather.2
  75.3 81.5 all-gather.4
